TPU v7x, 32 devices: a whole 2x2x4 slice. The times are simulated.
32 devices in a mesh: lat: 4 (over z), lon: 8 (over y, x, core).
Axes of the slice: x: 2, y: 2, z: 4, core: 2. Of those that a mesh axis runs over, the one named last changes fastest.
Arguments:
- latent: bfloat16 [4, 48, 192, 512], P(None, 'lat', 'lon'), may hold values from -6 to 6
- gain_first: float32 [512], replicated, may hold values from 0.25 to 1.75
- triple_first: bfloat16 [512, 1536], replicated, may hold values from -3.75 to 3.75
- output_first: bfloat16 [512, 512], replicated, may hold values from -0.25 to 0.25
- gain_merge: float32 [2048], replicated, may hold values from 0.25 to 1.75
- merge_weight: bfloat16 [2048, 1024], replicated, may hold values from -0.125 to 0.125
- gain_second: float32 [1024], replicated, may hold values from 0.25 to 1.75
- triple_second: bfloat16 [1024, 3072], replicated, may hold values from -2.6516504 to 2.6516504
- output_second: bfloat16 [1024, 1024], replicated, may hold values from -0.1875 to 0.1875
- split_weight: bfloat16 [1024, 2048], replicated, may hold values from -0.1875 to 0.1875
Outputs:
- decoded: bfloat16 [4, 48, 192, 512], P(None, 'lat', 'lon')
- level_means: float32 [4, 512], replicated
All inputs are finite; a program needn't handle non-finite values.
Results may differ from a plain program's by a relative error of at most 0.028.
Values may be sent and summed in bfloat16 or wider, within the bound.
No kernel may reach another device: no remote copies, remote signals or barrier semaphores. Data moves between devices by JAX's collectives and lax.ppermute only.
A program may use at most 192 MiB of HBM per device.

v0:
```python
import functools
import math

import jax
import jax.numpy as jnp
import numpy as np
from jax import lax
from jax.experimental import pallas as pl
from jax.experimental.pallas import tpu as pltpu
from jax.sharding import PartitionSpec as P

HD = 64
WIN_LEV = 2
WIN_LAT = 6
WIN_LON = 12
HALF_LAT = WIN_LAT // 2
HALF_LON = WIN_LON // 2
LANES = 128

epsilon = 1e-05
masked_score = -1e30
score_scale = HD**-0.5 * math.log2(math.e)

LIMITS = {"pack": 60, "first": 16, "rest": 20, "own": 8, "coarse": 16, "split": 8, "output": 8}


class Plan:
    def __init__(self, levels, height, width):
        self.levels, self.height, self.width = levels, height, width
        assert levels % WIN_LEV == 0
        assert height == 2 * WIN_LAT and width == 2 * WIN_LON
        self.groups = levels // WIN_LEV
        half_lev = WIN_LEV // 2
        self.group_levels = [
            [(g * WIN_LEV + half_lev + i) % levels for i in range(WIN_LEV)] for g in range(self.groups)
        ]
        self.order = [lv for group in self.group_levels for lv in group]
        ids = [(((lv + half_lev)) // WIN_LEV) for lv in range(levels)]
        self.group_split = [len({ids[lv] for lv in group}) > 1 for group in self.group_levels]
        self.window = WIN_LEV * WIN_LAT * WIN_LON
        self.windows = [(wr, wc) for wr in range(height // WIN_LAT) for wc in range(width // WIN_LON)]

        own = [(lv, r, c) for lv in range(levels) for r in range(height) for c in range(width)]

        def boxed(rows, cols):
            return [(lv, r, c) for lv in self.order for r in range(*rows) for c in range(*cols)]

        def frame(windows, g):
            return [
                (lv, HALF_LAT + wr * WIN_LAT + r, HALF_LON + wc * WIN_LON + c)
                for wr, wc in windows
                for lv in self.group_levels[g]
                for r in range(WIN_LAT)
                for c in range(WIN_LON)
            ]

        self.own = own
        self.blocks = [sum([frame([w], g) for g in range(self.groups)], []) for w in self.windows]
        self.first = self.blocks[0]
        self.rest = sum(self.blocks[1:], [])
        fl, fc, fh, fw = HALF_LAT, HALF_LON, height, width
        self.raw_lat = boxed((fh, fh + fl), (fc, fw))
        self.raw_lon = boxed((fl, fh), (fw, fw + fc))
        self.raw_diag = boxed((fh, fh + fl), (fw, fw + fc))
        self.res_lat = boxed((fh + fl, fh + 2 * fl), (2 * fc, fw + fc))
        self.res_lon = boxed((2 * fl, fh + fl), (fw + fc, fw + 2 * fc))
        self.res_diag = boxed((fh + fl, fh + 2 * fl), (fw + fc, fw + 2 * fc))
        self.coarse_rows, self.coarse_cols = height // 2, width // 2
        self.parts = [
            [
                (lv, 2 * fl + 2 * r + ro, 2 * fc + 2 * c + co)
                for lv in self.order
                for r in range(self.coarse_rows)
                for c in range(self.coarse_cols)
            ]
            for ro in range(2)
            for co in range(2)
        ]

    def shifted(self, cells, rows, cols):
        return [(lv, r - rows, c - cols) for lv, r, c in cells]


def scatter_map(source, target):
    place = {cell: i for i, cell in enumerate(target)}
    assert len(place) == len(target)
    return np.array([place.get(cell, -1) for cell in source], np.int32)


class Maps:
    def __init__(self):
        self.rows = []

    def add(self, vector):
        self.rows.append(vector)
        return (len(self.rows) - 1, len(vector))

    def array(self):
        width = -(-max(len(v) for v in self.rows) // LANES) * LANES
        height = -(-len(self.rows) // 8) * 8
        out = np.full((height, width), -1, np.int32)
        for i, v in enumerate(self.rows):
            out[i, : len(v)] = v
        return jnp.asarray(out)


def one_hot(maps_ref, key, out_rows):
    row, count = key
    index = maps_ref[row : row + 1, :count]
    hot = lax.broadcasted_iota(jnp.int32, (out_rows, count), 0) == index
    return jnp.where(hot, 1.0, 0.0).astype(jnp.bfloat16)


def picked(maps_ref, key, out_rows, source):
    return jnp.dot(one_hot(maps_ref, key, out_rows), source, preferred_element_type=jnp.float32)


def normed_rows(value, gain):
    mean = jnp.mean(value, -1, keepdims=True)
    centred = value - mean
    var = jnp.mean(centred * centred, -1, keepdims=True)
    return (centred * lax.rsqrt(var + epsilon) * gain).astype(jnp.bfloat16)


def score_bias(count, group_split, edge):
    span = count // WIN_LEV
    rows = lax.broadcasted_iota(jnp.int32, (count, count), 0)
    cols = lax.broadcasted_iota(jnp.int32, (count, count), 1)
    q_lev, k_lev = rows >= span, cols >= span
    q_in = rows - jnp.where(q_lev, span, 0)
    k_in = cols - jnp.where(k_lev, span, 0)
    half = span // 2
    apart = (q_in >= half) != (k_in >= half)
    apart = jnp.where(apart, edge, 0)
    if group_split:
        apart = jnp.where(q_lev != k_lev, 1, apart)
    return jnp.where(apart > 0, masked_score, 0.0)


def head_pair(q, k, v, bias, low, high):
    trans = (((1,), (1,)), ((), ()))
    outs = []
    for keep, fill in ((low, high), (high, low)):
        s = lax.dot_general(q, k * keep, trans, preferred_element_type=jnp.float32)
        if bias is not None:
            s = s + bias
        peak = jnp.max(s, -1, keepdims=True)
        p = jnp.exp2((s - peak) * score_scale).astype(jnp.bfloat16)
        outs.append(jnp.dot(p, v * keep + fill, preferred_element_type=jnp.float32))
    is_low = lax.broadcasted_iota(jnp.int32, outs[0].shape, 1) < HD
    top = jnp.where(is_low, outs[0], outs[1])
    bottom = pltpu.roll(jnp.where(is_low, outs[1], outs[0]), HD, 1)
    return (top / bottom).astype(jnp.bfloat16)


def lane_masks():
    lane = lax.broadcasted_iota(jnp.int32, (1, LANES), 1)
    low = jnp.where(lane < HD, 1.0, 0.0).astype(jnp.bfloat16)
    high = jnp.where(lane < HD, 0.0, 1.0).astype(jnp.bfloat16)
    return low, high


def block_attention(qkv, att, row, channels, pair, bias, count):
    low, high = lane_masks()
    rows = pl.ds(row, count)
    base = pair * LANES

    def lanes(offset):
        start = base + offset
        return pl.ds(start if isinstance(start, int) else pl.multiple_of(start, LANES), LANES)

    q = qkv[rows, lanes(0)]
    k = qkv[rows, lanes(channels)]
    v = qkv[rows, lanes(2 * channels)]
    att[rows, lanes(0)] = head_pair(q, k, v, bias, low, high)


def split_rows(out_refs, value):
    start = 0
    for out in out_refs:
        out[...] = value[start : start + out.shape[0]].astype(out.dtype)
        start += out.shape[0]


def pack_kernel(plan, keys, maps_hbm, x_hbm, lat_ref, lon_ref, diag_ref, maps_ref, x_ref, sems):
    copies = [
        pltpu.make_async_copy(maps_hbm, maps_ref, sems.at[0]),
        pltpu.make_async_copy(x_hbm, x_ref, sems.at[1]),
    ]
    for copy in copies:
        copy.start()
    copies[0].wait()
    lat_size, diag_size = lat_ref.shape[0], diag_ref.shape[0]
    near = one_hot(maps_ref, keys["near"], lat_size + diag_size)
    far = one_hot(maps_ref, keys["lon"], lon_ref.shape[0])
    copies[1].wait()
    tile = plan.height * plan.width
    strip = HALF_LAT * plan.width
    first_rows = jnp.concatenate([x_ref[lv * tile : lv * tile + strip, :] for lv in range(plan.levels)], 0)
    split_rows((lat_ref, diag_ref), jnp.dot(near, first_rows, preferred_element_type=jnp.float32))
    lon_ref[...] = jnp.dot(far, x_ref[...], preferred_element_type=jnp.float32).astype(lon_ref.dtype)


def fine_first_kernel(
    plan, keys, maps_ref, edge_ref, x_ref, gain_ref, w_ref, wo_ref, y_ref, rest_ref, sent_ref, bias, qkv, att
):
    channels = x_ref.shape[1]
    x = x_ref[...]
    count = plan.window
    tokens = picked(maps_ref, keys["first"], y_ref.shape[0], x)
    normed = normed_rows(tokens, gain_ref[...])
    qkv[...] = jnp.dot(normed, w_ref[...], preferred_element_type=jnp.float32).astype(jnp.bfloat16)
    rest_ref[...] = picked(maps_ref, keys["rest"], rest_ref.shape[0], x).astype(jnp.bfloat16)
    for g in range(plan.groups):
        bias[2 * g] = score_bias(count, plan.group_split[g], 0)
        bias[2 * g + 1] = score_bias(count, plan.group_split[g], edge_ref[0])
    for pair in range(channels // LANES):
        for g in range(plan.groups):
            b = bias[2 * g] if plan.group_split[g] else None
            block_attention(qkv, att, g * count, channels, pair, b, count)
    update = jnp.dot(att[...], wo_ref[...], preferred_element_type=jnp.float32)
    y = (tokens + update).astype(jnp.bfloat16)
    y_ref[...] = y
    sent_ref[...] = picked(maps_ref, keys["sent", "first"], sent_ref.shape[0], y).astype(jnp.bfloat16)


def fine_rest_kernel(
    plan, keys, maps_ref, bias, sent_ref, rest_ref, lat_ref, lon_ref, diag_ref, gain_ref, w_ref, wo_ref,
    y_ref, slat_ref, slon_ref, sdiag_ref, tokens, qkv, att,
):
    channels = rest_ref.shape[1]
    count = plan.window
    block = plan.groups * count
    spread = len(plan.windows) - 1
    raw = {"raw_lat": lat_ref, "raw_lon": lon_ref, "raw_diag": diag_ref}
    for w in range(spread):
        rows = slice(w * block, (w + 1) * block)
        value = rest_ref[rows, :].astype(jnp.float32)
        for name, ref in raw.items():
            if (name, w) in keys:
                value = value + picked(maps_ref, keys[name, w], block, ref[...])
        tokens[rows, :] = value
    normed = normed_rows(tokens[...], gain_ref[...])
    qkv[...] = jnp.dot(normed, w_ref[...], preferred_element_type=jnp.float32).astype(jnp.bfloat16)
    pairs = channels // LANES

    @pl.loop(0, spread)
    def _(w):
        below = jnp.where(w + 1 >= plan.width // WIN_LON, 1, 0)
        for pair in range(pairs):
            for g in range(plan.groups):
                row = pl.multiple_of(w * block + g * count, 16)
                block_attention(qkv, att, row, channels, pair, bias[2 * g + below], count)

    update = jnp.dot(att[...], wo_ref[...], preferred_element_type=jnp.float32)
    y = (tokens[...] + update).astype(jnp.bfloat16)
    y_ref[...] = y
    start = 0
    for name, out in (("res_lat", slat_ref), ("res_lon", slon_ref), ("res_diag", sdiag_ref)):
        size = out.shape[0]
        value = sent_ref[start : start + size, :].astype(jnp.float32)
        for w in range(spread):
            if (name, w) in keys:
                value = value + picked(maps_ref, keys[name, w], size, y[w * block : (w + 1) * block])
        out[...] = value.astype(jnp.bfloat16)
        start += size


def coarse_own_kernel(keys, maps_ref, first_ref, rest_ref, part_ref):
    value = picked(maps_ref, keys["parts", "first"], part_ref.shape[0], first_ref[...])
    value = value + picked(maps_ref, keys["parts", "rest"], part_ref.shape[0], rest_ref[...])
    part_ref[...] = value.astype(jnp.bfloat16)


def thirds(value):
    first = value.astype(jnp.bfloat16).astype(jnp.float32)
    second = (value - first).astype(jnp.bfloat16).astype(jnp.float32)
    return jnp.concatenate([first, second, value - first - second], 0).astype(jnp.bfloat16)


def summed_thirds(stacked, right):
    out = jnp.dot(stacked, right, preferred_element_type=jnp.float32)
    rows = out.shape[0] // 3
    return out[:rows] + out[rows : 2 * rows] + out[2 * rows :]


def coarse_kernel(
    plan, keys, maps_ref, bias, part_ref, lat_ref, lon_ref, diag_ref, gm_ref, wm_ref, gs_ref, ws_ref, wo_ref,
    wsp_ref, weight_ref, fine_ref, upper_ref, sums_ref, qkv, att,
):
    parts = len(plan.parts)
    channels = part_ref.shape[1]
    total = upper_ref.shape[0]
    wide = ws_ref.shape[0]
    count = plan.window
    value = part_ref[...].astype(jnp.float32)
    for name, ref in (("res_lat", lat_ref), ("res_lon", lon_ref), ("res_diag", diag_ref)):
        value = value + picked(maps_ref, keys["parts", name], parts * total, ref[...])
    fine_ref[...] = value.astype(jnp.bfloat16)

    def part(k):
        return fine_ref[k * total : (k + 1) * total, :].astype(jnp.float32)

    mean = sum(jnp.sum(part(k), -1, keepdims=True) for k in range(parts)) / (parts * channels)
    square = sum(jnp.sum((part(k) - mean) ** 2, -1, keepdims=True) for k in range(parts))
    scale = lax.rsqrt(square / (parts * channels) + epsilon)
    merged = 0.0
    for k in range(parts):
        span = slice(k * channels, (k + 1) * channels)
        normed = ((part(k) - mean) * scale * gm_ref[:, span]).astype(jnp.bfloat16)
        merged = merged + jnp.dot(normed, wm_ref[span, :], preferred_element_type=jnp.float32)
    coarse = merged.astype(jnp.bfloat16).astype(jnp.float32)
    normed = normed_rows(coarse, gs_ref[...])
    qkv[...] = jnp.dot(normed, ws_ref[...], preferred_element_type=jnp.float32).astype(jnp.bfloat16)

    at_once = 4

    @pl.loop(0, wide // LANES // at_once)
    def _(step):
        for i in range(at_once):
            for g in range(plan.groups):
                block_attention(qkv, att, g * count, wide, step * at_once + i, bias[2 * g + 1], count)

    update = jnp.dot(att[...], wo_ref[...], preferred_element_type=jnp.float32)
    upper = (coarse + update).astype(jnp.bfloat16)
    upper_ref[...] = upper
    levels = plan.levels
    span = total // levels
    token = lax.broadcasted_iota(jnp.int32, (levels, total), 1)
    level = lax.broadcasted_iota(jnp.int32, (levels, total), 0)
    inside = (token >= level * span) & (token < (level + 1) * span)
    rows = jnp.concatenate([jnp.where(inside, weight_ref[ro : ro + 1, :], 0.0) for ro in range(2)], 0)
    weights = thirds(rows)
    heavy = thirds(summed_thirds(weights, upper))
    spread = summed_thirds(heavy, wsp_ref[...])
    sums = 0.0
    for k in range(parts):
        ro = k // 2
        fine = summed_thirds(weights, fine_ref[k * total : (k + 1) * total, :])
        sums = sums + (fine + spread[:, k * channels : (k + 1) * channels])[ro * levels : (ro + 1) * levels]
    for i, lv in enumerate(plan.order):
        sums_ref[lv : lv + 1, :] = sums[i : i + 1]


def split_kernel(plan, keys, maps_ref, fine_ref, upper_ref, wsp_ref, own_ref, slat_ref, slon_ref, sdiag_ref, decoded):
    parts = len(plan.parts)
    total = upper_ref.shape[0]
    channels = fine_ref.shape[1]
    levels = plan.levels
    span = total // levels
    upper = upper_ref[...]
    for k in range(parts):
        spread = jnp.dot(upper, wsp_ref[:, k * channels : (k + 1) * channels], preferred_element_type=jnp.float32)
        value = (fine_ref[k * total : (k + 1) * total, :].astype(jnp.float32) + spread).astype(jnp.bfloat16)
        for i in range(levels):
            decoded[i, k * span : (k + 1) * span, :] = value[i * span : (i + 1) * span]
    quarter = parts * (span // 4)
    hot = one_hot(maps_ref, keys["quarters"], parts * span)
    for i in range(levels):
        moved = jnp.dot(hot, decoded[i], preferred_element_type=jnp.float32).astype(jnp.bfloat16)
        for q, out in enumerate((own_ref, slon_ref, slat_ref, sdiag_ref)):
            out[i * quarter : (i + 1) * quarter, :] = moved[q * quarter : (q + 1) * quarter]


def output_kernel(plan, keys, maps_ref, own_ref, lon_ref, lat_ref, diag_ref, out_ref):
    span = own_ref.shape[0] // plan.levels
    tile = plan.height * plan.width
    hot = one_hot(maps_ref, keys["output"], tile)
    for i, lv in enumerate(plan.order):
        rows = slice(i * span, (i + 1) * span)
        stacked = jnp.concatenate(
            [ref[rows, :].astype(jnp.float32) for ref in (own_ref, lon_ref, lat_ref, diag_ref)], 0
        ).astype(jnp.bfloat16)
        moved = jnp.dot(hot, stacked, preferred_element_type=jnp.float32)
        out_ref[lv * tile : (lv + 1) * tile, :] = moved.astype(jnp.bfloat16)


def all_summed(value, axes):
    for axis in axes:
        count = lax.axis_size(axis)
        if count & (count - 1):
            value = lax.psum(value, axis)
            continue
        step = 1
        while step < count:
            value = value + lax.ppermute(value, axis, [(i, i ^ step) for i in range(count)])
            step *= 2
    return value


def whole_step(
    latent, gain_first, triple_first, output_first, gain_merge, merge_weight, gain_second, triple_second,
    output_second, split_weight,
):
    levels, height, width, channels = latent.shape
    wide = merge_weight.shape[1]
    plan = Plan(levels, height, width)
    maps = Maps()
    lat_count, lon_count = lax.axis_size("lat"), lax.axis_size("lon")

    def moved(value, lat_step, lon_step):
        pairs = [
            (a * lon_count + b, (a + lat_step) % lat_count * lon_count + (b + lon_step) % lon_count)
            for a in range(lat_count)
            for b in range(lon_count)
        ]
        return lax.ppermute(value, ("lat", "lon"), pairs)

    raw = {"raw_lat": (plan.raw_lat, height, 0), "raw_lon": (plan.raw_lon, 0, width), "raw_diag": (plan.raw_diag, height, width)}
    results = {"res_lat": (plan.res_lat, height, 0), "res_lon": (plan.res_lon, 0, width), "res_diag": (plan.res_diag, height, width)}
    pack_maps = Maps()
    strip = [cell for cell in plan.own if cell[1] < HALF_LAT]
    near = plan.shifted(*raw["raw_lat"]) + plan.shifted(*raw["raw_diag"])
    pack_keys = {
        "near": pack_maps.add(scatter_map(strip, near)),
        "lon": pack_maps.add(scatter_map(plan.own, plan.shifted(*raw["raw_lon"]))),
    }
    keys = {}

    def add(key, source, target):
        vector = scatter_map(source, target)
        if (vector >= 0).any():
            keys[key] = maps.add(vector)

    add("first", plan.own, plan.first)
    add("rest", plan.own, plan.rest)
    add(("sent", "first"), plan.first, sum([plan.shifted(*v) for v in results.values()], []))
    for w, block in enumerate(plan.blocks[1:]):
        for name, (cells, _, _) in raw.items():
            add((name, w), cells, block)
        for name, value in results.items():
            add((name, w), block, plan.shifted(*value))
    all_parts = sum(plan.parts, [])
    add(("parts", "first"), plan.first, all_parts)
    add(("parts", "rest"), plan.rest, all_parts)
    for name, (cells, _, _) in results.items():
        add(("parts", name), cells, all_parts)
    cells = [
        (2 * r + ro, 2 * c + co)
        for ro in range(2)
        for co in range(2)
        for r in range(plan.coarse_rows)
        for c in range(plan.coarse_cols)
    ]
    half_rows, half_cols = height // 2, width // 2
    quarters = [
        (qr * half_rows + r, qc * half_cols + c)
        for qr in range(2)
        for qc in range(2)
        for r in range(half_rows)
        for c in range(half_cols)
    ]
    keys["quarters"] = maps.add(scatter_map(cells, quarters))
    placed = [((r + half_rows) % height, (c + half_cols) % width) for r, c in quarters]
    keys["output"] = maps.add(scatter_map(placed, [(r, c) for r in range(height) for c in range(width)]))
    table, pack_table = maps.array(), pack_maps.array()

    vmem = pl.BlockSpec(memory_space=pltpu.VMEM)
    smem = pl.BlockSpec(memory_space=pltpu.SMEM)
    bf16 = jnp.bfloat16

    def call(body, outs, args, scratch=(), flops=0, limit=16, specs=None):
        size = sum(math.prod(a.shape) * a.dtype.itemsize for a in args)
        return pl.pallas_call(
            body,
            out_shape=[jax.ShapeDtypeStruct(s, d) for s, d in outs],
            in_specs=specs or [smem if a.ndim == 1 else vmem for a in args],
            out_specs=[vmem] * len(outs),
            scratch_shapes=list(scratch),
            cost_estimate=pl.CostEstimate(flops=flops, bytes_accessed=size, transcendentals=0),
            compiler_params=pltpu.CompilerParams(vmem_limit_bytes=limit << 20),
        )(*args)

    def rows_of(*counts):
        return [((n, channels), bf16) for n in counts]

    count = plan.window
    x = latent.reshape(levels * height * width, channels)
    edge = (lax.axis_index("lat") == lat_count - 1).astype(jnp.int32).reshape(1)
    n_first, n_rest, n_coarse = len(plan.first), len(plan.rest), len(plan.parts[0])
    n_part = len(plan.parts)
    n_sent = [len(cells) for cells, _, _ in results.values()]

    hbm = pl.BlockSpec(memory_space=pltpu.HBM)
    s_lat, s_lon, s_diag = call(
        functools.partial(pack_kernel, plan, pack_keys), rows_of(*[len(cells) for cells, _, _ in raw.values()]),
        (pack_table, x),
        [
            pltpu.VMEM(pack_table.shape, jnp.int32),
            pltpu.VMEM(x.shape, bf16),
            pltpu.SemaphoreType.DMA((2,)),
        ],
        flops=10**9, limit=LIMITS["pack"], specs=[hbm, hbm],
    )
    r_lat, r_lon, r_diag = moved(s_lat, -1, 0), moved(s_lon, 0, -1), moved(s_diag, -1, -1)
    gain1 = gain_first.reshape(1, channels)
    y_first, x_rest, sent, bias = call(
        functools.partial(fine_first_kernel, plan, keys),
        rows_of(n_first, n_rest, sum(n_sent)) + [((2 * plan.groups, count, count), jnp.float32)],
        (table, edge, x, gain1, triple_first, output_first),
        [pltpu.VMEM((n_first, 3 * channels), bf16), pltpu.VMEM((n_first, channels), bf16)],
        flops=4 * 10**9, limit=LIMITS["first"],
    )
    y_rest, s_lat, s_lon, s_diag = call(
        functools.partial(fine_rest_kernel, plan, keys), rows_of(n_rest, *n_sent),
        (table, bias, sent, x_rest, r_lat, r_lon, r_diag, gain1, triple_first, output_first),
        [
            pltpu.VMEM((n_rest, channels), jnp.float32),
            pltpu.VMEM((n_rest, 3 * channels), bf16),
            pltpu.VMEM((n_rest, channels), bf16),
        ],
        flops=6 * 10**9, limit=LIMITS["rest"],
    )
    r_lat, r_lon, r_diag = moved(s_lat, -1, 0), moved(s_lon, 0, -1), moved(s_diag, -1, -1)
    (parts,) = call(
        functools.partial(coarse_own_kernel, keys), rows_of(n_part * n_coarse),
        (table, y_first, y_rest), flops=4 * 10**9, limit=LIMITS["own"],
    )
    total_rows = height * lat_count
    total_cols = width * lon_count

    def row_weights(rows):
        return jnp.cos(jnp.pi * ((rows.astype(jnp.float32) + 0.5) / total_rows - 0.5))

    every = row_weights(jnp.arange(total_rows, dtype=jnp.int32))
    scale_total = jnp.sqrt(total_cols * jnp.sum(every * every))
    frame_rows = np.array([[r for _, r, _ in plan.parts[2 * ro]] for ro in range(2)], np.int32)
    weights = row_weights((lax.axis_index("lat") * height + frame_rows) % total_rows) / scale_total
    fine, upper, sums = call(
        functools.partial(coarse_kernel, plan, keys),
        rows_of(n_part * n_coarse) + [((n_coarse, wide), bf16), ((levels, channels), jnp.float32)],
        (
            table, bias, parts, r_lat, r_lon, r_diag, gain_merge.reshape(1, -1), merge_weight,
            gain_second.reshape(1, -1), triple_second, output_second, split_weight, weights,
        ),
        [pltpu.VMEM((n_coarse, 3 * wide), bf16), pltpu.VMEM((n_coarse, wide), bf16)],
        flops=8 * 10**9, limit=LIMITS["coarse"],
    )
    own, s_lat, s_lon, s_diag = call(
        functools.partial(split_kernel, plan, keys), rows_of(*[n_coarse] * 4),
        (table, fine, upper, split_weight), [pltpu.VMEM((levels, n_part * n_coarse // levels, channels), bf16)],
        flops=2 * 10**9, limit=LIMITS["split"],
    )
    d_lat, d_lon, d_diag = (moved(s_lat, 1, 0), moved(s_lon, 0, 1), moved(s_diag, 1, 1))
    means = all_summed(sums, ("lat", "lon"))
    (decoded,) = call(
        functools.partial(output_kernel, plan, keys),
        rows_of(levels * height * width), (table, own, d_lon, d_lat, d_diag), flops=10**9, limit=LIMITS["output"],
    )
    return decoded.reshape(latent.shape), means


def solution(mesh):
    return jax.shard_map(
        whole_step,
        mesh=mesh,
        in_specs=(P(None, "lat", "lon", None), P(), P(), P(), P(), P(), P(), P(), P(), P()),
        out_specs=(P(None, "lat", "lon", None), P()),
        check_vma=False,
    )
```

profile of v0, /device:TPU:0, one launch (start us, length us, event | category | flops | bytes accessed | tf_op | source)
XLA Modules:
  0.0 80.5 jit_solution(12039773143650770643)
XLA Ops:
  0.7 2.8 %shard_map.141 = (bf16[216,512]{1,0:T(8,128)(2,1)}, bf16[216,512]{1,0:T(8,128)(2,1)}, bf16[72,512]{1,0:T(8,128)(2,1)}) custom-call(s32[8,1152]{1,0:T(8,128)} %constant.46.clone.maps_hbm, bf16[1152,512]{1,0:T(8,128)(2,1)} %bitcast.8), custom_call_target="tpu_custom_call" | custom-call | flops 1000000000 | bytes 1216512 | tf_op jit(solution)/shard_map/pallas_call | solution.py:464
  3.5 5.1 %collective-permute-start = (bf16[216,512]{1,0:T(8,128)(2,1)}, bf16[216,512]{1,0:T(8,128)(2,1)S(1)}, u32[]{:S(2)}, u32[]{:S(2)}) collective-permute-start(bf16[216,512]{1,0:T(8,128)(2,1)} %get-tuple-element.24), channel_id=1, source_target_pairs={{0,24},{1,25},{2,26},{3,27},{4,28},{5,29},{6,30},{7,31},{8,0},{9,1... | collective-permute-start | bytes 663560 | tf_op jit(solution)/shard_map/ppermute | solution.py:407
  8.6 1.6 %collective-permute-start.1 = (bf16[216,512]{1,0:T(8,128)(2,1)}, bf16[216,512]{1,0:T(8,128)(2,1)}, u32[]{:S(2)}, u32[]{:S(2)}) collective-permute-start(bf16[216,512]{1,0:T(8,128)(2,1)} %get-tuple-element.25), channel_id=1, source_target_pairs={{0,7},{1,0},{2,1},{3,2},{4,3},{5,4},{6,5},{7,6},{8,15},{9,8},{10,9... | collective-permute-start | bytes 663560 | tf_op jit(solution)/shard_map/ppermute | solution.py:407
  10.2 0.8 %collective-permute-start.2 = (bf16[72,512]{1,0:T(8,128)(2,1)}, bf16[72,512]{1,0:T(8,128)(2,1)}, u32[]{:S(2)}, u32[]{:S(2)}) collective-permute-start(bf16[72,512]{1,0:T(8,128)(2,1)} %get-tuple-element.26), channel_id=1, source_target_pairs={{0,31},{1,24},{2,25},{3,26},{4,27},{5,28},{6,29},{7,30},{8,7},{9,0... | collective-permute-start | bytes 221192 | tf_op jit(solution)/shard_map/ppermute | solution.py:407
  11.0 0.7 multiply_reduce_fusion
  12.4 0.0 copy-start.9
  12.4 0.9 %copy-done.9 = s32[24,1152]{1,0:T(8,128)S(1)} copy-done((s32[24,1152]{1,0:T(8,128)S(1)}, s32[24,1152]{1,0:T(8,128)}, u32[]{:S(2)}) %copy-start.9) | copy-done | bytes 110616
  13.3 4.1 %shard_map.140 = (bf16[288,512]{1,0:T(8,128)(2,1)S(1)}, bf16[864,512]{1,0:T(8,128)(2,1)S(1)}, bf16[504,512]{1,0:T(8,128)(2,1)S(1)}, f32[4,144,144]{2,1,0:T(8,128)S(1)}) custom-call(s32[24,1152]{1,0:T(8,128)S(1)} %copy-done.9, s32[1]{0:T(128)} %bitcast.edge_ref, bf16[1152,512]{1,0:T(8,128)(2,1)S(1)} %bitcast.9, f32[1,512]{1,0:T(1,128)S(1)} %bitcast.12, ...), custom_call_target="tpu_custom_call" | custom-call | flops 4000000000 | bytes 3389444 | tf_op jit(solution)/shard_map/pallas_call | solution.py:464
  17.4 0.1 fusion.6.weight_ref
  17.5 0.0 slice-start.1
  17.5 8.1 %shard_map.142 = (bf16[864,512]{1,0:T(8,128)(2,1)S(1)}, bf16[216,512]{1,0:T(8,128)(2,1)S(1)}, bf16[216,512]{1,0:T(8,128)(2,1)S(1)}, bf16[72,512]{1,0:T(8,128)(2,1)S(1)}) custom-call(s32[24,1152]{1,0:T(8,128)S(1)} %copy-done.10, f32[4,144,144]{2,1,0:T(8,128)S(1)} %get-tuple-element.20.bias, bf16[504,512]{1,0:T(8,128)(2,1)S(1)} %get-tuple-element.22.sent_ref, ...), custom_call_target="tpu_custom_call" | custom-call | flops 6000000000 | bytes 4458496 | tf_op jit(solution)/shard_map/pallas_call | solution.py:464
  25.7 1.1 %collective-permute-start.3 = (bf16[216,512]{1,0:T(8,128)(2,1)S(1)}, bf16[216,512]{1,0:T(8,128)(2,1)S(1)}, u32[]{:S(2)}, u32[]{:S(2)}) collective-permute-start(bf16[216,512]{1,0:T(8,128)(2,1)S(1)} %get-tuple-element.28), channel_id=1, source_target_pairs={{0,24},{1,25},{2,26},{3,27},{4,28},{5,29},{6,30},{7,31},{8,0},{9,1... | collective-permute-start | bytes 663560 | tf_op jit(solution)/shard_map/ppermute | solution.py:407
  26.8 2.4 %collective-permute-start.4 = (bf16[216,512]{1,0:T(8,128)(2,1)S(1)}, bf16[216,512]{1,0:T(8,128)(2,1)S(1)}, u32[]{:S(2)}, u32[]{:S(2)}) collective-permute-start(bf16[216,512]{1,0:T(8,128)(2,1)S(1)} %get-tuple-element.29), channel_id=1, source_target_pairs={{0,7},{1,0},{2,1},{3,2},{4,3},{5,4},{6,5},{7,6},{8,15},{9,8},{10,9... | collective-permute-start | bytes 663560 | tf_op jit(solution)/shard_map/ppermute | solution.py:407
  29.2 0.0 collective-permute-start.5
  29.2 0.0 copy-start.7
  29.2 2.0 %shard_map.143.part_ref = bf16[1152,512]{1,0:T(8,128)(2,1)S(1)} custom-call(s32[24,1152]{1,0:T(8,128)S(1)} %copy-done.10, bf16[288,512]{1,0:T(8,128)(2,1)S(1)} %get-tuple-element.21.first_ref, bf16[864,512]{1,0:T(8,128)(2,1)S(1)} %get-tuple-element.27.rest_ref), custom_call_target="tpu_custom_call" | custom-call | flops 4000000000 | bytes 1290240 | tf_op jit(solution)/shard_map/pallas_call | solution.py:464
  31.2 2.5 %collective-permute-done.5.diag_ref = bf16[72,512]{1,0:T(8,128)(2,1)S(1)} collective-permute-done((bf16[72,512]{1,0:T(8,128)(2,1)S(1)}, bf16[72,512]{1,0:T(8,128)(2,1)S(1)}, u32[]{:S(2)}, u32[]{:S(2)}) %collective-permute-start.5) | collective-permute-done | bytes 73760 | tf_op jit(solution)/shard_map/ppermute | solution.py:407
  33.8 9.9 %shard_map.144 = (bf16[1152,512]{1,0:T(8,128)(2,1)S(1)}, bf16[288,1024]{1,0:T(8,128)(2,1)S(1)}, f32[4,512]{1,0:T(4,128)S(1)}) custom-call(s32[24,1152]{1,0:T(8,128)S(1)} %copy-done.10, f32[4,144,144]{2,1,0:T(8,128)S(1)} %get-tuple-element.20.bias, bf16[1152,512]{1,0:T(8,128)(2,1)S(1)} %shard_map.143.part_ref, ...), custom_call_target="tpu_custom_call" | custom-call | flops 8000000000 | bytes 18929920 | tf_op jit(solution)/shard_map/pallas_call | solution.py:464
  43.7 2.1 %shard_map.145 = (bf16[288,512]{1,0:T(8,128)(2,1)S(1)}, bf16[288,512]{1,0:T(8,128)(2,1)S(1)}, bf16[288,512]{1,0:T(8,128)(2,1)S(1)}, bf16[288,512]{1,0:T(8,128)(2,1)S(1)}) custom-call(s32[24,1152]{1,0:T(8,128)S(1)} %copy-done.10, bf16[1152,512]{1,0:T(8,128)(2,1)S(1)} %get-tuple-element.31.fine_ref, bf16[288,1024]{1,0:T(8,128)(2,1)S(1)} %get-tuple-element.32.upper_ref, ...), custom_call_target="tpu_custom_call" | custom-call | flops 2000000000 | bytes 6074368 | tf_op jit(solution)/shard_map/pallas_call | solution.py:464
  45.8 0.6 collective-permute-start.6
  46.4 1.0 %collective-permute-start.7 = (bf16[288,512]{1,0:T(8,128)(2,1)S(1)}, bf16[288,512]{1,0:T(8,128)(2,1)S(1)}, u32[]{:S(2)}, u32[]{:S(2)}) collective-permute-start(bf16[288,512]{1,0:T(8,128)(2,1)S(1)} %get-tuple-element.35), channel_id=1, source_target_pairs={{0,8},{1,9},{2,10},{3,11},{4,12},{5,13},{6,14},{7,15},{8,16},{9,17... | collective-permute-start | bytes 884744 | tf_op jit(solution)/shard_map/ppermute | solution.py:407
  47.4 1.4 %collective-permute-start.8 = (bf16[288,512]{1,0:T(8,128)(2,1)S(1)}, bf16[288,512]{1,0:T(8,128)(2,1)S(1)}, u32[]{:S(2)}, u32[]{:S(2)}) collective-permute-start(bf16[288,512]{1,0:T(8,128)(2,1)S(1)} %get-tuple-element.36), channel_id=1, source_target_pairs={{0,9},{1,10},{2,11},{3,12},{4,13},{5,14},{6,15},{7,8},{8,17},{9,18... | collective-permute-start | bytes 884744 | tf_op jit(solution)/shard_map/ppermute | solution.py:407
  48.8 3.8 %collective-permute-start.9 = (f32[4,512]{1,0:T(4,128)S(1)}, f32[4,512]{1,0:T(4,128)S(1)}, u32[]{:S(2)}, u32[]{:S(2)}) collective-permute-start(f32[4,512]{1,0:T(4,128)S(1)} %get-tuple-element.37), channel_id=1, source_target_pairs={{0,8},{8,0},{16,24},{24,16},{1,9},{9,1},{17,25},{25,17},{2,10},{10... | collective-permute-start | bytes 24584 | tf_op jit(solution)/shard_map/ppermute | solution.py:386
  52.7 12.4 %collective-permute-done.9 = f32[4,512]{1,0:T(4,128)S(1)} collective-permute-done((f32[4,512]{1,0:T(4,128)S(1)}, f32[4,512]{1,0:T(4,128)S(1)}, u32[]{:S(2)}, u32[]{:S(2)}) %collective-permute-start.9) | collective-permute-done | bytes 8224 | tf_op jit(solution)/shard_map/ppermute | solution.py:386
  65.0 4.5 %collective-permute-done.10 = f32[4,512]{1,0:T(4,128)S(1)} collective-permute-done((f32[4,512]{1,0:T(4,128)S(1)}, f32[4,512]{1,0:T(4,128)S(1)}, u32[]{:S(2)}, u32[]{:S(2)}) %collective-permute-start.10) | collective-permute-done | bytes 8224 | tf_op jit(solution)/shard_map/ppermute | solution.py:386
  69.6 1.2 %collective-permute-done.11 = f32[4,512]{1,0:T(4,128)S(1)} collective-permute-done((f32[4,512]{1,0:T(4,128)S(1)}, f32[4,512]{1,0:T(4,128)S(1)}, u32[]{:S(2)}, u32[]{:S(2)}) %collective-permute-start.11) | collective-permute-done | bytes 8224 | tf_op jit(solution)/shard_map/ppermute | solution.py:386
  70.8 2.0 %collective-permute-start.12 = (f32[4,512]{1,0:T(4,128)S(1)}, f32[4,512]{1,0:T(4,128)S(1)}, u32[]{:S(2)}, u32[]{:S(2)}) collective-permute-start(f32[4,512]{1,0:T(4,128)S(1)} %add.42), channel_id=1, source_target_pairs={{0,2},{1,3},{2,0},{3,1},{4,6},{5,7},{6,4},{7,5},{8,10},{9,11},{10,... | collective-permute-start | bytes 24584 | tf_op jit(solution)/shard_map/ppermute | solution.py:386
  72.7 1.7 %collective-permute-done.12 = f32[4,512]{1,0:T(4,128)S(1)} collective-permute-done((f32[4,512]{1,0:T(4,128)S(1)}, f32[4,512]{1,0:T(4,128)S(1)}, u32[]{:S(2)}, u32[]{:S(2)}) %collective-permute-start.12) | collective-permute-done | bytes 8224 | tf_op jit(solution)/shard_map/ppermute | solution.py:386
  74.4 1.7 %collective-permute-start.13 = (f32[4,512]{1,0:T(4,128)S(1)}, f32[4,512]{1,0:T(4,128)S(1)}, u32[]{:S(2)}, u32[]{:S(2)}) collective-permute-start(f32[4,512]{1,0:T(4,128)S(1)} %add.43), channel_id=1, source_target_pairs={{0,4},{1,5},{2,6},{3,7},{4,0},{5,1},{6,2},{7,3},{8,12},{9,13},{10,... | collective-permute-start | bytes 24584 | tf_op jit(solution)/shard_map/ppermute | solution.py:386
  76.1 2.0 %collective-permute-done.13 = f32[4,512]{1,0:T(4,128)S(1)} collective-permute-done((f32[4,512]{1,0:T(4,128)S(1)}, f32[4,512]{1,0:T(4,128)S(1)}, u32[]{:S(2)}, u32[]{:S(2)}) %collective-permute-start.13) | collective-permute-done | bytes 8224 | tf_op jit(solution)/shard_map/ppermute | solution.py:386
  78.1 0.6 add.44
  78.7 1.8 %shard_map.146 = bf16[1152,512]{1,0:T(8,128)(2,1)} custom-call(s32[24,1152]{1,0:T(8,128)S(1)} %copy-done.10, bf16[288,512]{1,0:T(8,128)(2,1)S(1)} %get-tuple-element.33.own_ref, bf16[288,512]{1,0:T(8,128)(2,1)S(1)} %collective-permute-done.6.lon_ref, bf16[288,512]{1,0:T(8,128)(2,1)S(1)} %collective-permute-done.7.lat_ref, ...), custom_call_target="tpu_custom_call" | custom-call | flops 1000000000 | bytes 1290240 | tf_op jit(solution)/shard_map/pallas_call | solution.py:464
  (39 shorter events, 0.1 us)
Async XLA Ops:
  0.6 11.8 %copy-start.3 = (bf16[512,1536]{1,0:T(8,128)(2,1)S(1)}, bf16[512,1536]{1,0:T(8,128)(2,1)}, u32[]{:S(2)}) copy-start(bf16[512,1536]{1,0:T(8,128)(2,1)} %w_ref.3) | copy-start | bytes 4718596
  0.6 11.8 %copy-start.4 = (bf16[4,12,24,512]{3,2,1,0:T(8,128)(2,1)S(1)}, bf16[4,12,24,512]{3,2,1,0:T(8,128)(2,1)}, u32[]{:S(2)}) copy-start(bf16[4,12,24,512]{3,2,1,0:T(8,128)(2,1)} %param.13) | copy-start | bytes 3538948
  0.7 11.8 %copy-start.5 = (bf16[512,512]{1,0:T(8,128)(2,1)S(1)}, bf16[512,512]{1,0:T(8,128)(2,1)}, u32[]{:S(2)}) copy-start(bf16[512,512]{1,0:T(8,128)(2,1)} %wo_ref.4) | copy-start | bytes 1572868
  0.7 11.8 %copy-start.8 = (f32[512]{0:T(512)S(1)}, f32[512]{0:T(512)}, u32[]{:S(2)}) copy-start(f32[512]{0:T(512)} %param.14) | copy-start | bytes 6148
  3.5 14.0 %collective-permute-start = (bf16[216,512]{1,0:T(8,128)(2,1)}, bf16[216,512]{1,0:T(8,128)(2,1)S(1)}, u32[]{:S(2)}, u32[]{:S(2)}) collective-permute-start(bf16[216,512]{1,0:T(8,128)(2,1)} %get-tuple-element.24), channel_id=1, source_target_pairs={{0,24},{1,25},{2,26},{3,27},{4,28},{5,29},{6,30},{7,31},{8,0},{9,1... | collective-permute-start | bytes 663560 | tf_op jit(solution)/shard_map/ppermute | solution.py:407
  8.6 8.9 %collective-permute-start.1 = (bf16[216,512]{1,0:T(8,128)(2,1)}, bf16[216,512]{1,0:T(8,128)(2,1)}, u32[]{:S(2)}, u32[]{:S(2)}) collective-permute-start(bf16[216,512]{1,0:T(8,128)(2,1)} %get-tuple-element.25), channel_id=1, source_target_pairs={{0,7},{1,0},{2,1},{3,2},{4,3},{5,4},{6,5},{7,6},{8,15},{9,8},{10,9... | collective-permute-start | bytes 663560 | tf_op jit(solution)/shard_map/ppermute | solution.py:407
  10.2 7.3 %collective-permute-start.2 = (bf16[72,512]{1,0:T(8,128)(2,1)}, bf16[72,512]{1,0:T(8,128)(2,1)}, u32[]{:S(2)}, u32[]{:S(2)}) collective-permute-start(bf16[72,512]{1,0:T(8,128)(2,1)} %get-tuple-element.26), channel_id=1, source_target_pairs={{0,31},{1,24},{2,25},{3,26},{4,27},{5,28},{6,29},{7,30},{8,7},{9,0... | collective-permute-start | bytes 221192 | tf_op jit(solution)/shard_map/ppermute | solution.py:407
  12.4 0.9 %copy-start.9 = (s32[24,1152]{1,0:T(8,128)S(1)}, s32[24,1152]{1,0:T(8,128)}, u32[]{:S(2)}) copy-start(s32[24,1152]{1,0:T(8,128)} %constant.45.clone.maps_ref) | copy-start | bytes 331780
  13.3 4.1 %copy-start.11 = (s32[2,288]{1,0:T(2,128)S(1)}, s32[2,288]{1,0:T(2,128)}, u32[]{:S(2)}) copy-start(s32[2,288]{1,0:T(2,128)} %constant.47.clone) | copy-start | bytes 6916
  13.3 4.2 %copy-start.10 = (s32[24,1152]{1,0:T(8,128)S(1)}, s32[24,1152]{1,0:T(8,128)}, u32[]{:S(2)}) copy-start(s32[24,1152]{1,0:T(8,128)} %constant.45.clone.maps_ref) | copy-start | bytes 331780
  13.3 20.4 %slice-start = ((s8[6291456]{0:T(1024)(128)(4,1)}), s8[4194304]{0:T(1024)(128)(4,1)S(1)}, s32[]{:S(2)}) async-start(s8[6291456]{0:T(1024)(128)(4,1)} %bitcast.6), calls=%async_computation | async-start | bytes 8388608
  17.5 16.2 %slice-start.1 = ((s8[6291456]{0:T(1024)(128)(4,1)}), s8[2097152]{0:T(1024)(128)(4,1)S(1)}, s32[]{:S(2)}) async-start(s8[6291456]{0:T(1024)(128)(4,1)} %bitcast.6), calls=%async_computation.1 | async-start | bytes 4194304
  25.7 8.1 %collective-permute-start.3 = (bf16[216,512]{1,0:T(8,128)(2,1)S(1)}, bf16[216,512]{1,0:T(8,128)(2,1)S(1)}, u32[]{:S(2)}, u32[]{:S(2)}) collective-permute-start(bf16[216,512]{1,0:T(8,128)(2,1)S(1)} %get-tuple-element.28), channel_id=1, source_target_pairs={{0,24},{1,25},{2,26},{3,27},{4,28},{5,29},{6,30},{7,31},{8,0},{9,1... | collective-permute-start | bytes 663560 | tf_op jit(solution)/shard_map/ppermute | solution.py:407
  26.8 7.0 %collective-permute-start.4 = (bf16[216,512]{1,0:T(8,128)(2,1)S(1)}, bf16[216,512]{1,0:T(8,128)(2,1)S(1)}, u32[]{:S(2)}, u32[]{:S(2)}) collective-permute-start(bf16[216,512]{1,0:T(8,128)(2,1)S(1)} %get-tuple-element.29), channel_id=1, source_target_pairs={{0,7},{1,0},{2,1},{3,2},{4,3},{5,4},{6,5},{7,6},{8,15},{9,8},{10,9... | collective-permute-start | bytes 663560 | tf_op jit(solution)/shard_map/ppermute | solution.py:407
  29.2 4.6 %collective-permute-start.5 = (bf16[72,512]{1,0:T(8,128)(2,1)S(1)}, bf16[72,512]{1,0:T(8,128)(2,1)S(1)}, u32[]{:S(2)}, u32[]{:S(2)}) collective-permute-start(bf16[72,512]{1,0:T(8,128)(2,1)S(1)} %get-tuple-element.30), channel_id=1, source_target_pairs={{0,31},{1,24},{2,25},{3,26},{4,27},{5,28},{6,29},{7,30},{8,7},{9,0... | collective-permute-start | bytes 221192 | tf_op jit(solution)/shard_map/ppermute | solution.py:407
  29.2 4.6 %copy-start = (bf16[2048,1024]{1,0:T(8,128)(2,1)S(1)}, bf16[2048,1024]{1,0:T(8,128)(2,1)}, u32[]{:S(2)}) copy-start(bf16[2048,1024]{1,0:T(8,128)(2,1)} %wm_ref.1) | copy-start | bytes 12582916
  29.2 4.6 %copy-start.1 = (bf16[1024,2048]{1,0:T(8,128)(2,1)S(1)}, bf16[1024,2048]{1,0:T(8,128)(2,1)}, u32[]{:S(2)}) copy-start(bf16[1024,2048]{1,0:T(8,128)(2,1)} %wsp_ref.3) | copy-start | bytes 12582916
  29.2 4.6 %copy-start.2 = (bf16[1024,1024]{1,0:T(8,128)(2,1)S(1)}, bf16[1024,1024]{1,0:T(8,128)(2,1)}, u32[]{:S(2)}) copy-start(bf16[1024,1024]{1,0:T(8,128)(2,1)} %wo_ref.5) | copy-start | bytes 6291460
  29.2 4.6 %copy-start.6 = (f32[2048]{0:T(1024)S(1)}, f32[2048]{0:T(1024)}, u32[]{:S(2)}) copy-start(f32[2048]{0:T(1024)} %param.17) | copy-start | bytes 24580
  29.2 4.6 %copy-start.7 = (f32[1024]{0:T(1024)S(1)}, f32[1024]{0:T(1024)}, u32[]{:S(2)}) copy-start(f32[1024]{0:T(1024)} %param.19) | copy-start | bytes 12292
  45.8 32.8 %collective-permute-start.6 = (bf16[288,512]{1,0:T(8,128)(2,1)S(1)}, bf16[288,512]{1,0:T(8,128)(2,1)S(1)}, u32[]{:S(2)}, u32[]{:S(2)}) collective-permute-start(bf16[288,512]{1,0:T(8,128)(2,1)S(1)} %get-tuple-element.34), channel_id=1, source_target_pairs={{0,1},{1,2},{2,3},{3,4},{4,5},{5,6},{6,7},{7,0},{8,9},{9,10},{10,1... | collective-permute-start | bytes 884744 | tf_op jit(solution)/shard_map/ppermute | solution.py:407
  46.4 32.3 %collective-permute-start.7 = (bf16[288,512]{1,0:T(8,128)(2,1)S(1)}, bf16[288,512]{1,0:T(8,128)(2,1)S(1)}, u32[]{:S(2)}, u32[]{:S(2)}) collective-permute-start(bf16[288,512]{1,0:T(8,128)(2,1)S(1)} %get-tuple-element.35), channel_id=1, source_target_pairs={{0,8},{1,9},{2,10},{3,11},{4,12},{5,13},{6,14},{7,15},{8,16},{9,17... | collective-permute-start | bytes 884744 | tf_op jit(solution)/shard_map/ppermute | solution.py:407
  47.4 31.2 %collective-permute-start.8 = (bf16[288,512]{1,0:T(8,128)(2,1)S(1)}, bf16[288,512]{1,0:T(8,128)(2,1)S(1)}, u32[]{:S(2)}, u32[]{:S(2)}) collective-permute-start(bf16[288,512]{1,0:T(8,128)(2,1)S(1)} %get-tuple-element.36), channel_id=1, source_target_pairs={{0,9},{1,10},{2,11},{3,12},{4,13},{5,14},{6,15},{7,8},{8,17},{9,18... | collective-permute-start | bytes 884744 | tf_op jit(solution)/shard_map/ppermute | solution.py:407
  48.8 16.2 %collective-permute-start.9 = (f32[4,512]{1,0:T(4,128)S(1)}, f32[4,512]{1,0:T(4,128)S(1)}, u32[]{:S(2)}, u32[]{:S(2)}) collective-permute-start(f32[4,512]{1,0:T(4,128)S(1)} %get-tuple-element.37), channel_id=1, source_target_pairs={{0,8},{8,0},{16,24},{24,16},{1,9},{9,1},{17,25},{25,17},{2,10},{10... | collective-permute-start | bytes 24584 | tf_op jit(solution)/shard_map/ppermute | solution.py:386
  65.0 4.5 %collective-permute-start.10 = (f32[4,512]{1,0:T(4,128)S(1)}, f32[4,512]{1,0:T(4,128)S(1)}, u32[]{:S(2)}, u32[]{:S(2)}) collective-permute-start(f32[4,512]{1,0:T(4,128)S(1)} %add.40), channel_id=1, source_target_pairs={{0,16},{8,24},{16,0},{24,8},{1,17},{9,25},{17,1},{25,9},{2,18},{10... | collective-permute-start | bytes 24584 | tf_op jit(solution)/shard_map/ppermute | solution.py:386
  69.6 1.2 %collective-permute-start.11 = (f32[4,512]{1,0:T(4,128)S(1)}, f32[4,512]{1,0:T(4,128)S(1)}, u32[]{:S(2)}, u32[]{:S(2)}) collective-permute-start(f32[4,512]{1,0:T(4,128)S(1)} %add.41), channel_id=1, source_target_pairs={{0,1},{1,0},{2,3},{3,2},{4,5},{5,4},{6,7},{7,6},{8,9},{9,8},{10,11... | collective-permute-start | bytes 24584 | tf_op jit(solution)/shard_map/ppermute | solution.py:386
  70.8 3.7 %collective-permute-start.12 = (f32[4,512]{1,0:T(4,128)S(1)}, f32[4,512]{1,0:T(4,128)S(1)}, u32[]{:S(2)}, u32[]{:S(2)}) collective-permute-start(f32[4,512]{1,0:T(4,128)S(1)} %add.42), channel_id=1, source_target_pairs={{0,2},{1,3},{2,0},{3,1},{4,6},{5,7},{6,4},{7,5},{8,10},{9,11},{10,... | collective-permute-start | bytes 24584 | tf_op jit(solution)/shard_map/ppermute | solution.py:386
  74.4 3.7 %collective-permute-start.13 = (f32[4,512]{1,0:T(4,128)S(1)}, f32[4,512]{1,0:T(4,128)S(1)}, u32[]{:S(2)}, u32[]{:S(2)}) collective-permute-start(f32[4,512]{1,0:T(4,128)S(1)} %add.43), channel_id=1, source_target_pairs={{0,4},{1,5},{2,6},{3,7},{4,0},{5,1},{6,2},{7,3},{8,12},{9,13},{10,... | collective-permute-start | bytes 24584 | tf_op jit(solution)/shard_map/ppermute | solution.py:386
where the time goes:
time: 80.7 us; the launch traced here: 80.5 us
  Pallas kernels  30.8 us (38%)
  waiting for transfers between devices  24.3 us (30%)
  starting transfers between devices  21.6 us (27%)
  between operations  1.57 us (2%)
  other arithmetic  1.37 us (2%)
  local copies, waits for them, and re-layouts  0.95 us (1%)
    pallas_call x7, Pallas kernels, call(): pl.pallas_call(body, out_shape=[jax.ShapeDtypeStruct(s, d) for s, d in ou...  30.8 us
    ppermute x5, waiting for transfers between devices, all_summed(): lax.ppermute(value, axis, [(i, i ^ step) for i in range(count)])  21.7 us
    ppermute x9, starting transfers between devices, moved(): return lax.ppermute(value, ('lat', 'lon'), pairs)  14.1 us
    ppermute x5, starting transfers between devices, all_summed(): lax.ppermute(value, axis, [(i, i ^ step) for i in range(count)])  7.47 us
    ppermute x9, waiting for transfers between devices, moved(): return lax.ppermute(value, ('lat', 'lon'), pairs)  2.54 us
  transfers between devices with their start and end apart: 14, of which 6 were waited for; matrix products, arithmetic and copies ran while one was open for 2% of the time, Pallas kernels for 8%

commit v1 on v0

v1 whole, which is shorter than its diff:
```python
import functools
import math

import jax
import jax.numpy as jnp
import numpy as np
from jax import lax
from jax.experimental import pallas as pl
from jax.experimental.pallas import tpu as pltpu
from jax.sharding import PartitionSpec as P

HD = 64
WIN_LEV = 2
WIN_LAT = 6
WIN_LON = 12
HALF_LAT = WIN_LAT // 2
HALF_LON = WIN_LON // 2
LANES = 128

epsilon = 1e-05
masked_score = -1e30
score_scale = HD**-0.5 * math.log2(math.e)

LIMITS = {"pack": 59, "first": 16, "edge": 16, "own": 12, "coarse": 16, "split": 8, "output": 8}


class Plan:
    def __init__(self, levels, height, width):
        self.levels, self.height, self.width = levels, height, width
        assert levels % WIN_LEV == 0
        assert height == 2 * WIN_LAT and width == 2 * WIN_LON
        self.groups = levels // WIN_LEV
        half_lev = WIN_LEV // 2
        self.group_levels = [
            [(g * WIN_LEV + half_lev + i) % levels for i in range(WIN_LEV)] for g in range(self.groups)
        ]
        self.order = [lv for group in self.group_levels for lv in group]
        ids = [(((lv + half_lev)) // WIN_LEV) for lv in range(levels)]
        self.group_split = [len({ids[lv] for lv in group}) > 1 for group in self.group_levels]
        self.window = WIN_LEV * WIN_LAT * WIN_LON
        self.windows = [(wr, wc) for wr in range(height // WIN_LAT) for wc in range(width // WIN_LON)]

        self.blocks = [
            cells_of(
                (HALF_LAT + wr * WIN_LAT, HALF_LAT + (wr + 1) * WIN_LAT),
                (HALF_LON + wc * WIN_LON, HALF_LON + (wc + 1) * WIN_LON),
            )
            for wr, wc in self.windows
        ]
        self.own = cells_of((0, height), (0, width))
        fl, fc, fh, fw = HALF_LAT, HALF_LON, height, width
        self.raw = {
            "raw_lat": cells_of((fh, fh + fl), (fc, fw)),
            "raw_diag": cells_of((fh, fh + fl), (fw, fw + fc)),
            "raw_lon": cells_of((fl, fh), (fw, fw + fc)),
        }
        self.results = {
            "res_lat": padded(cells_of((fh + fl, fh + 2 * fl), (2 * fc, fw + fc))),
            "res_lon": padded(cells_of((2 * fl, fh + fl), (fw + fc, fw + 2 * fc))),
            "res_diag": padded(cells_of((fh + fl, fh + 2 * fl), (fw + fc, fw + 2 * fc))),
        }
        self.coarse_rows, self.coarse_cols = height // 2, width // 2
        self.parts = [
            [
                (2 * fl + 2 * r + ro, 2 * fc + 2 * c + co)
                for r in range(self.coarse_rows)
                for c in range(self.coarse_cols)
            ]
            for ro in range(2)
            for co in range(2)
        ]


def cells_of(rows, cols):
    return [(r, c) for r in range(*rows) for c in range(*cols)]


def padded(cells):
    return cells + [None] * (-len(cells) % 8)


def shifted(cells, rows, cols):
    return [cell and (cell[0] - rows, cell[1] - cols) for cell in cells]


def scatter_map(source, target):
    place = {cell: i for i, cell in enumerate(target) if cell is not None}
    return np.array([-1 if cell is None else place.get(cell, -1) for cell in source], np.int32)


class Maps:
    def __init__(self):
        self.rows, self.keys = [], {}

    def add(self, key, source, target):
        self.keys[key] = (len(self.rows), len(source), len(target))
        self.rows.append(scatter_map(source, target))

    def array(self):
        width = -(-max(len(v) for v in self.rows) // LANES) * LANES
        height = -(-len(self.rows) // 8) * 8
        out = np.full((height, width), -1, np.int32)
        for i, v in enumerate(self.rows):
            out[i, : len(v)] = v
        return jnp.asarray(out)


def table_hot(maps_ref, key):
    row, count, out_rows = key
    return one_hot(maps_ref[row : row + 1, :count], out_rows)


def one_hot(index, out_rows):
    hot = lax.broadcasted_iota(jnp.int32, (out_rows, index.shape[1]), 0) == index
    return jnp.where(hot, 1.0, 0.0).astype(jnp.bfloat16)


def box_hot(levels, rows, cols, boxes, out_rows, turn=0):
    token = lax.broadcasted_iota(jnp.int32, (1, levels * rows * cols), 1)

    def divided(value, by):
        return jnp.floor((value.astype(jnp.float32) + 0.5) * (1.0 / by)).astype(jnp.int32)

    level = divided(token, rows * cols)
    inner = token - level * (rows * cols)
    row = divided(inner, cols)
    col = inner - row * cols
    slot = jnp.where(level >= turn, level - turn, level + levels - turn)
    place = jnp.full_like(token, -1)
    for r0, r1, c0, c1, base, level_step, row_step in boxes:
        inside = (row >= r0) & (row < r1) & (col >= c0) & (col < c1)
        place = jnp.where(inside, base + slot * level_step + (row - r0) * row_step + (col - c0), place)
    return one_hot(place, out_rows)


def moved_rows(hot, source):
    return jnp.dot(hot, source, preferred_element_type=jnp.float32)


def normed_rows(value, gain):
    mean = jnp.mean(value, -1, keepdims=True)
    centred = value - mean
    var = jnp.mean(centred * centred, -1, keepdims=True)
    return (centred * lax.rsqrt(var + epsilon) * gain).astype(jnp.bfloat16)


def score_bias(count, group_split, edge):
    span = count // WIN_LEV
    rows = lax.broadcasted_iota(jnp.int32, (count, count), 0)
    cols = lax.broadcasted_iota(jnp.int32, (count, count), 1)
    q_lev, k_lev = rows >= span, cols >= span
    q_in = rows - jnp.where(q_lev, span, 0)
    k_in = cols - jnp.where(k_lev, span, 0)
    half = span // 2
    apart = (q_in >= half) != (k_in >= half)
    apart = jnp.where(apart, edge, 0)
    if group_split:
        apart = jnp.where(q_lev != k_lev, 1, apart)
    return jnp.where(apart > 0, masked_score, 0.0)


def head_pair(q, k, v, bias, low, high):
    trans = (((1,), (1,)), ((), ()))
    outs = []
    for keep, fill in ((low, high), (high, low)):
        s = lax.dot_general(q, k * keep, trans, preferred_element_type=jnp.float32)
        if bias is not None:
            s = s + bias
        peak = jnp.max(s, -1, keepdims=True)
        p = jnp.exp2((s - peak) * score_scale).astype(jnp.bfloat16)
        outs.append(jnp.dot(p, v * keep + fill, preferred_element_type=jnp.float32))
    is_low = lax.broadcasted_iota(jnp.int32, outs[0].shape, 1) < HD
    top = jnp.where(is_low, outs[0], outs[1])
    bottom = pltpu.roll(jnp.where(is_low, outs[1], outs[0]), HD, 1)
    return (top / bottom).astype(jnp.bfloat16)


def lane_masks():
    lane = lax.broadcasted_iota(jnp.int32, (1, LANES), 1)
    low = jnp.where(lane < HD, 1.0, 0.0).astype(jnp.bfloat16)
    high = jnp.where(lane < HD, 0.0, 1.0).astype(jnp.bfloat16)
    return low, high


def block_attention(qkv, att, row, channels, pair, bias, count):
    low, high = lane_masks()
    rows = pl.ds(row, count)
    base = pair * LANES

    def lanes(offset):
        start = base + offset
        return pl.ds(start if isinstance(start, int) else pl.multiple_of(start, LANES), LANES)

    q = qkv[rows, lanes(0)]
    k = qkv[rows, lanes(channels)]
    v = qkv[rows, lanes(2 * channels)]
    att[rows, lanes(0)] = head_pair(q, k, v, bias, low, high)


def split_rows(out_refs, value):
    start = 0
    for out in out_refs:
        out[...] = value[start : start + out.shape[0]].astype(out.dtype)
        start += out.shape[0]


def pack_kernel(plan, x_hbm, lat_ref, diag_ref, lon_ref, near_ref, far_ref, sems):
    levels, height, width = plan.levels, plan.height, plan.width
    fl, fc = HALF_LAT, HALF_LON
    copies = [
        pltpu.make_async_copy(x_hbm.at[:, 0:fl], near_ref, sems.at[0]),
        pltpu.make_async_copy(x_hbm.at[:, fl:height, 0 : far_ref.shape[2]], far_ref, sems.at[1]),
    ]
    for copy in copies:
        copy.start()
    turn = WIN_LEV // 2
    across, down = width - fc, height - fl
    lat_size, diag_size = lat_ref.shape[0], diag_ref.shape[0]
    near = box_hot(
        levels, fl, width,
        [(0, fl, fc, width, 0, fl * across, across), (0, fl, 0, fc, lat_size, fl * fc, fc)],
        lat_size + diag_size, turn,
    )
    far = box_hot(levels, down, far_ref.shape[2], [(0, down, 0, fc, 0, down * fc, fc)], lon_ref.shape[0], turn)
    channels = x_hbm.shape[-1]
    copies[0].wait()
    split_rows((lat_ref, diag_ref), moved_rows(near, near_ref[...].reshape(-1, channels)))
    copies[1].wait()
    lon_ref[...] = moved_rows(far, far_ref[...].reshape(-1, channels)).astype(lon_ref.dtype)


def fine_first_kernel(
    plan, edge_ref, x_ref, gain_ref, w_ref, wo_ref, y_ref, *more
):
    rest_refs, (slat_ref, slon_ref, sdiag_ref, bias, qkv, att) = more[:-6], more[-6:]
    channels = x_ref.shape[1]
    levels, height, width = plan.levels, plan.height, plan.width
    fl, fc = HALF_LAT, HALF_LON
    turn = WIN_LEV // 2
    x = x_ref[...]
    count = plan.window
    area = WIN_LAT * WIN_LON
    block = y_ref.shape[0]

    def window_box(w, base):
        wr, wc = plan.windows[w]
        r0, c0 = fl + wr * WIN_LAT, fc + wc * WIN_LON
        return (r0, min(r0 + WIN_LAT, height), c0, min(c0 + WIN_LON, width), base, area, WIN_LON)

    tokens = moved_rows(box_hot(levels, height, width, [window_box(0, 0)], block, turn), x)
    normed = normed_rows(tokens, gain_ref[...])
    qkv[...] = jnp.dot(normed, w_ref[...], preferred_element_type=jnp.float32).astype(jnp.bfloat16)
    for w in range(1, len(plan.windows)):
        hot = box_hot(levels, height, width, [window_box(w, 0)], block, turn)
        rest_refs[w - 1][...] = moved_rows(hot, x).astype(jnp.bfloat16)
    for g in range(plan.groups):
        bias[2 * g] = score_bias(count, plan.group_split[g], 0)
        bias[2 * g + 1] = score_bias(count, plan.group_split[g], edge_ref[0])
    for pair in range(channels // LANES):
        for g in range(plan.groups):
            b = bias[2 * g] if plan.group_split[g] else None
            block_attention(qkv, att, g * count, channels, pair, b, count)
    update = jnp.dot(att[...], wo_ref[...], preferred_element_type=jnp.float32)
    y = (tokens + update).astype(jnp.bfloat16)
    y_ref[...] = y
    split_rows((slat_ref, slon_ref, sdiag_ref), moved_rows(sent_hot(plan, 0, sum(sent_sizes(plan))), y))


def sent_sizes(plan):
    return [plan.levels * len(cells) for cells in plan.results.values()]


def sent_hot(plan, w, out_rows, only=None):
    boxes, start = [], 0
    shifts = {"res_lat": (plan.height, 0), "res_lon": (0, plan.width), "res_diag": (plan.height, plan.width)}
    for name, cells in plan.results.items():
        sent = [cell for cell in shifted(cells, *shifts[name]) if cell is not None]
        r0, c0 = sent[0]
        r1, c1 = sent[-1]
        w0, v0 = plan.blocks[w][0]
        top, left = max(r0, w0), max(c0, v0)
        bottom, right = min(r1 + 1, w0 + WIN_LAT), min(c1 + 1, v0 + WIN_LON)
        if top < bottom and left < right and only in (None, name):
            row_step = c1 + 1 - c0
            base = start + (top - r0) * row_step + (left - c0)
            boxes.append((top - w0, bottom - w0, left - v0, right - v0, base, len(cells), row_step))
        if only is None:
            start += plan.levels * len(cells)
    if not boxes:
        return None
    return box_hot(plan.levels, WIN_LAT, WIN_LON, boxes, out_rows)


def raw_hot(plan, name, w, out_rows):
    cells = plan.raw[name]
    (r0, c0), (r1, c1) = cells[0], cells[-1]
    w0, v0 = plan.blocks[w][0]
    top, left = max(r0, w0), max(c0, v0)
    bottom, right = min(r1 + 1, w0 + WIN_LAT), min(c1 + 1, v0 + WIN_LON)
    if not (top < bottom and left < right):
        return None
    base = (top - w0) * WIN_LON + (left - v0)
    box = (top - r0, bottom - r0, left - c0, right - c0, base, WIN_LAT * WIN_LON, WIN_LON)
    return box_hot(plan.levels, r1 + 1 - r0, c1 + 1 - c0, [box], out_rows)


def fine_windows(plan, which, bias, rest_ref, raw, gain_ref, w_ref, wo_ref, y_ref, tokens, qkv, att):
    channels = rest_ref.shape[1]
    count = plan.window
    block = plan.groups * count
    for i, w in enumerate(which):
        value = rest_ref[i * block : (i + 1) * block, :].astype(jnp.float32)
        for name, ref in raw.items():
            hot = raw_hot(plan, name, w, block)
            if hot is not None:
                value = value + moved_rows(hot, ref[...])
        tokens[i * block : (i + 1) * block, :] = value
    normed = normed_rows(tokens[...], gain_ref[...])
    qkv[...] = jnp.dot(normed, w_ref[...], preferred_element_type=jnp.float32).astype(jnp.bfloat16)

    def window(i, below):
        for pair in range(channels // LANES):
            for g in range(plan.groups):
                row = i * block + g * count
                if not isinstance(row, int):
                    row = pl.multiple_of(row, 16)
                block_attention(qkv, att, row, channels, pair, bias[2 * g + below], count)

    belows = [plan.windows[w][0] for w in which]
    if len(which) == 1:
        window(0, belows[0])
    else:
        assert belows == list(range(len(which)))

        @pl.loop(0, len(which))
        def _(i):
            window(i, i)

    update = jnp.dot(att[...], wo_ref[...], preferred_element_type=jnp.float32)
    y = (tokens[...] + update).astype(jnp.bfloat16)
    y_ref[...] = y
    return y


def fine_edge_kernel(plan, w, name, raw_names, bias, sent_ref, rest_ref, *more):
    raw = dict(zip(raw_names, more))
    gain_ref, w_ref, wo_ref, y_ref, out_ref, tokens, qkv, att = more[len(raw_names) :]
    y = fine_windows(plan, [w], bias, rest_ref, raw, gain_ref, w_ref, wo_ref, y_ref, tokens, qkv, att)
    moved = moved_rows(sent_hot(plan, w, out_ref.shape[0], name), y)
    out_ref[...] = (sent_ref[...].astype(jnp.float32) + moved).astype(jnp.bfloat16)


def coarse_own_kernel(
    plan, keys, which, maps_ref, bias, first_ref, right_ref, below_ref, rest_ref, lat_ref, diag_ref, lon_ref, gain_ref, w_ref,
    wo_ref, part_ref, y_ref, tokens, qkv, att,
):
    raw = {"raw_lat": lat_ref, "raw_diag": diag_ref, "raw_lon": lon_ref}
    fine_windows(plan, which, bias, rest_ref, raw, gain_ref, w_ref, wo_ref, y_ref, tokens, qkv, att)
    area = WIN_LAT * WIN_LON
    hot = table_hot(maps_ref, keys["own"])
    total = part_ref.shape[0] // len(plan.parts)
    for i in range(plan.levels):
        rows = slice(i * area, (i + 1) * area)
        stacked = jnp.concatenate([ref[rows, :] for ref in (first_ref, right_ref, below_ref, y_ref)], 0)
        value = moved_rows(hot, stacked).astype(jnp.bfloat16)
        for k in range(len(plan.parts)):
            start = k * total + i * area
            part_ref[start : start + area, :] = value[k * area : (k + 1) * area]


def thirds(value):
    first = value.astype(jnp.bfloat16).astype(jnp.float32)
    second = (value - first).astype(jnp.bfloat16).astype(jnp.float32)
    return jnp.concatenate([first, second, value - first - second], 0).astype(jnp.bfloat16)


def summed_thirds(stacked, right):
    out = jnp.dot(stacked, right, preferred_element_type=jnp.float32)
    rows = out.shape[0] // 3
    return out[:rows] + out[rows : 2 * rows] + out[2 * rows :]


def coarse_kernel(
    plan, keys, maps_ref, bias, part_ref, lat_ref, lon_ref, diag_ref, gm_ref, wm_ref, gs_ref, ws_ref, wo_ref,
    wsp_ref, lat_index_ref, weight_ref, fine_ref, upper_ref, sums_ref, qkv, att,
):
    parts = len(plan.parts)
    channels = part_ref.shape[1]
    total = upper_ref.shape[0]
    wide = ws_ref.shape[0]
    count = plan.window
    levels = plan.levels
    area = total // levels
    hot = table_hot(maps_ref, keys["ahead"])
    for i in range(levels):
        pieces = []
        for ref in (lat_ref, lon_ref, diag_ref):
            size = ref.shape[0] // levels
            pieces.append(ref[i * size : (i + 1) * size, :])
        value = moved_rows(hot, jnp.concatenate(pieces, 0))
        for k in range(parts):
            rows = slice(k * total + i * area, k * total + (i + 1) * area)
            own = part_ref[rows, :].astype(jnp.float32)
            fine_ref[rows, :] = (own + value[k * area : (k + 1) * area]).astype(jnp.bfloat16)

    def part(k):
        return fine_ref[k * total : (k + 1) * total, :].astype(jnp.float32)

    mean = sum(jnp.sum(part(k), -1, keepdims=True) for k in range(parts)) / (parts * channels)
    square = sum(jnp.sum((part(k) - mean) ** 2, -1, keepdims=True) for k in range(parts))
    scale = lax.rsqrt(square / (parts * channels) + epsilon)
    merged = 0.0
    for k in range(parts):
        span = slice(k * channels, (k + 1) * channels)
        normed = ((part(k) - mean) * scale * gm_ref[:, span]).astype(jnp.bfloat16)
        merged = merged + jnp.dot(normed, wm_ref[span, :], preferred_element_type=jnp.float32)
    coarse = merged.astype(jnp.bfloat16).astype(jnp.float32)
    normed = normed_rows(coarse, gs_ref[...])
    qkv[...] = jnp.dot(normed, ws_ref[...], preferred_element_type=jnp.float32).astype(jnp.bfloat16)

    at_once = 4

    @pl.loop(0, wide // LANES // at_once)
    def _(step):
        for i in range(at_once):
            for g in range(plan.groups):
                block_attention(qkv, att, g * count, wide, step * at_once + i, bias[2 * g + 1], count)

    update = jnp.dot(att[...], wo_ref[...], preferred_element_type=jnp.float32)
    upper = (coarse + update).astype(jnp.bfloat16)
    upper_ref[...] = upper
    span = total // levels
    token = lax.broadcasted_iota(jnp.int32, (levels, total), 1)
    level = lax.broadcasted_iota(jnp.int32, (levels, total), 0)
    inside = (token >= level * span) & (token < (level + 1) * span)
    mine = weight_ref[lat_index_ref[0]]
    rows = jnp.concatenate([jnp.where(inside, mine[ro : ro + 1, :], 0.0) for ro in range(2)], 0)
    weights = thirds(rows)
    heavy = thirds(summed_thirds(weights, upper))
    spread = summed_thirds(heavy, wsp_ref[...])
    sums = 0.0
    for k in range(parts):
        ro = k // 2
        fine = summed_thirds(weights, fine_ref[k * total : (k + 1) * total, :])
        sums = sums + (fine + spread[:, k * channels : (k + 1) * channels])[ro * levels : (ro + 1) * levels]
    for i, lv in enumerate(plan.order):
        sums_ref[lv : lv + 1, :] = sums[i : i + 1]


def split_kernel(plan, keys, maps_ref, fine_ref, upper_ref, wsp_ref, own_ref, slat_ref, slon_ref, sdiag_ref, decoded):
    parts = len(plan.parts)
    total = upper_ref.shape[0]
    channels = fine_ref.shape[1]
    levels = plan.levels
    span = total // levels
    upper = upper_ref[...]
    for k in range(parts):
        spread = jnp.dot(upper, wsp_ref[:, k * channels : (k + 1) * channels], preferred_element_type=jnp.float32)
        value = (fine_ref[k * total : (k + 1) * total, :].astype(jnp.float32) + spread).astype(jnp.bfloat16)
        for i in range(levels):
            decoded[i, k * span : (k + 1) * span, :] = value[i * span : (i + 1) * span]
    quarter = parts * (span // 4)
    hot = table_hot(maps_ref, keys["quarters"])
    for i in range(levels):
        moved = jnp.dot(hot, decoded[i], preferred_element_type=jnp.float32).astype(jnp.bfloat16)
        for q, out in enumerate((own_ref, slon_ref, slat_ref, sdiag_ref)):
            out[i * quarter : (i + 1) * quarter, :] = moved[q * quarter : (q + 1) * quarter]


def output_kernel(plan, keys, maps_ref, own_ref, lon_ref, lat_ref, diag_ref, out_ref):
    span = own_ref.shape[0] // plan.levels
    tile = plan.height * plan.width
    hot = table_hot(maps_ref, keys["output"])
    for i, lv in enumerate(plan.order):
        rows = slice(i * span, (i + 1) * span)
        stacked = jnp.concatenate(
            [ref[rows, :].astype(jnp.float32) for ref in (own_ref, lon_ref, lat_ref, diag_ref)], 0
        ).astype(jnp.bfloat16)
        moved = jnp.dot(hot, stacked, preferred_element_type=jnp.float32)
        out_ref[lv * tile : (lv + 1) * tile, :] = moved.astype(jnp.bfloat16)


def all_summed(value, axes):
    for axis in axes:
        count = lax.axis_size(axis)
        if count & (count - 1):
            value = lax.psum(value, axis)
            continue
        step = 1
        while step < count:
            value = value + lax.ppermute(value, axis, [(i, i ^ step) for i in range(count)])
            step *= 2
    return value


def whole_step(
    latent, gain_first, triple_first, output_first, gain_merge, merge_weight, gain_second, triple_second,
    output_second, split_weight,
):
    levels, height, width, channels = latent.shape
    wide = merge_weight.shape[1]
    plan = Plan(levels, height, width)
    maps = Maps()
    lat_count, lon_count = lax.axis_size("lat"), lax.axis_size("lon")

    def moved(value, lat_step, lon_step):
        pairs = [
            (a * lon_count + b, (a + lat_step) % lat_count * lon_count + (b + lon_step) % lon_count)
            for a in range(lat_count)
            for b in range(lon_count)
        ]
        return lax.ppermute(value, ("lat", "lon"), pairs)

    all_parts = sum(plan.parts, [])
    maps.add("own", sum(plan.blocks, []), all_parts)
    maps.add("ahead", sum(plan.results.values(), []), all_parts)
    cells = [
        (2 * r + ro, 2 * c + co)
        for ro in range(2)
        for co in range(2)
        for r in range(plan.coarse_rows)
        for c in range(plan.coarse_cols)
    ]
    half_rows, half_cols = height // 2, width // 2
    quarters = [
        (qr * half_rows + r, qc * half_cols + c)
        for qr in range(2)
        for qc in range(2)
        for r in range(half_rows)
        for c in range(half_cols)
    ]
    maps.add("quarters", cells, quarters)
    placed = [((r + half_rows) % height, (c + half_cols) % width) for r, c in quarters]
    maps.add("output", placed, plan.own)
    table, keys = maps.array(), maps.keys

    vmem = pl.BlockSpec(memory_space=pltpu.VMEM)
    smem = pl.BlockSpec(memory_space=pltpu.SMEM)
    bf16 = jnp.bfloat16

    def call(body, outs, args, scratch=(), flops=0, limit=16, specs=None):
        size = sum(math.prod(a.shape) * a.dtype.itemsize for a in args)
        return pl.pallas_call(
            body,
            out_shape=[jax.ShapeDtypeStruct(s, d) for s, d in outs],
            in_specs=specs or [smem if a.ndim == 1 else vmem for a in args],
            out_specs=[vmem] * len(outs),
            scratch_shapes=list(scratch),
            cost_estimate=pl.CostEstimate(flops=flops, bytes_accessed=size, transcendentals=0),
            compiler_params=pltpu.CompilerParams(vmem_limit_bytes=limit << 20),
        )(*args)

    def rows_of(*counts):
        return [((n, channels), bf16) for n in counts]

    count = plan.window
    x = latent.reshape(levels * height * width, channels)
    lat_index = lax.axis_index("lat").astype(jnp.int32)
    edge = (lat_index == lat_count - 1).astype(jnp.int32).reshape(1)
    n_block = plan.groups * count
    n_coarse = levels * len(plan.parts[0])
    n_part = len(plan.parts)
    n_sent = sent_sizes(plan)

    hbm = pl.BlockSpec(memory_space=pltpu.HBM)
    margin = -(-HALF_LON // 8) * 8
    s_lat, s_diag, s_lon = call(
        functools.partial(pack_kernel, plan),
        rows_of(*[levels * len(cells) for cells in plan.raw.values()]), (latent,),
        [
            pltpu.VMEM((levels, HALF_LAT, width, channels), bf16),
            pltpu.VMEM((levels, height - HALF_LAT, margin, channels), bf16),
            pltpu.SemaphoreType.DMA((2,)),
        ],
        flops=10**9, limit=LIMITS["pack"], specs=[hbm],
    )
    r_lat = moved(s_lat, -1, 0)
    r_diag = moved(s_diag, -1, -1)
    r_lon = moved(s_lon, 0, -1)
    gain1 = gain_first.reshape(1, channels)
    y_first, x_right, x_below, x_last, s_lat, s_lon, s_diag, bias = call(
        functools.partial(fine_first_kernel, plan),
        rows_of(n_block, *[n_block] * (len(plan.windows) - 1), *n_sent)
        + [((2 * plan.groups, count, count), jnp.float32)],
        (edge, x, gain1, triple_first, output_first),
        [pltpu.VMEM((n_block, 3 * channels), bf16), pltpu.VMEM((n_block, channels), bf16)],
        flops=4 * 10**9, limit=LIMITS["first"],
    )
    fine_scratch = [
        pltpu.VMEM((n_block, channels), jnp.float32),
        pltpu.VMEM((n_block, 3 * channels), bf16),
        pltpu.VMEM((n_block, channels), bf16),
    ]
    fine_weights = (gain1, triple_first, output_first)

    def fine_edge(w, direction, sent, rest, raws):
        return call(
            functools.partial(fine_edge_kernel, plan, w, direction, list(raws)),
            rows_of(n_block, sent.shape[0]), (bias, sent, rest, *raws.values(), *fine_weights),
            fine_scratch, flops=2 * 10**9, limit=LIMITS["edge"],
        )

    y_right, s_lat = fine_edge(1, "res_lat", s_lat, x_right, {"raw_lon": r_lon})
    q_lat = moved(s_lat, -1, 0)
    q_diag = moved(s_diag, -1, -1)
    y_below, s_lon = fine_edge(2, "res_lon", s_lon, x_below, {"raw_lat": r_lat})
    q_lon = moved(s_lon, 0, -1)
    (parts,) = call(
        functools.partial(coarse_own_kernel, plan, keys, [len(plan.windows) - 1]),
        rows_of(n_part * n_coarse),
        (table, bias, y_first, y_right, y_below, x_last, r_lat, r_diag, r_lon, *fine_weights),
        [pltpu.VMEM((n_block, channels), bf16)] + fine_scratch, flops=4 * 10**9, limit=LIMITS["own"],
    )
    total_rows, total_cols = height * lat_count, width * lon_count
    angle = np.pi * ((np.arange(total_rows) + 0.5) / total_rows - 0.5)
    every = np.cos(angle)
    scaled = every / np.sqrt(total_cols * np.sum(every * every))
    frame_rows = np.array([[r for r, _ in plan.parts[2 * ro]] * levels for ro in range(2)])
    row_of = (np.arange(lat_count)[:, None, None] * height + frame_rows) % total_rows
    weights = jnp.asarray(scaled[row_of], jnp.float32)
    fine, upper, sums = call(
        functools.partial(coarse_kernel, plan, keys),
        rows_of(n_part * n_coarse) + [((n_coarse, wide), bf16), ((levels, channels), jnp.float32)],
        (
            table, bias, parts, q_lat, q_lon, q_diag, gain_merge.reshape(1, -1), merge_weight,
            gain_second.reshape(1, -1), triple_second, output_second, split_weight, lat_index.reshape(1), weights,
        ),
        [pltpu.VMEM((n_coarse, 3 * wide), bf16), pltpu.VMEM((n_coarse, wide), bf16)],
        flops=8 * 10**9, limit=LIMITS["coarse"],
    )
    own, s_lat, s_lon, s_diag = call(
        functools.partial(split_kernel, plan, keys), rows_of(*[n_coarse] * 4),
        (table, fine, upper, split_weight), [pltpu.VMEM((levels, n_part * n_coarse // levels, channels), bf16)],
        flops=2 * 10**9, limit=LIMITS["split"],
    )
    d_lat, d_lon, d_diag = (moved(s_lat, 1, 0), moved(s_lon, 0, 1), moved(s_diag, 1, 1))
    means = all_summed(sums, ("lat", "lon"))
    (decoded,) = call(
        functools.partial(output_kernel, plan, keys),
        rows_of(levels * height * width), (table, own, d_lon, d_lat, d_diag), flops=10**9, limit=LIMITS["output"],
    )
    return decoded.reshape(latent.shape), means


def solution(mesh):
    return jax.shard_map(
        whole_step,
        mesh=mesh,
        in_specs=(P(None, "lat", "lon", None), P(), P(), P(), P(), P(), P(), P(), P(), P()),
        out_specs=(P(None, "lat", "lon", None), P()),
        check_vma=False,
    )
```

time: 80.7 us -> 77.9 us (0.965)
  waiting for transfers between devices: 24.3 us -> 27.2 us
  starting transfers between devices: 21.6 us -> 19.4 us
  Pallas kernels: 30.8 us -> 29.6 us
  local copies, waits for them, and re-layouts: 0.95 us -> 0.07 us
    ppermute x5, waiting for transfers between devices: 21.7 us -> 23.8 us  [all_summed(): lax.ppermute(value, axis, [(i, i ^ step) for i in range(count)])]
    ppermute x5, starting transfers between devices: 7.47 us -> 5.93 us  [all_summed(): lax.ppermute(value, axis, [(i, i ^ step) for i in range(count)])]
    pallas_call x7 -> x8, Pallas kernels: 30.8 us -> 29.6 us  [call(): pl.pallas_call(body, out_shape=[jax.ShapeDtypeStruct(s, d) for s, d in ou...]
    unnamed x28 -> x26, local copies, waits for them, and re-layouts: 0.95 us -> 0.07 us
    ppermute x9, waiting for transfers between devices: 2.54 us -> 3.41 us  [moved(): return lax.ppermute(value, ('lat', 'lon'), pairs)]
  transfers between devices with their start and end apart: 14 -> 14, of which waited for: 6 -> 7; matrix products, arithmetic and copies ran while one was open for 2% -> 1% of each run, Pallas kernels for 8% -> 18%
where the time goes in v1:
time: 77.9 us; the launch traced here: 77.8 us
  Pallas kernels  29.6 us (38%)
  waiting for transfers between devices  27.2 us (35%)
  starting transfers between devices  19.4 us (25%)
  between operations  0.89 us (1%)
    pallas_call x8, Pallas kernels, call(): pl.pallas_call(body, out_shape=[jax.ShapeDtypeStruct(s, d) for s, d in ou...  29.6 us
    ppermute x5, waiting for transfers between devices, all_summed(): lax.ppermute(value, axis, [(i, i ^ step) for i in range(count)])  23.8 us
    ppermute x9, starting transfers between devices, moved(): return lax.ppermute(value, ('lat', 'lon'), pairs)  13.4 us
    ppermute x5, starting transfers between devices, all_summed(): lax.ppermute(value, axis, [(i, i ^ step) for i in range(count)])  5.93 us
    ppermute x9, waiting for transfers between devices, moved(): return lax.ppermute(value, ('lat', 'lon'), pairs)  3.41 us
  transfers between devices with their start and end apart: 14, of which 7 were waited for; matrix products, arithmetic and copies ran while one was open for 1% of the time, Pallas kernels for 18%

profile of v1, /device:TPU:0, one launch (start us, length us, event | category | flops | bytes accessed | tf_op | source)
XLA Modules:
  0.0 77.8 jit_solution(11428043735947585171)
XLA Ops:
  0.7 2.4 %shard_map.132 = (bf16[216,512]{1,0:T(8,128)(2,1)}, bf16[72,512]{1,0:T(8,128)(2,1)}, bf16[216,512]{1,0:T(8,128)(2,1)}) custom-call(bf16[4,12,24,512]{3,2,1,0:T(8,128)(2,1)} %x_hbm.1), custom_call_target="tpu_custom_call" | custom-call | flops 1000000000 | bytes 1179648 | tf_op jit(solution)/shard_map/pallas_call | solution.py:543
  3.1 6.5 %collective-permute-start.2 = (bf16[72,512]{1,0:T(8,128)(2,1)}, bf16[72,512]{1,0:T(8,128)(2,1)}, u32[]{:S(2)}, u32[]{:S(2)}) collective-permute-start(bf16[72,512]{1,0:T(8,128)(2,1)} %get-tuple-element.35), channel_id=1, source_target_pairs={{0,31},{1,24},{2,25},{3,26},{4,27},{5,28},{6,29},{7,30},{8,7},{9,0... | collective-permute-start | bytes 221192 | tf_op jit(solution)/shard_map/ppermute | solution.py:512
  9.5 0.9 %collective-permute-start = (bf16[216,512]{1,0:T(8,128)(2,1)}, bf16[216,512]{1,0:T(8,128)(2,1)S(1)}, u32[]{:S(2)}, u32[]{:S(2)}) collective-permute-start(bf16[216,512]{1,0:T(8,128)(2,1)} %get-tuple-element.28), channel_id=1, source_target_pairs={{0,7},{1,0},{2,1},{3,2},{4,3},{5,4},{6,5},{7,6},{8,15},{9,8},{10,9... | collective-permute-start | bytes 663560 | tf_op jit(solution)/shard_map/ppermute | solution.py:512
  10.4 0.4 collective-permute-start.1
  10.9 4.1 %shard_map.131 = (bf16[288,512]{1,0:T(8,128)(2,1)S(1)}, bf16[288,512]{1,0:T(8,128)(2,1)S(1)}, bf16[288,512]{1,0:T(8,128)(2,1)S(1)}, bf16[288,512]{1,0:T(8,128)(2...) custom-call(s32[1]{0:T(128)} %bitcast.edge_ref, ...), custom_call_target="tpu_custom_call" | custom-call | flops 4000000000 | bytes 3278852 | tf_op jit(solution)/shard_map/pallas_call | solution.py:543
  14.9 0.1 collective-permute-start.5
  15.0 2.7 %collective-permute-done.1.more_0_.lat_ref = bf16[216,512]{1,0:T(8,128)(2,1)} collective-permute-done((bf16[216,512]{1,0:T(8,128)(2,1)}, bf16[216,512]{1,0:T(8,128)(2,1)}, u32[]{:S(2)}, u32[]{:S(2)}) %collective-permute-start.1) | collective-permute-done | bytes 221216 | tf_op jit(solution)/shard_map/ppermute | solution.py:512
  17.7 3.4 %shard_map.134 = (bf16[288,512]{1,0:T(8,128)(2,1)S(1)}, bf16[224,512]{1,0:T(8,128)(2,1)S(1)}) custom-call(f32[4,144,144]{2,1,0:T(8,128)S(1)} %get-tuple-element.24.bias, bf16[224,512]{1,0:T(8,128)(2,1)S(1)} %get-tuple-element.30.sent_ref, bf16[288,512]{1,0:T(8,128)(2,1)S(1)} %get-tuple-element.31.rest_ref, ...), custom_call_target="tpu_custom_call" | custom-call | flops 2000000000 | bytes 3176448 | tf_op jit(solution)/shard_map/pallas_call | solution.py:543
  21.1 0.1 collective-permute-start.4
  21.2 0.0 copy-start.9
  21.2 0.0 slice-start
  21.2 2.4 %shard_map.133 = (bf16[288,512]{1,0:T(8,128)(2,1)S(1)}, bf16[224,512]{1,0:T(8,128)(2,1)S(1)}) custom-call(f32[4,144,144]{2,1,0:T(8,128)S(1)} %get-tuple-element.24.bias, bf16[224,512]{1,0:T(8,128)(2,1)S(1)} %get-tuple-element.26.sent_ref, bf16[288,512]{1,0:T(8,128)(2,1)S(1)} %get-tuple-element.27.rest_ref, ...), custom_call_target="tpu_custom_call" | custom-call | flops 2000000000 | bytes 3176448 | tf_op jit(solution)/shard_map/pallas_call | solution.py:543
  23.6 4.2 %collective-permute-start.3 = (bf16[224,512]{1,0:T(8,128)(2,1)S(1)}, bf16[224,512]{1,0:T(8,128)(2,1)S(1)}, u32[]{:S(2)}, u32[]{:S(2)}) collective-permute-start(bf16[224,512]{1,0:T(8,128)(2,1)S(1)} %get-tuple-element.36), channel_id=1, source_target_pairs={{0,24},{1,25},{2,26},{3,27},{4,28},{5,29},{6,30},{7,31},{8,0},{9,1... | collective-permute-start | bytes 688136 | tf_op jit(solution)/shard_map/ppermute | solution.py:512
  27.9 0.0 copy-start.10
  28.0 4.1 %shard_map.135.part_ref = bf16[1152,512]{1,0:T(8,128)(2,1)S(1)} custom-call(s32[8,384]{1,0:T(8,128)S(1)} %copy-done.9, f32[4,144,144]{2,1,0:T(8,128)S(1)} %get-tuple-element.24.bias, bf16[288,512]{1,0:T(8,128)(2,1)S(1)} %get-tuple-element.25.first_ref, bf16[288,512]{1,0:T(8,128)(2,1)S(1)} %get-tuple-element.29.right_ref, ...), custom_call_target="tpu_custom_call" | custom-call | flops 4000000000 | bytes 4139008 | tf_op jit(solution)/shard_map/pallas_call | solution.py:543
  32.1 0.7 collective-permute-done.3.lat_ref
  32.9 9.2 %shard_map.136 = (bf16[1152,512]{1,0:T(8,128)(2,1)S(1)}, bf16[288,1024]{1,0:T(8,128)(2,1)S(1)}, f32[4,512]{1,0:T(4,128)S(1)}) custom-call(s32[8,384]{1,0:T(8,128)S(1)} %copy-done.9, f32[4,144,144]{2,1,0:T(8,128)S(1)} %get-tuple-element.24.bias, bf16[1152,512]{1,0:T(8,128)(2,1)S(1)} %shard_map.135.part_ref, ...), custom_call_target="tpu_custom_call" | custom-call | flops 8000000000 | bytes 18879492 | tf_op jit(solution)/shard_map/pallas_call | solution.py:543
  42.1 2.1 %shard_map.137 = (bf16[288,512]{1,0:T(8,128)(2,1)S(1)}, bf16[288,512]{1,0:T(8,128)(2,1)S(1)}, bf16[288,512]{1,0:T(8,128)(2,1)S(1)}, bf16[288,512]{1,0:T(8,128)(2,1)S(1)}) custom-call(s32[8,384]{1,0:T(8,128)S(1)} %copy-done.9, bf16[1152,512]{1,0:T(8,128)(2,1)S(1)} %get-tuple-element.39.fine_ref, bf16[288,1024]{1,0:T(8,128)(2,1)S(1)} %get-tuple-element.40.upper_ref, ...), custom_call_target="tpu_custom_call" | custom-call | flops 2000000000 | bytes 5976064 | tf_op jit(solution)/shard_map/pallas_call | solution.py:543
  44.2 0.1 collective-permute-start.6
  44.3 0.1 collective-permute-start.7
  44.4 1.2 %collective-permute-start.8 = (bf16[288,512]{1,0:T(8,128)(2,1)S(1)}, bf16[288,512]{1,0:T(8,128)(2,1)S(1)}, u32[]{:S(2)}, u32[]{:S(2)}) collective-permute-start(bf16[288,512]{1,0:T(8,128)(2,1)S(1)} %get-tuple-element.44), channel_id=1, source_target_pairs={{0,9},{1,10},{2,11},{3,12},{4,13},{5,14},{6,15},{7,8},{8,17},{9,18... | collective-permute-start | bytes 884744 | tf_op jit(solution)/shard_map/ppermute | solution.py:512
  45.6 3.5 %collective-permute-start.9 = (f32[4,512]{1,0:T(4,128)S(1)}, f32[4,512]{1,0:T(4,128)S(1)}, u32[]{:S(2)}, u32[]{:S(2)}) collective-permute-start(f32[4,512]{1,0:T(4,128)S(1)} %get-tuple-element.45), channel_id=1, source_target_pairs={{0,8},{8,0},{16,24},{24,16},{1,9},{9,1},{17,25},{25,17},{2,10},{10... | collective-permute-start | bytes 24584 | tf_op jit(solution)/shard_map/ppermute | solution.py:491
  49.1 13.2 %collective-permute-done.9 = f32[4,512]{1,0:T(4,128)S(1)} collective-permute-done((f32[4,512]{1,0:T(4,128)S(1)}, f32[4,512]{1,0:T(4,128)S(1)}, u32[]{:S(2)}, u32[]{:S(2)}) %collective-permute-start.9) | collective-permute-done | bytes 8224 | tf_op jit(solution)/shard_map/ppermute | solution.py:491
  62.3 0.6 collective-permute-start.10
  62.9 4.0 %collective-permute-done.10 = f32[4,512]{1,0:T(4,128)S(1)} collective-permute-done((f32[4,512]{1,0:T(4,128)S(1)}, f32[4,512]{1,0:T(4,128)S(1)}, u32[]{:S(2)}, u32[]{:S(2)}) %collective-permute-start.10) | collective-permute-done | bytes 8224 | tf_op jit(solution)/shard_map/ppermute | solution.py:491
  66.9 1.2 %collective-permute-done.11 = f32[4,512]{1,0:T(4,128)S(1)} collective-permute-done((f32[4,512]{1,0:T(4,128)S(1)}, f32[4,512]{1,0:T(4,128)S(1)}, u32[]{:S(2)}, u32[]{:S(2)}) %collective-permute-start.11) | collective-permute-done | bytes 8224 | tf_op jit(solution)/shard_map/ppermute | solution.py:491
  68.0 0.6 collective-permute-start.12
  68.7 3.0 %collective-permute-done.12 = f32[4,512]{1,0:T(4,128)S(1)} collective-permute-done((f32[4,512]{1,0:T(4,128)S(1)}, f32[4,512]{1,0:T(4,128)S(1)}, u32[]{:S(2)}, u32[]{:S(2)}) %collective-permute-start.12) | collective-permute-done | bytes 8224 | tf_op jit(solution)/shard_map/ppermute | solution.py:491
  71.7 1.2 %collective-permute-start.13 = (f32[4,512]{1,0:T(4,128)S(1)}, f32[4,512]{1,0:T(4,128)S(1)}, u32[]{:S(2)}, u32[]{:S(2)}) collective-permute-start(f32[4,512]{1,0:T(4,128)S(1)} %add.18), channel_id=1, source_target_pairs={{0,4},{1,5},{2,6},{3,7},{4,0},{5,1},{6,2},{7,3},{8,12},{9,13},{10,... | collective-permute-start | bytes 24584 | tf_op jit(solution)/shard_map/ppermute | solution.py:491
  72.9 2.5 %collective-permute-done.13 = f32[4,512]{1,0:T(4,128)S(1)} collective-permute-done((f32[4,512]{1,0:T(4,128)S(1)}, f32[4,512]{1,0:T(4,128)S(1)}, u32[]{:S(2)}, u32[]{:S(2)}) %collective-permute-start.13) | collective-permute-done | bytes 8224 | tf_op jit(solution)/shard_map/ppermute | solution.py:491
  75.4 0.6 add.19
  76.0 1.8 %shard_map.138 = bf16[1152,512]{1,0:T(8,128)(2,1)} custom-call(s32[8,384]{1,0:T(8,128)S(1)} %copy-done.9, bf16[288,512]{1,0:T(8,128)(2,1)S(1)} %get-tuple-element.41.own_ref, bf16[288,512]{1,0:T(8,128)(2,1)S(1)} %collective-permute-done.6.lon_ref, bf16[288,512]{1,0:T(8,128)(2,1)S(1)} %collective-permute-done.7.lat_ref, ...), custom_call_target="tpu_custom_call" | custom-call | flops 1000000000 | bytes 1191936 | tf_op jit(solution)/shard_map/pallas_call | solution.py:543
  (36 shorter events, 0.1 us)
Async XLA Ops:
  0.6 10.2 %copy-start.4 = (bf16[4,12,24,512]{3,2,1,0:T(8,128)(2,1)S(1)}, bf16[4,12,24,512]{3,2,1,0:T(8,128)(2,1)}, u32[]{:S(2)}) copy-start(bf16[4,12,24,512]{3,2,1,0:T(8,128)(2,1)} %x_hbm.1) | copy-start | bytes 3538948
  0.6 10.2 %copy-start.5 = (bf16[512,512]{1,0:T(8,128)(2,1)S(1)}, bf16[512,512]{1,0:T(8,128)(2,1)}, u32[]{:S(2)}) copy-start(bf16[512,512]{1,0:T(8,128)(2,1)} %wo_ref.4) | copy-start | bytes 1572868
  0.7 10.2 %copy-start.3 = (bf16[512,1536]{1,0:T(8,128)(2,1)S(1)}, bf16[512,1536]{1,0:T(8,128)(2,1)}, u32[]{:S(2)}) copy-start(bf16[512,1536]{1,0:T(8,128)(2,1)} %w_ref.3) | copy-start | bytes 4718596
  0.7 10.2 %copy-start.8 = (f32[512]{0:T(512)S(1)}, f32[512]{0:T(512)}, u32[]{:S(2)}) copy-start(f32[512]{0:T(512)} %param.13) | copy-start | bytes 6148
  3.1 24.8 %collective-permute-start.2 = (bf16[72,512]{1,0:T(8,128)(2,1)}, bf16[72,512]{1,0:T(8,128)(2,1)}, u32[]{:S(2)}, u32[]{:S(2)}) collective-permute-start(bf16[72,512]{1,0:T(8,128)(2,1)} %get-tuple-element.35), channel_id=1, source_target_pairs={{0,31},{1,24},{2,25},{3,26},{4,27},{5,28},{6,29},{7,30},{8,7},{9,0... | collective-permute-start | bytes 221192 | tf_op jit(solution)/shard_map/ppermute | solution.py:512
  9.5 11.6 %collective-permute-start = (bf16[216,512]{1,0:T(8,128)(2,1)}, bf16[216,512]{1,0:T(8,128)(2,1)S(1)}, u32[]{:S(2)}, u32[]{:S(2)}) collective-permute-start(bf16[216,512]{1,0:T(8,128)(2,1)} %get-tuple-element.28), channel_id=1, source_target_pairs={{0,7},{1,0},{2,1},{3,2},{4,3},{5,4},{6,5},{7,6},{8,15},{9,8},{10,9... | collective-permute-start | bytes 663560 | tf_op jit(solution)/shard_map/ppermute | solution.py:512
  10.4 7.3 %collective-permute-start.1 = (bf16[216,512]{1,0:T(8,128)(2,1)}, bf16[216,512]{1,0:T(8,128)(2,1)}, u32[]{:S(2)}, u32[]{:S(2)}) collective-permute-start(bf16[216,512]{1,0:T(8,128)(2,1)} %get-tuple-element.32), channel_id=1, source_target_pairs={{0,24},{1,25},{2,26},{3,27},{4,28},{5,29},{6,30},{7,31},{8,0},{9,1... | collective-permute-start | bytes 663560 | tf_op jit(solution)/shard_map/ppermute | solution.py:512
  14.9 17.2 %collective-permute-start.5 = (bf16[96,512]{1,0:T(8,128)(2,1)S(1)}, bf16[96,512]{1,0:T(8,128)(2,1)S(1)}, u32[]{:S(2)}, u32[]{:S(2)}) collective-permute-start(bf16[96,512]{1,0:T(8,128)(2,1)S(1)} %get-tuple-element.38), channel_id=1, source_target_pairs={{0,31},{1,24},{2,25},{3,26},{4,27},{5,28},{6,29},{7,30},{8,7},{9,0... | collective-permute-start | bytes 294920 | tf_op jit(solution)/shard_map/ppermute | solution.py:512
  21.1 11.0 %collective-permute-start.4 = (bf16[224,512]{1,0:T(8,128)(2,1)S(1)}, bf16[224,512]{1,0:T(8,128)(2,1)S(1)}, u32[]{:S(2)}, u32[]{:S(2)}) collective-permute-start(bf16[224,512]{1,0:T(8,128)(2,1)S(1)} %get-tuple-element.37), channel_id=1, source_target_pairs={{0,7},{1,0},{2,1},{3,2},{4,3},{5,4},{6,5},{7,6},{8,15},{9,8},{10,9... | collective-permute-start | bytes 688136 | tf_op jit(solution)/shard_map/ppermute | solution.py:512
  21.2 6.7 %copy-start.9 = (s32[8,384]{1,0:T(8,128)S(1)}, s32[8,384]{1,0:T(8,128)}, u32[]{:S(2)}) copy-start(s32[8,384]{1,0:T(8,128)} %constant.11.clone.maps_ref) | copy-start | bytes 36868
  21.2 11.6 %slice-start = ((s8[6291456]{0:T(1024)(128)(4,1)}), s8[4194304]{0:T(1024)(128)(4,1)S(1)}, s32[]{:S(2)}) async-start(s8[6291456]{0:T(1024)(128)(4,1)} %bitcast.7), calls=%async_computation | async-start | bytes 8388608
  23.6 9.2 %collective-permute-start.3 = (bf16[224,512]{1,0:T(8,128)(2,1)S(1)}, bf16[224,512]{1,0:T(8,128)(2,1)S(1)}, u32[]{:S(2)}, u32[]{:S(2)}) collective-permute-start(bf16[224,512]{1,0:T(8,128)(2,1)S(1)} %get-tuple-element.36), channel_id=1, source_target_pairs={{0,24},{1,25},{2,26},{3,27},{4,28},{5,29},{6,30},{7,31},{8,0},{9,1... | collective-permute-start | bytes 688136 | tf_op jit(solution)/shard_map/ppermute | solution.py:512
  27.9 4.9 %slice-start.1 = ((s8[6291456]{0:T(1024)(128)(4,1)}), s8[2097152]{0:T(1024)(128)(4,1)S(1)}, s32[]{:S(2)}) async-start(s8[6291456]{0:T(1024)(128)(4,1)} %bitcast.7), calls=%async_computation.1 | async-start | bytes 4194304
  27.9 4.9 %copy-start = (bf16[2048,1024]{1,0:T(8,128)(2,1)S(1)}, bf16[2048,1024]{1,0:T(8,128)(2,1)}, u32[]{:S(2)}) copy-start(bf16[2048,1024]{1,0:T(8,128)(2,1)} %wm_ref.1) | copy-start | bytes 12582916
  27.9 4.9 %copy-start.1 = (bf16[1024,2048]{1,0:T(8,128)(2,1)S(1)}, bf16[1024,2048]{1,0:T(8,128)(2,1)}, u32[]{:S(2)}) copy-start(bf16[1024,2048]{1,0:T(8,128)(2,1)} %wsp_ref.3) | copy-start | bytes 12582916
  27.9 4.9 %copy-start.2 = (bf16[1024,1024]{1,0:T(8,128)(2,1)S(1)}, bf16[1024,1024]{1,0:T(8,128)(2,1)}, u32[]{:S(2)}) copy-start(bf16[1024,1024]{1,0:T(8,128)(2,1)} %wo_ref.5) | copy-start | bytes 6291460
  27.9 4.9 %copy-start.6 = (f32[2048]{0:T(1024)S(1)}, f32[2048]{0:T(1024)}, u32[]{:S(2)}) copy-start(f32[2048]{0:T(1024)} %param.16) | copy-start | bytes 24580
  27.9 4.9 %copy-start.7 = (f32[1024]{0:T(1024)S(1)}, f32[1024]{0:T(1024)}, u32[]{:S(2)}) copy-start(f32[1024]{0:T(1024)} %param.18) | copy-start | bytes 12292
  27.9 4.9 %copy-start.10 = (f32[4,2,288]{2,1,0:T(2,128)S(1)}, f32[4,2,288]{2,1,0:T(2,128)}, u32[]{:S(2)}) copy-start(f32[4,2,288]{2,1,0:T(2,128)} %constant.12.clone.weight_ref) | copy-start | bytes 27652
  44.2 31.7 %collective-permute-start.6 = (bf16[288,512]{1,0:T(8,128)(2,1)S(1)}, bf16[288,512]{1,0:T(8,128)(2,1)S(1)}, u32[]{:S(2)}, u32[]{:S(2)}) collective-permute-start(bf16[288,512]{1,0:T(8,128)(2,1)S(1)} %get-tuple-element.42), channel_id=1, source_target_pairs={{0,1},{1,2},{2,3},{3,4},{4,5},{5,6},{6,7},{7,0},{8,9},{9,10},{10,1... | collective-permute-start | bytes 884744 | tf_op jit(solution)/shard_map/ppermute | solution.py:512
  44.3 31.7 %collective-permute-start.7 = (bf16[288,512]{1,0:T(8,128)(2,1)S(1)}, bf16[288,512]{1,0:T(8,128)(2,1)S(1)}, u32[]{:S(2)}, u32[]{:S(2)}) collective-permute-start(bf16[288,512]{1,0:T(8,128)(2,1)S(1)} %get-tuple-element.43), channel_id=1, source_target_pairs={{0,8},{1,9},{2,10},{3,11},{4,12},{5,13},{6,14},{7,15},{8,16},{9,17... | collective-permute-start | bytes 884744 | tf_op jit(solution)/shard_map/ppermute | solution.py:512
  44.4 31.6 %collective-permute-start.8 = (bf16[288,512]{1,0:T(8,128)(2,1)S(1)}, bf16[288,512]{1,0:T(8,128)(2,1)S(1)}, u32[]{:S(2)}, u32[]{:S(2)}) collective-permute-start(bf16[288,512]{1,0:T(8,128)(2,1)S(1)} %get-tuple-element.44), channel_id=1, source_target_pairs={{0,9},{1,10},{2,11},{3,12},{4,13},{5,14},{6,15},{7,8},{8,17},{9,18... | collective-permute-start | bytes 884744 | tf_op jit(solution)/shard_map/ppermute | solution.py:512
  45.6 16.7 %collective-permute-start.9 = (f32[4,512]{1,0:T(4,128)S(1)}, f32[4,512]{1,0:T(4,128)S(1)}, u32[]{:S(2)}, u32[]{:S(2)}) collective-permute-start(f32[4,512]{1,0:T(4,128)S(1)} %get-tuple-element.45), channel_id=1, source_target_pairs={{0,8},{8,0},{16,24},{24,16},{1,9},{9,1},{17,25},{25,17},{2,10},{10... | collective-permute-start | bytes 24584 | tf_op jit(solution)/shard_map/ppermute | solution.py:491
  62.3 4.5 %collective-permute-start.10 = (f32[4,512]{1,0:T(4,128)S(1)}, f32[4,512]{1,0:T(4,128)S(1)}, u32[]{:S(2)}, u32[]{:S(2)}) collective-permute-start(f32[4,512]{1,0:T(4,128)S(1)} %add.15), channel_id=1, source_target_pairs={{0,16},{8,24},{16,0},{24,8},{1,17},{9,25},{17,1},{25,9},{2,18},{10... | collective-permute-start | bytes 24584 | tf_op jit(solution)/shard_map/ppermute | solution.py:491
  66.9 1.2 %collective-permute-start.11 = (f32[4,512]{1,0:T(4,128)S(1)}, f32[4,512]{1,0:T(4,128)S(1)}, u32[]{:S(2)}, u32[]{:S(2)}) collective-permute-start(f32[4,512]{1,0:T(4,128)S(1)} %add.16), channel_id=1, source_target_pairs={{0,1},{1,0},{2,3},{3,2},{4,5},{5,4},{6,7},{7,6},{8,9},{9,8},{10,11... | collective-permute-start | bytes 24584 | tf_op jit(solution)/shard_map/ppermute | solution.py:491
  68.0 3.7 %collective-permute-start.12 = (f32[4,512]{1,0:T(4,128)S(1)}, f32[4,512]{1,0:T(4,128)S(1)}, u32[]{:S(2)}, u32[]{:S(2)}) collective-permute-start(f32[4,512]{1,0:T(4,128)S(1)} %add.17), channel_id=1, source_target_pairs={{0,2},{1,3},{2,0},{3,1},{4,6},{5,7},{6,4},{7,5},{8,10},{9,11},{10,... | collective-permute-start | bytes 24584 | tf_op jit(solution)/shard_map/ppermute | solution.py:491
  71.7 3.7 %collective-permute-start.13 = (f32[4,512]{1,0:T(4,128)S(1)}, f32[4,512]{1,0:T(4,128)S(1)}, u32[]{:S(2)}, u32[]{:S(2)}) collective-permute-start(f32[4,512]{1,0:T(4,128)S(1)} %add.18), channel_id=1, source_target_pairs={{0,4},{1,5},{2,6},{3,7},{4,0},{5,1},{6,2},{7,3},{8,12},{9,13},{10,... | collective-permute-start | bytes 24584 | tf_op jit(solution)/shard_map/ppermute | solution.py:491

commit v2 on v1

--- a/solution.py
+++ b/solution.py
@@ -418,7 +418,7 @@
     normed = normed_rows(coarse, gs_ref[...])
     qkv[...] = jnp.dot(normed, ws_ref[...], preferred_element_type=jnp.float32).astype(jnp.bfloat16)
 
-    at_once = 4
+    at_once = 8
 
     @pl.loop(0, wide // LANES // at_once)
     def _(step):
@@ -467,7 +467,10 @@
             out[i * quarter : (i + 1) * quarter, :] = moved[q * quarter : (q + 1) * quarter]
 
 
-def output_kernel(plan, keys, maps_ref, own_ref, lon_ref, lat_ref, diag_ref, out_ref):
+def output_kernel(
+    plan, keys, maps_ref, own_ref, lon_ref, lat_ref, diag_ref, sums_ref, other_ref, out_ref, means_ref
+):
+    means_ref[...] = sums_ref[...] + other_ref[...]
     span = own_ref.shape[0] // plan.levels
     tile = plan.height * plan.width
     hot = table_hot(maps_ref, keys["output"])
@@ -480,17 +483,18 @@
         out_ref[lv * tile : (lv + 1) * tile, :] = moved.astype(jnp.bfloat16)
 
 
-def all_summed(value, axes):
-    for axis in axes:
+def all_but_summed(value):
+    steps = {}
+    for axis in ("lat", "lon"):
         count = lax.axis_size(axis)
-        if count & (count - 1):
-            value = lax.psum(value, axis)
-            continue
-        step = 1
-        while step < count:
-            value = value + lax.ppermute(value, axis, [(i, i ^ step) for i in range(count)])
-            step *= 2
-    return value
+        assert count & (count - 1) == 0
+        steps[axis] = [(axis, 1 << i) for i in range(count.bit_length() - 1)]
+    order = steps["lat"][:1] + steps["lon"][1:] + steps["lon"][:1] + steps["lat"][1:]
+    other = jnp.zeros_like(value)
+    for number, (axis, step) in enumerate(order):
+        value = value if number == 0 else value + other
+        other = lax.ppermute(value, axis, [(i, i ^ step) for i in range(lax.axis_size(axis))])
+    return value, other
 
 
 def whole_step(
@@ -634,10 +638,11 @@
         flops=2 * 10**9, limit=LIMITS["split"],
     )
     d_lat, d_lon, d_diag = (moved(s_lat, 1, 0), moved(s_lon, 0, 1), moved(s_diag, 1, 1))
-    means = all_summed(sums, ("lat", "lon"))
-    (decoded,) = call(
+    sums, other_sums = all_but_summed(sums)
+    decoded, means = call(
         functools.partial(output_kernel, plan, keys),
-        rows_of(levels * height * width), (table, own, d_lon, d_lat, d_diag), flops=10**9, limit=LIMITS["output"],
+        rows_of(levels * height * width) + [((levels, channels), jnp.float32)],
+        (table, own, d_lon, d_lat, d_diag, sums, other_sums), flops=10**9, limit=LIMITS["output"],
     )
     return decoded.reshape(latent.shape), means
 

time: 77.9 us -> 75.9 us (0.974)
  Pallas kernels: 29.6 us -> 28.2 us
    pallas_call x8, Pallas kernels: 29.6 us -> 28.2 us  [call(): pl.pallas_call(body, out_shape=[jax.ShapeDtypeStruct(s, d) for s, d in ou...]
  transfers between devices with their start and end apart: 14 -> 14, of which waited for: 7 -> 7; matrix products, arithmetic and copies ran while one was open for 1% -> 0% of each run, Pallas kernels for 18% -> 19%
where the time goes in v2:
time: 75.9 us; the launch traced here: 75.8 us
  Pallas kernels  28.2 us (37%)
  waiting for transfers between devices  27.2 us (36%)
  starting transfers between devices  19.4 us (26%)
  between operations  0.9 us (1%)
    pallas_call x8, Pallas kernels, call(): pl.pallas_call(body, out_shape=[jax.ShapeDtypeStruct(s, d) for s, d in ou...  28.2 us
    ppermute x5, waiting for transfers between devices, all_but_summed(): lax.ppermute(value, axis, [(i, i ^ step) for i in range(lax.axis_size(axi...  23.8 us
    ppermute x9, starting transfers between devices, moved(): return lax.ppermute(value, ('lat', 'lon'), pairs)  13.4 us
    ppermute x5, starting transfers between devices, all_but_summed(): lax.ppermute(value, axis, [(i, i ^ step) for i in range(lax.axis_size(axi...  5.93 us
    ppermute x9, waiting for transfers between devices, moved(): return lax.ppermute(value, ('lat', 'lon'), pairs)  3.41 us
  transfers between devices with their start and end apart: 14, of which 7 were waited for; matrix products, arithmetic and copies ran while one was open for 0% of the time, Pallas kernels for 19%

profile of v2, /device:TPU:0, one launch (start us, length us, event | category | flops | bytes accessed | tf_op | source)
XLA Modules:
  0.0 75.8 jit_solution(8696528029577364351)
XLA Ops:
  0.7 2.4 %shard_map.132 = (bf16[216,512]{1,0:T(8,128)(2,1)}, bf16[72,512]{1,0:T(8,128)(2,1)}, bf16[216,512]{1,0:T(8,128)(2,1)}) custom-call(bf16[4,12,24,512]{3,2,1,0:T(8,128)(2,1)} %x_hbm.1), custom_call_target="tpu_custom_call" | custom-call | flops 1000000000 | bytes 1179648 | tf_op jit(solution)/shard_map/pallas_call | solution.py:547
  3.1 6.5 %collective-permute-start.2 = (bf16[72,512]{1,0:T(8,128)(2,1)}, bf16[72,512]{1,0:T(8,128)(2,1)}, u32[]{:S(2)}, u32[]{:S(2)}) collective-permute-start(bf16[72,512]{1,0:T(8,128)(2,1)} %get-tuple-element.37), channel_id=1, source_target_pairs={{0,31},{1,24},{2,25},{3,26},{4,27},{5,28},{6,29},{7,30},{8,7},{9,0... | collective-permute-start | bytes 221192 | tf_op jit(solution)/shard_map/ppermute | solution.py:516
  9.5 0.9 %collective-permute-start = (bf16[216,512]{1,0:T(8,128)(2,1)}, bf16[216,512]{1,0:T(8,128)(2,1)S(1)}, u32[]{:S(2)}, u32[]{:S(2)}) collective-permute-start(bf16[216,512]{1,0:T(8,128)(2,1)} %get-tuple-element.30), channel_id=1, source_target_pairs={{0,7},{1,0},{2,1},{3,2},{4,3},{5,4},{6,5},{7,6},{8,15},{9,8},{10,9... | collective-permute-start | bytes 663560 | tf_op jit(solution)/shard_map/ppermute | solution.py:516
  10.4 0.4 collective-permute-start.1
  10.8 4.1 %shard_map.131 = (bf16[288,512]{1,0:T(8,128)(2,1)S(1)}, bf16[288,512]{1,0:T(8,128)(2,1)S(1)}, bf16[288,512]{1,0:T(8,128)(2,1)S(1)}, bf16[288,512]{1,0:T(8,128)(2...) custom-call(s32[1]{0:T(128)} %bitcast.edge_ref, ...), custom_call_target="tpu_custom_call" | custom-call | flops 4000000000 | bytes 3278852 | tf_op jit(solution)/shard_map/pallas_call | solution.py:547
  14.9 0.1 collective-permute-start.5
  15.0 2.7 %collective-permute-done.1.more_0_.lat_ref = bf16[216,512]{1,0:T(8,128)(2,1)} collective-permute-done((bf16[216,512]{1,0:T(8,128)(2,1)}, bf16[216,512]{1,0:T(8,128)(2,1)}, u32[]{:S(2)}, u32[]{:S(2)}) %collective-permute-start.1) | collective-permute-done | bytes 221216 | tf_op jit(solution)/shard_map/ppermute | solution.py:516
  17.7 3.4 %shard_map.134 = (bf16[288,512]{1,0:T(8,128)(2,1)S(1)}, bf16[224,512]{1,0:T(8,128)(2,1)S(1)}) custom-call(f32[4,144,144]{2,1,0:T(8,128)S(1)} %get-tuple-element.26.bias, bf16[224,512]{1,0:T(8,128)(2,1)S(1)} %get-tuple-element.32.sent_ref, bf16[288,512]{1,0:T(8,128)(2,1)S(1)} %get-tuple-element.33.rest_ref, ...), custom_call_target="tpu_custom_call" | custom-call | flops 2000000000 | bytes 3176448 | tf_op jit(solution)/shard_map/pallas_call | solution.py:547
  21.1 0.1 collective-permute-start.4
  21.2 0.0 copy-start.9
  21.2 0.0 slice-start
  21.2 2.4 %shard_map.133 = (bf16[288,512]{1,0:T(8,128)(2,1)S(1)}, bf16[224,512]{1,0:T(8,128)(2,1)S(1)}) custom-call(f32[4,144,144]{2,1,0:T(8,128)S(1)} %get-tuple-element.26.bias, bf16[224,512]{1,0:T(8,128)(2,1)S(1)} %get-tuple-element.28.sent_ref, bf16[288,512]{1,0:T(8,128)(2,1)S(1)} %get-tuple-element.29.rest_ref, ...), custom_call_target="tpu_custom_call" | custom-call | flops 2000000000 | bytes 3176448 | tf_op jit(solution)/shard_map/pallas_call | solution.py:547
  23.6 4.2 %collective-permute-start.3 = (bf16[224,512]{1,0:T(8,128)(2,1)S(1)}, bf16[224,512]{1,0:T(8,128)(2,1)S(1)}, u32[]{:S(2)}, u32[]{:S(2)}) collective-permute-start(bf16[224,512]{1,0:T(8,128)(2,1)S(1)} %get-tuple-element.38), channel_id=1, source_target_pairs={{0,24},{1,25},{2,26},{3,27},{4,28},{5,29},{6,30},{7,31},{8,0},{9,1... | collective-permute-start | bytes 688136 | tf_op jit(solution)/shard_map/ppermute | solution.py:516
  27.9 0.0 copy-start.1
  27.9 0.0 copy-start.10
  27.9 4.1 %shard_map.135.part_ref = bf16[1152,512]{1,0:T(8,128)(2,1)S(1)} custom-call(s32[8,384]{1,0:T(8,128)S(1)} %copy-done.9, f32[4,144,144]{2,1,0:T(8,128)S(1)} %get-tuple-element.26.bias, bf16[288,512]{1,0:T(8,128)(2,1)S(1)} %get-tuple-element.27.first_ref, bf16[288,512]{1,0:T(8,128)(2,1)S(1)} %get-tuple-element.31.right_ref, ...), custom_call_target="tpu_custom_call" | custom-call | flops 4000000000 | bytes 4139008 | tf_op jit(solution)/shard_map/pallas_call | solution.py:547
  32.1 0.7 collective-permute-done.3.lat_ref
  32.9 7.8 %shard_map.136 = (bf16[1152,512]{1,0:T(8,128)(2,1)S(1)}, bf16[288,1024]{1,0:T(8,128)(2,1)S(1)}, f32[4,512]{1,0:T(4,128)S(1)}) custom-call(s32[8,384]{1,0:T(8,128)S(1)} %copy-done.9, f32[4,144,144]{2,1,0:T(8,128)S(1)} %get-tuple-element.26.bias, bf16[1152,512]{1,0:T(8,128)(2,1)S(1)} %shard_map.135.part_ref, ...), custom_call_target="tpu_custom_call" | custom-call | flops 8000000000 | bytes 18879492 | tf_op jit(solution)/shard_map/pallas_call | solution.py:547
  40.7 2.1 %shard_map.137 = (bf16[288,512]{1,0:T(8,128)(2,1)S(1)}, bf16[288,512]{1,0:T(8,128)(2,1)S(1)}, bf16[288,512]{1,0:T(8,128)(2,1)S(1)}, bf16[288,512]{1,0:T(8,128)(2,1)S(1)}) custom-call(s32[8,384]{1,0:T(8,128)S(1)} %copy-done.9, bf16[1152,512]{1,0:T(8,128)(2,1)S(1)} %get-tuple-element.41.fine_ref, bf16[288,1024]{1,0:T(8,128)(2,1)S(1)} %get-tuple-element.42.upper_ref, ...), custom_call_target="tpu_custom_call" | custom-call | flops 2000000000 | bytes 5976064 | tf_op jit(solution)/shard_map/pallas_call | solution.py:547
  42.8 0.1 collective-permute-start.6
  42.9 0.1 collective-permute-start.7
  43.0 1.2 %collective-permute-start.8 = (bf16[288,512]{1,0:T(8,128)(2,1)S(1)}, bf16[288,512]{1,0:T(8,128)(2,1)S(1)}, u32[]{:S(2)}, u32[]{:S(2)}) collective-permute-start(bf16[288,512]{1,0:T(8,128)(2,1)S(1)} %get-tuple-element.46), channel_id=1, source_target_pairs={{0,9},{1,10},{2,11},{3,12},{4,13},{5,14},{6,15},{7,8},{8,17},{9,18... | collective-permute-start | bytes 884744 | tf_op jit(solution)/shard_map/ppermute | solution.py:516
  44.2 3.5 %collective-permute-start.9 = (f32[4,512]{1,0:T(4,128)S(1)}, f32[4,512]{1,0:T(4,128)S(1)}, u32[]{:S(2)}, u32[]{:S(2)}) collective-permute-start(f32[4,512]{1,0:T(4,128)S(1)} %get-tuple-element.47), channel_id=1, source_target_pairs={{0,8},{8,0},{16,24},{24,16},{1,9},{9,1},{17,25},{25,17},{2,10},{10... | collective-permute-start | bytes 24584 | tf_op jit(solution)/shard_map/ppermute | solution.py:496
  47.7 13.2 %collective-permute-done.9 = f32[4,512]{1,0:T(4,128)S(1)} collective-permute-done((f32[4,512]{1,0:T(4,128)S(1)}, f32[4,512]{1,0:T(4,128)S(1)}, u32[]{:S(2)}, u32[]{:S(2)}) %collective-permute-start.9) | collective-permute-done | bytes 8224 | tf_op jit(solution)/shard_map/ppermute | solution.py:496
  60.9 0.6 collective-permute-start.10
  61.5 3.0 %collective-permute-done.10 = f32[4,512]{1,0:T(4,128)S(1)} collective-permute-done((f32[4,512]{1,0:T(4,128)S(1)}, f32[4,512]{1,0:T(4,128)S(1)}, u32[]{:S(2)}, u32[]{:S(2)}) %collective-permute-start.10) | collective-permute-done | bytes 8224 | tf_op jit(solution)/shard_map/ppermute | solution.py:496
  64.6 1.2 %collective-permute-start.11 = (f32[4,512]{1,0:T(4,128)S(1)}, f32[4,512]{1,0:T(4,128)S(1)}, u32[]{:S(2)}, u32[]{:S(2)}) collective-permute-start(f32[4,512]{1,0:T(4,128)S(1)} %add.13), channel_id=1, source_target_pairs={{0,4},{1,5},{2,6},{3,7},{4,0},{5,1},{6,2},{7,3},{8,12},{9,13},{10,... | collective-permute-start | bytes 24584 | tf_op jit(solution)/shard_map/ppermute | solution.py:496
  65.7 2.5 %collective-permute-done.11 = f32[4,512]{1,0:T(4,128)S(1)} collective-permute-done((f32[4,512]{1,0:T(4,128)S(1)}, f32[4,512]{1,0:T(4,128)S(1)}, u32[]{:S(2)}, u32[]{:S(2)}) %collective-permute-start.11) | collective-permute-done | bytes 8224 | tf_op jit(solution)/shard_map/ppermute | solution.py:496
  68.2 1.2 %collective-permute-done.12 = f32[4,512]{1,0:T(4,128)S(1)} collective-permute-done((f32[4,512]{1,0:T(4,128)S(1)}, f32[4,512]{1,0:T(4,128)S(1)}, u32[]{:S(2)}, u32[]{:S(2)}) %collective-permute-start.12) | collective-permute-done | bytes 8224 | tf_op jit(solution)/shard_map/ppermute | solution.py:496
  69.4 0.6 collective-permute-start.13
  70.0 4.0 %collective-permute-done.13.other_ref = f32[4,512]{1,0:T(4,128)S(1)} collective-permute-done((f32[4,512]{1,0:T(4,128)S(1)}, f32[4,512]{1,0:T(4,128)S(1)}, u32[]{:S(2)}, u32[]{:S(2)}) %collective-permute-start.13) | collective-permute-done | bytes 8224 | tf_op jit(solution)/shard_map/ppermute | solution.py:496
  74.0 1.8 %shard_map.138 = (bf16[1152,512]{1,0:T(8,128)(2,1)}, f32[4,512]{1,0:T(4,128)}) custom-call(s32[8,384]{1,0:T(8,128)S(1)} %copy-done.9, bf16[288,512]{1,0:T(8,128)(2,1)S(1)} %get-tuple-element.43.own_ref, bf16[288,512]{1,0:T(8,128)(2,1)S(1)} %collective-permute-done.6.lon_ref, bf16[288,512]{1,0:T(8,128)(2,1)S(1)} %collective-permute-done.7.lat_ref, ...), custom_call_target="tpu_custom_call" | custom-call | flops 1000000000 | bytes 1208320 | tf_op jit(solution)/shard_map/pallas_call | solution.py:547
  (35 shorter events, 0.1 us)
Async XLA Ops:
  0.6 10.2 %copy-start.4 = (bf16[4,12,24,512]{3,2,1,0:T(8,128)(2,1)S(1)}, bf16[4,12,24,512]{3,2,1,0:T(8,128)(2,1)}, u32[]{:S(2)}) copy-start(bf16[4,12,24,512]{3,2,1,0:T(8,128)(2,1)} %x_hbm.1) | copy-start | bytes 3538948
  0.6 10.2 %copy-start.5 = (bf16[512,512]{1,0:T(8,128)(2,1)S(1)}, bf16[512,512]{1,0:T(8,128)(2,1)}, u32[]{:S(2)}) copy-start(bf16[512,512]{1,0:T(8,128)(2,1)} %wo_ref.4) | copy-start | bytes 1572868
  0.7 10.2 %copy-start.3 = (bf16[512,1536]{1,0:T(8,128)(2,1)S(1)}, bf16[512,1536]{1,0:T(8,128)(2,1)}, u32[]{:S(2)}) copy-start(bf16[512,1536]{1,0:T(8,128)(2,1)} %w_ref.3) | copy-start | bytes 4718596
  0.7 10.2 %copy-start.8 = (f32[512]{0:T(512)S(1)}, f32[512]{0:T(512)}, u32[]{:S(2)}) copy-start(f32[512]{0:T(512)} %param.13) | copy-start | bytes 6148
  3.1 24.8 %collective-permute-start.2 = (bf16[72,512]{1,0:T(8,128)(2,1)}, bf16[72,512]{1,0:T(8,128)(2,1)}, u32[]{:S(2)}, u32[]{:S(2)}) collective-permute-start(bf16[72,512]{1,0:T(8,128)(2,1)} %get-tuple-element.37), channel_id=1, source_target_pairs={{0,31},{1,24},{2,25},{3,26},{4,27},{5,28},{6,29},{7,30},{8,7},{9,0... | collective-permute-start | bytes 221192 | tf_op jit(solution)/shard_map/ppermute | solution.py:516
  9.5 11.6 %collective-permute-start = (bf16[216,512]{1,0:T(8,128)(2,1)}, bf16[216,512]{1,0:T(8,128)(2,1)S(1)}, u32[]{:S(2)}, u32[]{:S(2)}) collective-permute-start(bf16[216,512]{1,0:T(8,128)(2,1)} %get-tuple-element.30), channel_id=1, source_target_pairs={{0,7},{1,0},{2,1},{3,2},{4,3},{5,4},{6,5},{7,6},{8,15},{9,8},{10,9... | collective-permute-start | bytes 663560 | tf_op jit(solution)/shard_map/ppermute | solution.py:516
  10.4 7.3 %collective-permute-start.1 = (bf16[216,512]{1,0:T(8,128)(2,1)}, bf16[216,512]{1,0:T(8,128)(2,1)}, u32[]{:S(2)}, u32[]{:S(2)}) collective-permute-start(bf16[216,512]{1,0:T(8,128)(2,1)} %get-tuple-element.34), channel_id=1, source_target_pairs={{0,24},{1,25},{2,26},{3,27},{4,28},{5,29},{6,30},{7,31},{8,0},{9,1... | collective-permute-start | bytes 663560 | tf_op jit(solution)/shard_map/ppermute | solution.py:516
  14.9 17.2 %collective-permute-start.5 = (bf16[96,512]{1,0:T(8,128)(2,1)S(1)}, bf16[96,512]{1,0:T(8,128)(2,1)S(1)}, u32[]{:S(2)}, u32[]{:S(2)}) collective-permute-start(bf16[96,512]{1,0:T(8,128)(2,1)S(1)} %get-tuple-element.40), channel_id=1, source_target_pairs={{0,31},{1,24},{2,25},{3,26},{4,27},{5,28},{6,29},{7,30},{8,7},{9,0... | collective-permute-start | bytes 294920 | tf_op jit(solution)/shard_map/ppermute | solution.py:516
  21.1 11.0 %collective-permute-start.4 = (bf16[224,512]{1,0:T(8,128)(2,1)S(1)}, bf16[224,512]{1,0:T(8,128)(2,1)S(1)}, u32[]{:S(2)}, u32[]{:S(2)}) collective-permute-start(bf16[224,512]{1,0:T(8,128)(2,1)S(1)} %get-tuple-element.39), channel_id=1, source_target_pairs={{0,7},{1,0},{2,1},{3,2},{4,3},{5,4},{6,5},{7,6},{8,15},{9,8},{10,9... | collective-permute-start | bytes 688136 | tf_op jit(solution)/shard_map/ppermute | solution.py:516
  21.2 6.7 %copy-start.9 = (s32[8,384]{1,0:T(8,128)S(1)}, s32[8,384]{1,0:T(8,128)}, u32[]{:S(2)}) copy-start(s32[8,384]{1,0:T(8,128)} %constant.11.clone.maps_ref) | copy-start | bytes 36868
  21.2 11.6 %slice-start = ((s8[6291456]{0:T(1024)(128)(4,1)}), s8[4194304]{0:T(1024)(128)(4,1)S(1)}, s32[]{:S(2)}) async-start(s8[6291456]{0:T(1024)(128)(4,1)} %bitcast.7), calls=%async_computation | async-start | bytes 8388608
  23.6 9.2 %collective-permute-start.3 = (bf16[224,512]{1,0:T(8,128)(2,1)S(1)}, bf16[224,512]{1,0:T(8,128)(2,1)S(1)}, u32[]{:S(2)}, u32[]{:S(2)}) collective-permute-start(bf16[224,512]{1,0:T(8,128)(2,1)S(1)} %get-tuple-element.38), channel_id=1, source_target_pairs={{0,24},{1,25},{2,26},{3,27},{4,28},{5,29},{6,30},{7,31},{8,0},{9,1... | collective-permute-start | bytes 688136 | tf_op jit(solution)/shard_map/ppermute | solution.py:516
  27.9 4.9 %slice-start.1 = ((s8[6291456]{0:T(1024)(128)(4,1)}), s8[2097152]{0:T(1024)(128)(4,1)S(1)}, s32[]{:S(2)}) async-start(s8[6291456]{0:T(1024)(128)(4,1)} %bitcast.7), calls=%async_computation.1 | async-start | bytes 4194304
  27.9 4.9 %copy-start = (bf16[2048,1024]{1,0:T(8,128)(2,1)S(1)}, bf16[2048,1024]{1,0:T(8,128)(2,1)}, u32[]{:S(2)}) copy-start(bf16[2048,1024]{1,0:T(8,128)(2,1)} %wm_ref.1) | copy-start | bytes 12582916
  27.9 4.9 %copy-start.1 = (bf16[1024,2048]{1,0:T(8,128)(2,1)S(1)}, bf16[1024,2048]{1,0:T(8,128)(2,1)}, u32[]{:S(2)}) copy-start(bf16[1024,2048]{1,0:T(8,128)(2,1)} %wsp_ref.3) | copy-start | bytes 12582916
  27.9 4.9 %copy-start.2 = (bf16[1024,1024]{1,0:T(8,128)(2,1)S(1)}, bf16[1024,1024]{1,0:T(8,128)(2,1)}, u32[]{:S(2)}) copy-start(bf16[1024,1024]{1,0:T(8,128)(2,1)} %wo_ref.5) | copy-start | bytes 6291460
  27.9 4.9 %copy-start.6 = (f32[2048]{0:T(1024)S(1)}, f32[2048]{0:T(1024)}, u32[]{:S(2)}) copy-start(f32[2048]{0:T(1024)} %param.16) | copy-start | bytes 24580
  27.9 4.9 %copy-start.7 = (f32[1024]{0:T(1024)S(1)}, f32[1024]{0:T(1024)}, u32[]{:S(2)}) copy-start(f32[1024]{0:T(1024)} %param.18) | copy-start | bytes 12292
  27.9 4.9 %copy-start.10 = (f32[4,2,288]{2,1,0:T(2,128)S(1)}, f32[4,2,288]{2,1,0:T(2,128)}, u32[]{:S(2)}) copy-start(f32[4,2,288]{2,1,0:T(2,128)} %constant.12.clone.weight_ref) | copy-start | bytes 27652
  42.8 31.1 %collective-permute-start.6 = (bf16[288,512]{1,0:T(8,128)(2,1)S(1)}, bf16[288,512]{1,0:T(8,128)(2,1)S(1)}, u32[]{:S(2)}, u32[]{:S(2)}) collective-permute-start(bf16[288,512]{1,0:T(8,128)(2,1)S(1)} %get-tuple-element.44), channel_id=1, source_target_pairs={{0,1},{1,2},{2,3},{3,4},{4,5},{5,6},{6,7},{7,0},{8,9},{9,10},{10,1... | collective-permute-start | bytes 884744 | tf_op jit(solution)/shard_map/ppermute | solution.py:516
  42.9 31.1 %collective-permute-start.7 = (bf16[288,512]{1,0:T(8,128)(2,1)S(1)}, bf16[288,512]{1,0:T(8,128)(2,1)S(1)}, u32[]{:S(2)}, u32[]{:S(2)}) collective-permute-start(bf16[288,512]{1,0:T(8,128)(2,1)S(1)} %get-tuple-element.45), channel_id=1, source_target_pairs={{0,8},{1,9},{2,10},{3,11},{4,12},{5,13},{6,14},{7,15},{8,16},{9,17... | collective-permute-start | bytes 884744 | tf_op jit(solution)/shard_map/ppermute | solution.py:516
  43.0 31.0 %collective-permute-start.8 = (bf16[288,512]{1,0:T(8,128)(2,1)S(1)}, bf16[288,512]{1,0:T(8,128)(2,1)S(1)}, u32[]{:S(2)}, u32[]{:S(2)}) collective-permute-start(bf16[288,512]{1,0:T(8,128)(2,1)S(1)} %get-tuple-element.46), channel_id=1, source_target_pairs={{0,9},{1,10},{2,11},{3,12},{4,13},{5,14},{6,15},{7,8},{8,17},{9,18... | collective-permute-start | bytes 884744 | tf_op jit(solution)/shard_map/ppermute | solution.py:516
  44.2 16.7 %collective-permute-start.9 = (f32[4,512]{1,0:T(4,128)S(1)}, f32[4,512]{1,0:T(4,128)S(1)}, u32[]{:S(2)}, u32[]{:S(2)}) collective-permute-start(f32[4,512]{1,0:T(4,128)S(1)} %get-tuple-element.47), channel_id=1, source_target_pairs={{0,8},{8,0},{16,24},{24,16},{1,9},{9,1},{17,25},{25,17},{2,10},{10... | collective-permute-start | bytes 24584 | tf_op jit(solution)/shard_map/ppermute | solution.py:496
  60.9 3.7 %collective-permute-start.10 = (f32[4,512]{1,0:T(4,128)S(1)}, f32[4,512]{1,0:T(4,128)S(1)}, u32[]{:S(2)}, u32[]{:S(2)}) collective-permute-start(f32[4,512]{1,0:T(4,128)S(1)} %add.12), channel_id=1, source_target_pairs={{0,2},{1,3},{2,0},{3,1},{4,6},{5,7},{6,4},{7,5},{8,10},{9,11},{10,... | collective-permute-start | bytes 24584 | tf_op jit(solution)/shard_map/ppermute | solution.py:496
  64.6 3.7 %collective-permute-start.11 = (f32[4,512]{1,0:T(4,128)S(1)}, f32[4,512]{1,0:T(4,128)S(1)}, u32[]{:S(2)}, u32[]{:S(2)}) collective-permute-start(f32[4,512]{1,0:T(4,128)S(1)} %add.13), channel_id=1, source_target_pairs={{0,4},{1,5},{2,6},{3,7},{4,0},{5,1},{6,2},{7,3},{8,12},{9,13},{10,... | collective-permute-start | bytes 24584 | tf_op jit(solution)/shard_map/ppermute | solution.py:496
  68.2 1.2 %collective-permute-start.12 = (f32[4,512]{1,0:T(4,128)S(1)}, f32[4,512]{1,0:T(4,128)S(1)}, u32[]{:S(2)}, u32[]{:S(2)}) collective-permute-start(f32[4,512]{1,0:T(4,128)S(1)} %add.14), channel_id=1, source_target_pairs={{0,1},{1,0},{2,3},{3,2},{4,5},{5,4},{6,7},{7,6},{8,9},{9,8},{10,11... | collective-permute-start | bytes 24584 | tf_op jit(solution)/shard_map/ppermute | solution.py:496
  69.4 4.5 %collective-permute-start.13 = (f32[4,512]{1,0:T(4,128)S(1)}, f32[4,512]{1,0:T(4,128)S(1)}, u32[]{:S(2)}, u32[]{:S(2)}) collective-permute-start(f32[4,512]{1,0:T(4,128)S(1)} %add.15.sums_ref), channel_id=1, source_target_pairs={{0,16},{8,24},{16,0},{24,8},{1,17},{9,25},{17,1},{25,9},{2,18},{10... | collective-permute-start | bytes 24584 | tf_op jit(solution)/shard_map/ppermute | solution.py:496

commit v3 on v2

--- a/solution.py
+++ b/solution.py
@@ -232,27 +232,35 @@
 def fine_first_kernel(
     plan, edge_ref, x_ref, gain_ref, w_ref, wo_ref, y_ref, *more
 ):
-    rest_refs, (slat_ref, slon_ref, sdiag_ref, bias, qkv, att) = more[:-6], more[-6:]
+    rest_refs, (slat_ref, slon_ref, sdiag_ref, bias, qkv, att, tokens_ref) = more[:-7], more[-7:]
     channels = x_ref.shape[1]
     levels, height, width = plan.levels, plan.height, plan.width
     fl, fc = HALF_LAT, HALF_LON
-    turn = WIN_LEV // 2
-    x = x_ref[...]
     count = plan.window
     area = WIN_LAT * WIN_LON
-    block = y_ref.shape[0]
-
-    def window_box(w, base):
-        wr, wc = plan.windows[w]
-        r0, c0 = fl + wr * WIN_LAT, fc + wc * WIN_LON
-        return (r0, min(r0 + WIN_LAT, height), c0, min(c0 + WIN_LON, width), base, area, WIN_LON)
-
-    tokens = moved_rows(box_hot(levels, height, width, [window_box(0, 0)], block, turn), x)
+
+    def level_hot(rows):
+        boxes = [
+            (0, rows, fc, fc + WIN_LON, 0, 0, WIN_LON),
+            (0, rows, fc + WIN_LON, width, area, 0, WIN_LON),
+        ]
+        return box_hot(1, rows, width, boxes, 2 * area)
+
+    split_row = fl + WIN_LAT
+    top_hot, bottom_hot = level_hot(WIN_LAT), level_hot(height - split_row)
+    right_ref, below_ref, last_ref = rest_refs
+    for i, lv in enumerate(plan.order):
+        start = lv * height * width
+        rows = slice(i * area, (i + 1) * area)
+        top = moved_rows(top_hot, x_ref[start + fl * width : start + split_row * width, :])
+        tokens_ref[rows, :] = top[:area]
+        right_ref[rows, :] = top[area:].astype(jnp.bfloat16)
+        bottom = moved_rows(bottom_hot, x_ref[start + split_row * width : start + height * width, :])
+        below_ref[rows, :] = bottom[:area].astype(jnp.bfloat16)
+        last_ref[rows, :] = bottom[area:].astype(jnp.bfloat16)
+    tokens = tokens_ref[...]
     normed = normed_rows(tokens, gain_ref[...])
     qkv[...] = jnp.dot(normed, w_ref[...], preferred_element_type=jnp.float32).astype(jnp.bfloat16)
-    for w in range(1, len(plan.windows)):
-        hot = box_hot(levels, height, width, [window_box(w, 0)], block, turn)
-        rest_refs[w - 1][...] = moved_rows(hot, x).astype(jnp.bfloat16)
     for g in range(plan.groups):
         bias[2 * g] = score_bias(count, plan.group_split[g], 0)
         bias[2 * g + 1] = score_bias(count, plan.group_split[g], edge_ref[0])
@@ -263,14 +271,21 @@
     update = jnp.dot(att[...], wo_ref[...], preferred_element_type=jnp.float32)
     y = (tokens + update).astype(jnp.bfloat16)
     y_ref[...] = y
-    split_rows((slat_ref, slon_ref, sdiag_ref), moved_rows(sent_hot(plan, 0, sum(sent_sizes(plan))), y))
+    hot = sent_hot(plan, 0)
+    for i in range(levels):
+        moved = moved_rows(hot, y_ref[i * area : (i + 1) * area, :]).astype(jnp.bfloat16)
+        start = 0
+        for out in (slat_ref, slon_ref, sdiag_ref):
+            size = out.shape[0] // levels
+            out[i * size : (i + 1) * size, :] = moved[start : start + size]
+            start += size
 
 
 def sent_sizes(plan):
     return [plan.levels * len(cells) for cells in plan.results.values()]
 
 
-def sent_hot(plan, w, out_rows, only=None):
+def sent_hot(plan, w, only=None):
     boxes, start = [], 0
     shifts = {"res_lat": (plan.height, 0), "res_lon": (0, plan.width), "res_diag": (plan.height, plan.width)}
     for name, cells in plan.results.items():
@@ -285,10 +300,9 @@
             base = start + (top - r0) * row_step + (left - c0)
             boxes.append((top - w0, bottom - w0, left - v0, right - v0, base, len(cells), row_step))
         if only is None:
-            start += plan.levels * len(cells)
-    if not boxes:
-        return None
-    return box_hot(plan.levels, WIN_LAT, WIN_LON, boxes, out_rows)
+            start += len(cells)
+    out_rows = start if only is None else len(plan.results[only])
+    return box_hot(1, WIN_LAT, WIN_LON, boxes, out_rows)
 
 
 def raw_hot(plan, name, w, out_rows):
@@ -345,9 +359,13 @@
 def fine_edge_kernel(plan, w, name, raw_names, bias, sent_ref, rest_ref, *more):
     raw = dict(zip(raw_names, more))
     gain_ref, w_ref, wo_ref, y_ref, out_ref, tokens, qkv, att = more[len(raw_names) :]
-    y = fine_windows(plan, [w], bias, rest_ref, raw, gain_ref, w_ref, wo_ref, y_ref, tokens, qkv, att)
-    moved = moved_rows(sent_hot(plan, w, out_ref.shape[0], name), y)
-    out_ref[...] = (sent_ref[...].astype(jnp.float32) + moved).astype(jnp.bfloat16)
+    fine_windows(plan, [w], bias, rest_ref, raw, gain_ref, w_ref, wo_ref, y_ref, tokens, qkv, att)
+    hot = sent_hot(plan, w, name)
+    area, size = WIN_LAT * WIN_LON, out_ref.shape[0] // plan.levels
+    for i in range(plan.levels):
+        rows = slice(i * size, (i + 1) * size)
+        moved = moved_rows(hot, y_ref[i * area : (i + 1) * area, :])
+        out_ref[rows, :] = (sent_ref[rows, :].astype(jnp.float32) + moved).astype(jnp.bfloat16)
 
 
 def coarse_own_kernel(
@@ -587,7 +605,11 @@
         rows_of(n_block, *[n_block] * (len(plan.windows) - 1), *n_sent)
         + [((2 * plan.groups, count, count), jnp.float32)],
         (edge, x, gain1, triple_first, output_first),
-        [pltpu.VMEM((n_block, 3 * channels), bf16), pltpu.VMEM((n_block, channels), bf16)],
+        [
+            pltpu.VMEM((n_block, 3 * channels), bf16),
+            pltpu.VMEM((n_block, channels), bf16),
+            pltpu.VMEM((n_block, channels), jnp.float32),
+        ],
         flops=4 * 10**9, limit=LIMITS["first"],
     )
     fine_scratch = [

time: 75.9 us -> 75.6 us (level)
  waiting for transfers between devices: 27.2 us -> 29.9 us
  Pallas kernels: 28.2 us -> 26.4 us
  starting transfers between devices: 19.4 us -> 18.2 us
    ppermute x9, waiting for transfers between devices: 3.41 us -> 6.35 us  [moved(): return lax.ppermute(value, ('lat', 'lon'), pairs)]
    pallas_call x8, Pallas kernels: 28.2 us -> 26.4 us  [call(): pl.pallas_call(body, out_shape=[jax.ShapeDtypeStruct(s, d) for s, d in ou...]
    ppermute x9, starting transfers between devices: 13.4 us -> 12.1 us  [moved(): return lax.ppermute(value, ('lat', 'lon'), pairs)]
  transfers between devices with their start and end apart: 14 -> 14, of which waited for: 7 -> 7; matrix products, arithmetic and copies ran while one was open for 0% -> 0% of each run, Pallas kernels for 19% -> 16%
where the time goes in v3:
time: 75.6 us; the launch traced here: 75.5 us
  waiting for transfers between devices  29.9 us (40%)
  Pallas kernels  26.4 us (35%)
  starting transfers between devices  18.2 us (24%)
  between operations  0.88 us (1%)
    pallas_call x8, Pallas kernels, call(): pl.pallas_call(body, out_shape=[jax.ShapeDtypeStruct(s, d) for s, d in ou...  26.4 us
    ppermute x5, waiting for transfers between devices, all_but_summed(): lax.ppermute(value, axis, [(i, i ^ step) for i in range(lax.axis_size(axi...  23.5 us
    ppermute x9, starting transfers between devices, moved(): return lax.ppermute(value, ('lat', 'lon'), pairs)  12.1 us
    ppermute x9, waiting for transfers between devices, moved(): return lax.ppermute(value, ('lat', 'lon'), pairs)  6.35 us
    ppermute x5, starting transfers between devices, all_but_summed(): lax.ppermute(value, axis, [(i, i ^ step) for i in range(lax.axis_size(axi...  6.18 us
  transfers between devices with their start and end apart: 14, of which 7 were waited for; matrix products, arithmetic and copies ran while one was open for 0% of the time, Pallas kernels for 16%

profile of v3, /device:TPU:0, one launch (start us, length us, event | category | flops | bytes accessed | tf_op | source)
XLA Modules:
  0.0 75.5 jit_solution(12970835598089407717)
XLA Ops:
  0.7 2.4 %shard_map.132 = (bf16[216,512]{1,0:T(8,128)(2,1)}, bf16[72,512]{1,0:T(8,128)(2,1)}, bf16[216,512]{1,0:T(8,128)(2,1)}) custom-call(bf16[4,12,24,512]{3,2,1,0:T(8,128)(2,1)} %x_hbm.1), custom_call_target="tpu_custom_call" | custom-call | flops 1000000000 | bytes 1179648 | tf_op jit(solution)/shard_map/pallas_call | solution.py:565
  3.1 6.5 %collective-permute-start.2 = (bf16[72,512]{1,0:T(8,128)(2,1)}, bf16[72,512]{1,0:T(8,128)(2,1)}, u32[]{:S(2)}, u32[]{:S(2)}) collective-permute-start(bf16[72,512]{1,0:T(8,128)(2,1)} %get-tuple-element.37), channel_id=1, source_target_pairs={{0,31},{1,24},{2,25},{3,26},{4,27},{5,28},{6,29},{7,30},{8,7},{9,0... | collective-permute-start | bytes 221192 | tf_op jit(solution)/shard_map/ppermute | solution.py:534
  9.5 0.9 %collective-permute-start = (bf16[216,512]{1,0:T(8,128)(2,1)}, bf16[216,512]{1,0:T(8,128)(2,1)S(1)}, u32[]{:S(2)}, u32[]{:S(2)}) collective-permute-start(bf16[216,512]{1,0:T(8,128)(2,1)} %get-tuple-element.30), channel_id=1, source_target_pairs={{0,7},{1,0},{2,1},{3,2},{4,3},{5,4},{6,5},{7,6},{8,15},{9,8},{10,9... | collective-permute-start | bytes 663560 | tf_op jit(solution)/shard_map/ppermute | solution.py:534
  10.4 0.4 collective-permute-start.1
  10.8 2.5 %shard_map.131 = (bf16[288,512]{1,0:T(8,128)(2,1)S(1)}, bf16[288,512]{1,0:T(8,128)(2,1)S(1)}, bf16[288,512]{1,0:T(8,128)(2,1)S(1)}, bf16[288,512]{1,0:T(8,128)(2...) custom-call(s32[1]{0:T(128)} %bitcast.edge_ref, ...), custom_call_target="tpu_custom_call" | custom-call | flops 4000000000 | bytes 3278852 | tf_op jit(solution)/shard_map/pallas_call | solution.py:565
  13.4 0.1 collective-permute-start.5
  13.5 5.3 %collective-permute-done.1.more_0_.lat_ref = bf16[216,512]{1,0:T(8,128)(2,1)} collective-permute-done((bf16[216,512]{1,0:T(8,128)(2,1)}, bf16[216,512]{1,0:T(8,128)(2,1)}, u32[]{:S(2)}, u32[]{:S(2)}) %collective-permute-start.1) | collective-permute-done | bytes 221216 | tf_op jit(solution)/shard_map/ppermute | solution.py:534
  18.7 3.3 %shard_map.134 = (bf16[288,512]{1,0:T(8,128)(2,1)S(1)}, bf16[224,512]{1,0:T(8,128)(2,1)S(1)}) custom-call(f32[4,144,144]{2,1,0:T(8,128)S(1)} %get-tuple-element.26.bias, bf16[224,512]{1,0:T(8,128)(2,1)S(1)} %get-tuple-element.32.sent_ref, bf16[288,512]{1,0:T(8,128)(2,1)S(1)} %get-tuple-element.33.rest_ref, ...), custom_call_target="tpu_custom_call" | custom-call | flops 2000000000 | bytes 3176448 | tf_op jit(solution)/shard_map/pallas_call | solution.py:565
  22.0 0.1 collective-permute-start.4
  22.1 0.0 copy-start.9
  22.1 0.0 slice-start
  22.1 2.3 %shard_map.133 = (bf16[288,512]{1,0:T(8,128)(2,1)S(1)}, bf16[224,512]{1,0:T(8,128)(2,1)S(1)}) custom-call(f32[4,144,144]{2,1,0:T(8,128)S(1)} %get-tuple-element.26.bias, bf16[224,512]{1,0:T(8,128)(2,1)S(1)} %get-tuple-element.28.sent_ref, bf16[288,512]{1,0:T(8,128)(2,1)S(1)} %get-tuple-element.29.rest_ref, ...), custom_call_target="tpu_custom_call" | custom-call | flops 2000000000 | bytes 3176448 | tf_op jit(solution)/shard_map/pallas_call | solution.py:565
  24.4 3.2 %collective-permute-start.3 = (bf16[224,512]{1,0:T(8,128)(2,1)S(1)}, bf16[224,512]{1,0:T(8,128)(2,1)S(1)}, u32[]{:S(2)}, u32[]{:S(2)}) collective-permute-start(bf16[224,512]{1,0:T(8,128)(2,1)S(1)} %get-tuple-element.38), channel_id=1, source_target_pairs={{0,24},{1,25},{2,26},{3,27},{4,28},{5,29},{6,30},{7,31},{8,0},{9,1... | collective-permute-start | bytes 688136 | tf_op jit(solution)/shard_map/ppermute | solution.py:534
  27.6 0.0 copy-start.1
  27.6 0.0 copy-start.10
  27.7 4.1 %shard_map.135.part_ref = bf16[1152,512]{1,0:T(8,128)(2,1)S(1)} custom-call(s32[8,384]{1,0:T(8,128)S(1)} %copy-done.9, f32[4,144,144]{2,1,0:T(8,128)S(1)} %get-tuple-element.26.bias, bf16[288,512]{1,0:T(8,128)(2,1)S(1)} %get-tuple-element.27.first_ref, bf16[288,512]{1,0:T(8,128)(2,1)S(1)} %get-tuple-element.31.right_ref, ...), custom_call_target="tpu_custom_call" | custom-call | flops 4000000000 | bytes 4139008 | tf_op jit(solution)/shard_map/pallas_call | solution.py:565
  31.8 1.1 %collective-permute-done.3.lat_ref = bf16[224,512]{1,0:T(8,128)(2,1)S(1)} collective-permute-done((bf16[224,512]{1,0:T(8,128)(2,1)S(1)}, bf16[224,512]{1,0:T(8,128)(2,1)S(1)}, u32[]{:S(2)}, u32[]{:S(2)}) %collective-permute-start.3) | collective-permute-done | bytes 229408 | tf_op jit(solution)/shard_map/ppermute | solution.py:534
  32.9 7.8 %shard_map.136 = (bf16[1152,512]{1,0:T(8,128)(2,1)S(1)}, bf16[288,1024]{1,0:T(8,128)(2,1)S(1)}, f32[4,512]{1,0:T(4,128)S(1)}) custom-call(s32[8,384]{1,0:T(8,128)S(1)} %copy-done.9, f32[4,144,144]{2,1,0:T(8,128)S(1)} %get-tuple-element.26.bias, bf16[1152,512]{1,0:T(8,128)(2,1)S(1)} %shard_map.135.part_ref, ...), custom_call_target="tpu_custom_call" | custom-call | flops 8000000000 | bytes 18879492 | tf_op jit(solution)/shard_map/pallas_call | solution.py:565
  40.8 2.1 %shard_map.137 = (bf16[288,512]{1,0:T(8,128)(2,1)S(1)}, bf16[288,512]{1,0:T(8,128)(2,1)S(1)}, bf16[288,512]{1,0:T(8,128)(2,1)S(1)}, bf16[288,512]{1,0:T(8,128)(2,1)S(1)}) custom-call(s32[8,384]{1,0:T(8,128)S(1)} %copy-done.9, bf16[1152,512]{1,0:T(8,128)(2,1)S(1)} %get-tuple-element.41.fine_ref, bf16[288,1024]{1,0:T(8,128)(2,1)S(1)} %get-tuple-element.42.upper_ref, ...), custom_call_target="tpu_custom_call" | custom-call | flops 2000000000 | bytes 5976064 | tf_op jit(solution)/shard_map/pallas_call | solution.py:565
  42.9 0.1 collective-permute-start.6
  43.0 0.1 collective-permute-start.7
  43.0 0.9 %collective-permute-start.8 = (bf16[288,512]{1,0:T(8,128)(2,1)S(1)}, bf16[288,512]{1,0:T(8,128)(2,1)S(1)}, u32[]{:S(2)}, u32[]{:S(2)}) collective-permute-start(bf16[288,512]{1,0:T(8,128)(2,1)S(1)} %get-tuple-element.46), channel_id=1, source_target_pairs={{0,9},{1,10},{2,11},{3,12},{4,13},{5,14},{6,15},{7,8},{8,17},{9,18... | collective-permute-start | bytes 884744 | tf_op jit(solution)/shard_map/ppermute | solution.py:534
  43.9 3.5 %collective-permute-start.9 = (f32[4,512]{1,0:T(4,128)S(1)}, f32[4,512]{1,0:T(4,128)S(1)}, u32[]{:S(2)}, u32[]{:S(2)}) collective-permute-start(f32[4,512]{1,0:T(4,128)S(1)} %get-tuple-element.47), channel_id=1, source_target_pairs={{0,8},{8,0},{16,24},{24,16},{1,9},{9,1},{17,25},{25,17},{2,10},{10... | collective-permute-start | bytes 24584 | tf_op jit(solution)/shard_map/ppermute | solution.py:514
  47.4 13.2 %collective-permute-done.9 = f32[4,512]{1,0:T(4,128)S(1)} collective-permute-done((f32[4,512]{1,0:T(4,128)S(1)}, f32[4,512]{1,0:T(4,128)S(1)}, u32[]{:S(2)}, u32[]{:S(2)}) %collective-permute-start.9) | collective-permute-done | bytes 8224 | tf_op jit(solution)/shard_map/ppermute | solution.py:514
  60.6 0.6 collective-permute-start.10
  61.2 3.0 %collective-permute-done.10 = f32[4,512]{1,0:T(4,128)S(1)} collective-permute-done((f32[4,512]{1,0:T(4,128)S(1)}, f32[4,512]{1,0:T(4,128)S(1)}, u32[]{:S(2)}, u32[]{:S(2)}) %collective-permute-start.10) | collective-permute-done | bytes 8224 | tf_op jit(solution)/shard_map/ppermute | solution.py:514
  64.3 1.5 %collective-permute-start.11 = (f32[4,512]{1,0:T(4,128)S(1)}, f32[4,512]{1,0:T(4,128)S(1)}, u32[]{:S(2)}, u32[]{:S(2)}) collective-permute-start(f32[4,512]{1,0:T(4,128)S(1)} %add.13), channel_id=1, source_target_pairs={{0,4},{1,5},{2,6},{3,7},{4,0},{5,1},{6,2},{7,3},{8,12},{9,13},{10,... | collective-permute-start | bytes 24584 | tf_op jit(solution)/shard_map/ppermute | solution.py:514
  65.8 2.1 %collective-permute-done.11 = f32[4,512]{1,0:T(4,128)S(1)} collective-permute-done((f32[4,512]{1,0:T(4,128)S(1)}, f32[4,512]{1,0:T(4,128)S(1)}, u32[]{:S(2)}, u32[]{:S(2)}) %collective-permute-start.11) | collective-permute-done | bytes 8224 | tf_op jit(solution)/shard_map/ppermute | solution.py:514
  67.9 1.2 %collective-permute-done.12 = f32[4,512]{1,0:T(4,128)S(1)} collective-permute-done((f32[4,512]{1,0:T(4,128)S(1)}, f32[4,512]{1,0:T(4,128)S(1)}, u32[]{:S(2)}, u32[]{:S(2)}) %collective-permute-start.12) | collective-permute-done | bytes 8224 | tf_op jit(solution)/shard_map/ppermute | solution.py:514
  69.1 0.6 collective-permute-start.13
  69.7 4.0 %collective-permute-done.13.other_ref = f32[4,512]{1,0:T(4,128)S(1)} collective-permute-done((f32[4,512]{1,0:T(4,128)S(1)}, f32[4,512]{1,0:T(4,128)S(1)}, u32[]{:S(2)}, u32[]{:S(2)}) %collective-permute-start.13) | collective-permute-done | bytes 8224 | tf_op jit(solution)/shard_map/ppermute | solution.py:514
  73.7 1.8 %shard_map.138 = (bf16[1152,512]{1,0:T(8,128)(2,1)}, f32[4,512]{1,0:T(4,128)}) custom-call(s32[8,384]{1,0:T(8,128)S(1)} %copy-done.9, bf16[288,512]{1,0:T(8,128)(2,1)S(1)} %get-tuple-element.43.own_ref, bf16[288,512]{1,0:T(8,128)(2,1)S(1)} %collective-permute-done.6.lon_ref, bf16[288,512]{1,0:T(8,128)(2,1)S(1)} %collective-permute-done.7.lat_ref, ...), custom_call_target="tpu_custom_call" | custom-call | flops 1000000000 | bytes 1208320 | tf_op jit(solution)/shard_map/pallas_call | solution.py:565
  (35 shorter events, 0.1 us)
Async XLA Ops:
  0.6 10.2 %copy-start.4 = (bf16[4,12,24,512]{3,2,1,0:T(8,128)(2,1)S(1)}, bf16[4,12,24,512]{3,2,1,0:T(8,128)(2,1)}, u32[]{:S(2)}) copy-start(bf16[4,12,24,512]{3,2,1,0:T(8,128)(2,1)} %x_hbm.1) | copy-start | bytes 3538948
  0.6 10.2 %copy-start.5 = (bf16[512,512]{1,0:T(8,128)(2,1)S(1)}, bf16[512,512]{1,0:T(8,128)(2,1)}, u32[]{:S(2)}) copy-start(bf16[512,512]{1,0:T(8,128)(2,1)} %wo_ref.4) | copy-start | bytes 1572868
  0.7 10.2 %copy-start.3 = (bf16[512,1536]{1,0:T(8,128)(2,1)S(1)}, bf16[512,1536]{1,0:T(8,128)(2,1)}, u32[]{:S(2)}) copy-start(bf16[512,1536]{1,0:T(8,128)(2,1)} %w_ref.3) | copy-start | bytes 4718596
  0.7 10.2 %copy-start.8 = (f32[512]{0:T(512)S(1)}, f32[512]{0:T(512)}, u32[]{:S(2)}) copy-start(f32[512]{0:T(512)} %param.13) | copy-start | bytes 6148
  3.1 24.5 %collective-permute-start.2 = (bf16[72,512]{1,0:T(8,128)(2,1)}, bf16[72,512]{1,0:T(8,128)(2,1)}, u32[]{:S(2)}, u32[]{:S(2)}) collective-permute-start(bf16[72,512]{1,0:T(8,128)(2,1)} %get-tuple-element.37), channel_id=1, source_target_pairs={{0,31},{1,24},{2,25},{3,26},{4,27},{5,28},{6,29},{7,30},{8,7},{9,0... | collective-permute-start | bytes 221192 | tf_op jit(solution)/shard_map/ppermute | solution.py:534
  9.5 12.5 %collective-permute-start = (bf16[216,512]{1,0:T(8,128)(2,1)}, bf16[216,512]{1,0:T(8,128)(2,1)S(1)}, u32[]{:S(2)}, u32[]{:S(2)}) collective-permute-start(bf16[216,512]{1,0:T(8,128)(2,1)} %get-tuple-element.30), channel_id=1, source_target_pairs={{0,7},{1,0},{2,1},{3,2},{4,3},{5,4},{6,5},{7,6},{8,15},{9,8},{10,9... | collective-permute-start | bytes 663560 | tf_op jit(solution)/shard_map/ppermute | solution.py:534
  10.4 8.4 %collective-permute-start.1 = (bf16[216,512]{1,0:T(8,128)(2,1)}, bf16[216,512]{1,0:T(8,128)(2,1)}, u32[]{:S(2)}, u32[]{:S(2)}) collective-permute-start(bf16[216,512]{1,0:T(8,128)(2,1)} %get-tuple-element.34), channel_id=1, source_target_pairs={{0,24},{1,25},{2,26},{3,27},{4,28},{5,29},{6,30},{7,31},{8,0},{9,1... | collective-permute-start | bytes 663560 | tf_op jit(solution)/shard_map/ppermute | solution.py:534
  13.4 18.4 %collective-permute-start.5 = (bf16[96,512]{1,0:T(8,128)(2,1)S(1)}, bf16[96,512]{1,0:T(8,128)(2,1)S(1)}, u32[]{:S(2)}, u32[]{:S(2)}) collective-permute-start(bf16[96,512]{1,0:T(8,128)(2,1)S(1)} %get-tuple-element.40), channel_id=1, source_target_pairs={{0,31},{1,24},{2,25},{3,26},{4,27},{5,28},{6,29},{7,30},{8,7},{9,0... | collective-permute-start | bytes 294920 | tf_op jit(solution)/shard_map/ppermute | solution.py:534
  22.0 9.8 %collective-permute-start.4 = (bf16[224,512]{1,0:T(8,128)(2,1)S(1)}, bf16[224,512]{1,0:T(8,128)(2,1)S(1)}, u32[]{:S(2)}, u32[]{:S(2)}) collective-permute-start(bf16[224,512]{1,0:T(8,128)(2,1)S(1)} %get-tuple-element.39), channel_id=1, source_target_pairs={{0,7},{1,0},{2,1},{3,2},{4,3},{5,4},{6,5},{7,6},{8,15},{9,8},{10,9... | collective-permute-start | bytes 688136 | tf_op jit(solution)/shard_map/ppermute | solution.py:534
  22.1 5.5 %copy-start.9 = (s32[8,384]{1,0:T(8,128)S(1)}, s32[8,384]{1,0:T(8,128)}, u32[]{:S(2)}) copy-start(s32[8,384]{1,0:T(8,128)} %constant.11.clone.maps_ref) | copy-start | bytes 36868
  22.1 10.8 %slice-start = ((s8[6291456]{0:T(1024)(128)(4,1)}), s8[4194304]{0:T(1024)(128)(4,1)S(1)}, s32[]{:S(2)}) async-start(s8[6291456]{0:T(1024)(128)(4,1)} %bitcast.7), calls=%async_computation | async-start | bytes 8388608
  24.4 8.5 %collective-permute-start.3 = (bf16[224,512]{1,0:T(8,128)(2,1)S(1)}, bf16[224,512]{1,0:T(8,128)(2,1)S(1)}, u32[]{:S(2)}, u32[]{:S(2)}) collective-permute-start(bf16[224,512]{1,0:T(8,128)(2,1)S(1)} %get-tuple-element.38), channel_id=1, source_target_pairs={{0,24},{1,25},{2,26},{3,27},{4,28},{5,29},{6,30},{7,31},{8,0},{9,1... | collective-permute-start | bytes 688136 | tf_op jit(solution)/shard_map/ppermute | solution.py:534
  27.6 5.3 %slice-start.1 = ((s8[6291456]{0:T(1024)(128)(4,1)}), s8[2097152]{0:T(1024)(128)(4,1)S(1)}, s32[]{:S(2)}) async-start(s8[6291456]{0:T(1024)(128)(4,1)} %bitcast.7), calls=%async_computation.1 | async-start | bytes 4194304
  27.6 5.3 %copy-start = (bf16[2048,1024]{1,0:T(8,128)(2,1)S(1)}, bf16[2048,1024]{1,0:T(8,128)(2,1)}, u32[]{:S(2)}) copy-start(bf16[2048,1024]{1,0:T(8,128)(2,1)} %wm_ref.1) | copy-start | bytes 12582916
  27.6 5.3 %copy-start.1 = (bf16[1024,2048]{1,0:T(8,128)(2,1)S(1)}, bf16[1024,2048]{1,0:T(8,128)(2,1)}, u32[]{:S(2)}) copy-start(bf16[1024,2048]{1,0:T(8,128)(2,1)} %wsp_ref.3) | copy-start | bytes 12582916
  27.6 5.3 %copy-start.2 = (bf16[1024,1024]{1,0:T(8,128)(2,1)S(1)}, bf16[1024,1024]{1,0:T(8,128)(2,1)}, u32[]{:S(2)}) copy-start(bf16[1024,1024]{1,0:T(8,128)(2,1)} %wo_ref.5) | copy-start | bytes 6291460
  27.6 5.3 %copy-start.6 = (f32[2048]{0:T(1024)S(1)}, f32[2048]{0:T(1024)}, u32[]{:S(2)}) copy-start(f32[2048]{0:T(1024)} %param.16) | copy-start | bytes 24580
  27.6 5.3 %copy-start.7 = (f32[1024]{0:T(1024)S(1)}, f32[1024]{0:T(1024)}, u32[]{:S(2)}) copy-start(f32[1024]{0:T(1024)} %param.18) | copy-start | bytes 12292
  27.6 5.3 %copy-start.10 = (f32[4,2,288]{2,1,0:T(2,128)S(1)}, f32[4,2,288]{2,1,0:T(2,128)}, u32[]{:S(2)}) copy-start(f32[4,2,288]{2,1,0:T(2,128)} %constant.12.clone.weight_ref) | copy-start | bytes 27652
  42.9 30.7 %collective-permute-start.6 = (bf16[288,512]{1,0:T(8,128)(2,1)S(1)}, bf16[288,512]{1,0:T(8,128)(2,1)S(1)}, u32[]{:S(2)}, u32[]{:S(2)}) collective-permute-start(bf16[288,512]{1,0:T(8,128)(2,1)S(1)} %get-tuple-element.44), channel_id=1, source_target_pairs={{0,1},{1,2},{2,3},{3,4},{4,5},{5,6},{6,7},{7,0},{8,9},{9,10},{10,1... | collective-permute-start | bytes 884744 | tf_op jit(solution)/shard_map/ppermute | solution.py:534
  43.0 30.7 %collective-permute-start.7 = (bf16[288,512]{1,0:T(8,128)(2,1)S(1)}, bf16[288,512]{1,0:T(8,128)(2,1)S(1)}, u32[]{:S(2)}, u32[]{:S(2)}) collective-permute-start(bf16[288,512]{1,0:T(8,128)(2,1)S(1)} %get-tuple-element.45), channel_id=1, source_target_pairs={{0,8},{1,9},{2,10},{3,11},{4,12},{5,13},{6,14},{7,15},{8,16},{9,17... | collective-permute-start | bytes 884744 | tf_op jit(solution)/shard_map/ppermute | solution.py:534
  43.0 30.6 %collective-permute-start.8 = (bf16[288,512]{1,0:T(8,128)(2,1)S(1)}, bf16[288,512]{1,0:T(8,128)(2,1)S(1)}, u32[]{:S(2)}, u32[]{:S(2)}) collective-permute-start(bf16[288,512]{1,0:T(8,128)(2,1)S(1)} %get-tuple-element.46), channel_id=1, source_target_pairs={{0,9},{1,10},{2,11},{3,12},{4,13},{5,14},{6,15},{7,8},{8,17},{9,18... | collective-permute-start | bytes 884744 | tf_op jit(solution)/shard_map/ppermute | solution.py:534
  43.9 16.7 %collective-permute-start.9 = (f32[4,512]{1,0:T(4,128)S(1)}, f32[4,512]{1,0:T(4,128)S(1)}, u32[]{:S(2)}, u32[]{:S(2)}) collective-permute-start(f32[4,512]{1,0:T(4,128)S(1)} %get-tuple-element.47), channel_id=1, source_target_pairs={{0,8},{8,0},{16,24},{24,16},{1,9},{9,1},{17,25},{25,17},{2,10},{10... | collective-permute-start | bytes 24584 | tf_op jit(solution)/shard_map/ppermute | solution.py:514
  60.6 3.7 %collective-permute-start.10 = (f32[4,512]{1,0:T(4,128)S(1)}, f32[4,512]{1,0:T(4,128)S(1)}, u32[]{:S(2)}, u32[]{:S(2)}) collective-permute-start(f32[4,512]{1,0:T(4,128)S(1)} %add.12), channel_id=1, source_target_pairs={{0,2},{1,3},{2,0},{3,1},{4,6},{5,7},{6,4},{7,5},{8,10},{9,11},{10,... | collective-permute-start | bytes 24584 | tf_op jit(solution)/shard_map/ppermute | solution.py:514
  64.3 3.7 %collective-permute-start.11 = (f32[4,512]{1,0:T(4,128)S(1)}, f32[4,512]{1,0:T(4,128)S(1)}, u32[]{:S(2)}, u32[]{:S(2)}) collective-permute-start(f32[4,512]{1,0:T(4,128)S(1)} %add.13), channel_id=1, source_target_pairs={{0,4},{1,5},{2,6},{3,7},{4,0},{5,1},{6,2},{7,3},{8,12},{9,13},{10,... | collective-permute-start | bytes 24584 | tf_op jit(solution)/shard_map/ppermute | solution.py:514
  67.9 1.2 %collective-permute-start.12 = (f32[4,512]{1,0:T(4,128)S(1)}, f32[4,512]{1,0:T(4,128)S(1)}, u32[]{:S(2)}, u32[]{:S(2)}) collective-permute-start(f32[4,512]{1,0:T(4,128)S(1)} %add.14), channel_id=1, source_target_pairs={{0,1},{1,0},{2,3},{3,2},{4,5},{5,4},{6,7},{7,6},{8,9},{9,8},{10,11... | collective-permute-start | bytes 24584 | tf_op jit(solution)/shard_map/ppermute | solution.py:514
  69.1 4.5 %collective-permute-start.13 = (f32[4,512]{1,0:T(4,128)S(1)}, f32[4,512]{1,0:T(4,128)S(1)}, u32[]{:S(2)}, u32[]{:S(2)}) collective-permute-start(f32[4,512]{1,0:T(4,128)S(1)} %add.15.sums_ref), channel_id=1, source_target_pairs={{0,16},{8,24},{16,0},{24,8},{1,17},{9,25},{17,1},{25,9},{2,18},{10... | collective-permute-start | bytes 24584 | tf_op jit(solution)/shard_map/ppermute | solution.py:514

commit v4 on v3

--- a/solution.py
+++ b/solution.py
@@ -356,9 +356,13 @@
     return y
 
 
-def fine_edge_kernel(plan, w, name, raw_names, bias, sent_ref, rest_ref, *more):
+def fine_edge_kernel(plan, w, name, raw_names, bias, sent_ref, rest_ref, last_ref, *more):
     raw = dict(zip(raw_names, more))
-    gain_ref, w_ref, wo_ref, y_ref, out_ref, tokens, qkv, att = more[len(raw_names) :]
+    gain_ref, w_ref, wo_ref, y_ref, out_ref, last_out_ref, tokens, qkv, att = more[len(raw_names) :]
+    last = last_ref[...].astype(jnp.float32)
+    for raw_name, ref in raw.items():
+        last = last + moved_rows(raw_hot(plan, raw_name, len(plan.windows) - 1, last.shape[0]), ref[...])
+    last_out_ref[...] = last.astype(jnp.bfloat16)
     fine_windows(plan, [w], bias, rest_ref, raw, gain_ref, w_ref, wo_ref, y_ref, tokens, qkv, att)
     hot = sent_hot(plan, w, name)
     area, size = WIN_LAT * WIN_LON, out_ref.shape[0] // plan.levels
@@ -369,21 +373,32 @@
 
 
 def coarse_own_kernel(
-    plan, keys, which, maps_ref, bias, first_ref, right_ref, below_ref, rest_ref, lat_ref, diag_ref, lon_ref, gain_ref, w_ref,
-    wo_ref, part_ref, y_ref, tokens, qkv, att,
+    plan, keys, which, maps_ref, bias, first_ref, right_ref, below_ref, rest_ref, diag_hbm, gain_ref, w_ref,
+    wo_ref, part_ref, y_ref, tokens, qkv, att, diag_ref, sem,
 ):
-    raw = {"raw_lat": lat_ref, "raw_diag": diag_ref, "raw_lon": lon_ref}
-    fine_windows(plan, which, bias, rest_ref, raw, gain_ref, w_ref, wo_ref, y_ref, tokens, qkv, att)
+    copy = pltpu.make_async_copy(diag_hbm, diag_ref, sem)
+    copy.start()
     area = WIN_LAT * WIN_LON
+    parts = len(plan.parts)
+    total = part_ref.shape[0] // parts
     hot = table_hot(maps_ref, keys["own"])
-    total = part_ref.shape[0] // len(plan.parts)
     for i in range(plan.levels):
         rows = slice(i * area, (i + 1) * area)
-        stacked = jnp.concatenate([ref[rows, :] for ref in (first_ref, right_ref, below_ref, y_ref)], 0)
+        stacked = jnp.concatenate([ref[rows, :] for ref in (first_ref, right_ref, below_ref)], 0)
         value = moved_rows(hot, stacked).astype(jnp.bfloat16)
-        for k in range(len(plan.parts)):
+        for k in range(parts):
             start = k * total + i * area
             part_ref[start : start + area, :] = value[k * area : (k + 1) * area]
+    copy.wait()
+    raw = {"raw_diag": diag_ref}
+    fine_windows(plan, which, bias, rest_ref, raw, gain_ref, w_ref, wo_ref, y_ref, tokens, qkv, att)
+    hot = table_hot(maps_ref, keys["own_last"])
+    for i in range(plan.levels):
+        value = moved_rows(hot, y_ref[i * area : (i + 1) * area, :])
+        for k in range(parts):
+            rows = slice(k * total + i * area, k * total + (i + 1) * area)
+            early = part_ref[rows, :].astype(jnp.float32)
+            part_ref[rows, :] = (early + value[k * area : (k + 1) * area]).astype(jnp.bfloat16)
 
 
 def thirds(value):
@@ -485,10 +500,7 @@
             out[i * quarter : (i + 1) * quarter, :] = moved[q * quarter : (q + 1) * quarter]
 
 
-def output_kernel(
-    plan, keys, maps_ref, own_ref, lon_ref, lat_ref, diag_ref, sums_ref, other_ref, out_ref, means_ref
-):
-    means_ref[...] = sums_ref[...] + other_ref[...]
+def output_kernel(plan, keys, maps_ref, own_ref, lon_ref, lat_ref, diag_ref, out_ref):
     span = own_ref.shape[0] // plan.levels
     tile = plan.height * plan.width
     hot = table_hot(maps_ref, keys["output"])
@@ -534,7 +546,8 @@
         return lax.ppermute(value, ("lat", "lon"), pairs)
 
     all_parts = sum(plan.parts, [])
-    maps.add("own", sum(plan.blocks, []), all_parts)
+    maps.add("own", sum(plan.blocks[:-1], []), all_parts)
+    maps.add("own_last", plan.blocks[-1], all_parts)
     maps.add("ahead", sum(plan.results.values(), []), all_parts)
     cells = [
         (2 * r + ro, 2 * c + co)
@@ -619,23 +632,24 @@
     ]
     fine_weights = (gain1, triple_first, output_first)
 
-    def fine_edge(w, direction, sent, rest, raws):
+    def fine_edge(w, direction, sent, rest, last, raws):
         return call(
             functools.partial(fine_edge_kernel, plan, w, direction, list(raws)),
-            rows_of(n_block, sent.shape[0]), (bias, sent, rest, *raws.values(), *fine_weights),
+            rows_of(n_block, sent.shape[0], n_block), (bias, sent, rest, last, *raws.values(), *fine_weights),
             fine_scratch, flops=2 * 10**9, limit=LIMITS["edge"],
         )
 
-    y_right, s_lat = fine_edge(1, "res_lat", s_lat, x_right, {"raw_lon": r_lon})
+    y_right, s_lat, x_last = fine_edge(1, "res_lat", s_lat, x_right, x_last, {"raw_lon": r_lon})
     q_lat = moved(s_lat, -1, 0)
     q_diag = moved(s_diag, -1, -1)
-    y_below, s_lon = fine_edge(2, "res_lon", s_lon, x_below, {"raw_lat": r_lat})
+    y_below, s_lon, x_last = fine_edge(2, "res_lon", s_lon, x_below, x_last, {"raw_lat": r_lat})
     q_lon = moved(s_lon, 0, -1)
     (parts,) = call(
         functools.partial(coarse_own_kernel, plan, keys, [len(plan.windows) - 1]),
         rows_of(n_part * n_coarse),
-        (table, bias, y_first, y_right, y_below, x_last, r_lat, r_diag, r_lon, *fine_weights),
-        [pltpu.VMEM((n_block, channels), bf16)] + fine_scratch, flops=4 * 10**9, limit=LIMITS["own"],
+        (table, bias, y_first, y_right, y_below, x_last, r_diag, *fine_weights),
+        [pltpu.VMEM((n_block, channels), bf16), *fine_scratch, pltpu.VMEM(r_diag.shape, bf16), pltpu.SemaphoreType.DMA],
+        flops=4 * 10**9, limit=LIMITS["own"], specs=[vmem] * 6 + [hbm] + [vmem] * len(fine_weights),
     )
     total_rows, total_cols = height * lat_count, width * lon_count
     angle = np.pi * ((np.arange(total_rows) + 0.5) / total_rows - 0.5)
@@ -661,12 +675,11 @@
     )
     d_lat, d_lon, d_diag = (moved(s_lat, 1, 0), moved(s_lon, 0, 1), moved(s_diag, 1, 1))
     sums, other_sums = all_but_summed(sums)
-    decoded, means = call(
-        functools.partial(output_kernel, plan, keys),
-        rows_of(levels * height * width) + [((levels, channels), jnp.float32)],
-        (table, own, d_lon, d_lat, d_diag, sums, other_sums), flops=10**9, limit=LIMITS["output"],
-    )
-    return decoded.reshape(latent.shape), means
+    (decoded,) = call(
+        functools.partial(output_kernel, plan, keys), rows_of(levels * height * width),
+        (table, own, d_lon, d_lat, d_diag), flops=10**9, limit=LIMITS["output"],
+    )
+    return decoded.reshape(latent.shape), sums + other_sums
 
 
 def solution(mesh):

time: 75.6 us -> 72.9 us (0.964)
  waiting for transfers between devices: 29.9 us -> 26.8 us
    ppermute x9, waiting for transfers between devices: 6.35 us -> 3.27 us  [moved(): return lax.ppermute(value, ('lat', 'lon'), pairs)]
  transfers between devices with their start and end apart: 14 -> 14, of which waited for: 7 -> 8; matrix products, arithmetic and copies ran while one was open for 0% -> 1% of each run, Pallas kernels for 16% -> 17%
where the time goes in v4:
time: 72.9 us; the launch traced here: 72.8 us
  waiting for transfers between devices  26.8 us (37%)
  Pallas kernels  26.2 us (36%)
  starting transfers between devices  18.3 us (25%)
  between operations  0.85 us (1%)
    pallas_call x8, Pallas kernels, call(): pl.pallas_call(body, out_shape=[jax.ShapeDtypeStruct(s, d) for s, d in ou...  26.2 us
    ppermute x5, waiting for transfers between devices, all_but_summed(): lax.ppermute(value, axis, [(i, i ^ step) for i in range(lax.axis_size(axi...  23.5 us
    ppermute x9, starting transfers between devices, moved(): return lax.ppermute(value, ('lat', 'lon'), pairs)  12.3 us
    ppermute x5, starting transfers between devices, all_but_summed(): lax.ppermute(value, axis, [(i, i ^ step) for i in range(lax.axis_size(axi...  5.97 us
    ppermute x9, waiting for transfers between devices, moved(): return lax.ppermute(value, ('lat', 'lon'), pairs)  3.27 us
  transfers between devices with their start and end apart: 14, of which 8 were waited for; matrix products, arithmetic and copies ran while one was open for 1% of the time, Pallas kernels for 17%

profile of v4, /device:TPU:0, one launch (start us, length us, event | category | flops | bytes accessed | tf_op | source)
XLA Modules:
  0.0 72.8 jit_solution(15142625976239634613)
XLA Ops:
  0.7 2.4 %shard_map.132 = (bf16[216,512]{1,0:T(8,128)(2,1)}, bf16[72,512]{1,0:T(8,128)(2,1)}, bf16[216,512]{1,0:T(8,128)(2,1)}) custom-call(bf16[4,12,24,512]{3,2,1,0:T(8,128)(2,1)} %x_hbm.1), custom_call_target="tpu_custom_call" | custom-call | flops 1000000000 | bytes 1179648 | tf_op jit(solution)/shard_map/pallas_call | solution.py:578
  3.1 6.5 %collective-permute-start.2 = (bf16[72,512]{1,0:T(8,128)(2,1)}, bf16[72,512]{1,0:T(8,128)(2,1)}, u32[]{:S(2)}, u32[]{:S(2)}) collective-permute-start(bf16[72,512]{1,0:T(8,128)(2,1)} %get-tuple-element.39), channel_id=1, source_target_pairs={{0,31},{1,24},{2,25},{3,26},{4,27},{5,28},{6,29},{7,30},{8,7},{9,0... | collective-permute-start | bytes 221192 | tf_op jit(solution)/shard_map/ppermute | solution.py:546
  9.5 0.9 %collective-permute-start = (bf16[216,512]{1,0:T(8,128)(2,1)}, bf16[216,512]{1,0:T(8,128)(2,1)}, u32[]{:S(2)}, u32[]{:S(2)}) collective-permute-start(bf16[216,512]{1,0:T(8,128)(2,1)} %get-tuple-element.31), channel_id=1, source_target_pairs={{0,7},{1,0},{2,1},{3,2},{4,3},{5,4},{6,5},{7,6},{8,15},{9,8},{10,9... | collective-permute-start | bytes 663560 | tf_op jit(solution)/shard_map/ppermute | solution.py:546
  10.4 0.4 collective-permute-start.1
  10.9 2.5 %shard_map.131 = (bf16[288,512]{1,0:T(8,128)(2,1)S(1)}, bf16[288,512]{1,0:T(8,128)(2,1)S(1)}, bf16[288,512]{1,0:T(8,128)(2,1)S(1)}, bf16[288,512]{1,0:T(8,128)(2...) custom-call(s32[1]{0:T(128)} %bitcast.edge_ref, ...), custom_call_target="tpu_custom_call" | custom-call | flops 4000000000 | bytes 3278852 | tf_op jit(solution)/shard_map/pallas_call | solution.py:578
  13.4 0.1 collective-permute-start.5
  13.5 0.7 collective-permute-done.more_0_
  14.2 3.3 %shard_map.133 = (bf16[288,512]{1,0:T(8,128)(2,1)S(1)}, bf16[224,512]{1,0:T(8,128)(2,1)S(1)}, bf16[288,512]{1,0:T(8,128)(2,1)S(1)}) custom-call(f32[4,144,144]{2,1,0:T(8,128)S(1)} %get-tuple-element.26.bias, bf16[224,512]{1,0:T(8,128)(2,1)S(1)} %get-tuple-element.28.sent_ref, bf16[288,512]{1,0:T(8,128)(2,1)S(1)} %get-tuple-element.29.rest_ref, ...), custom_call_target="tpu_custom_call" | custom-call | flops 2000000000 | bytes 3471360 | tf_op jit(solution)/shard_map/pallas_call | solution.py:578
  17.5 1.2 %collective-permute-done.1.more_0_ = bf16[216,512]{1,0:T(8,128)(2,1)S(1)} collective-permute-done((bf16[216,512]{1,0:T(8,128)(2,1)}, bf16[216,512]{1,0:T(8,128)(2,1)S(1)}, u32[]{:S(2)}, u32[]{:S(2)}) %collective-permute-start.1) | collective-permute-done | bytes 221216 | tf_op jit(solution)/shard_map/ppermute | solution.py:546
  18.6 2.4 %shard_map.134 = (bf16[288,512]{1,0:T(8,128)(2,1)S(1)}, bf16[224,512]{1,0:T(8,128)(2,1)S(1)}, bf16[288,512]{1,0:T(8,128)(2,1)S(1)}) custom-call(f32[4,144,144]{2,1,0:T(8,128)S(1)} %get-tuple-element.26.bias, bf16[224,512]{1,0:T(8,128)(2,1)S(1)} %get-tuple-element.33.sent_ref, bf16[288,512]{1,0:T(8,128)(2,1)S(1)} %get-tuple-element.34.rest_ref, ...), custom_call_target="tpu_custom_call" | custom-call | flops 2000000000 | bytes 3471360 | tf_op jit(solution)/shard_map/pallas_call | solution.py:578
  21.0 1.7 %collective-permute-start.4 = (bf16[224,512]{1,0:T(8,128)(2,1)S(1)}, bf16[224,512]{1,0:T(8,128)(2,1)S(1)}, u32[]{:S(2)}, u32[]{:S(2)}) collective-permute-start(bf16[224,512]{1,0:T(8,128)(2,1)S(1)} %get-tuple-element.41), channel_id=1, source_target_pairs={{0,7},{1,0},{2,1},{3,2},{4,3},{5,4},{6,5},{7,6},{8,15},{9,8},{10,9... | collective-permute-start | bytes 688136 | tf_op jit(solution)/shard_map/ppermute | solution.py:546
  22.7 1.4 %collective-permute-start.3 = (bf16[224,512]{1,0:T(8,128)(2,1)S(1)}, bf16[224,512]{1,0:T(8,128)(2,1)S(1)}, u32[]{:S(2)}, u32[]{:S(2)}) collective-permute-start(bf16[224,512]{1,0:T(8,128)(2,1)S(1)} %get-tuple-element.40), channel_id=1, source_target_pairs={{0,24},{1,25},{2,26},{3,27},{4,28},{5,29},{6,30},{7,31},{8,0},{9,1... | collective-permute-start | bytes 688136 | tf_op jit(solution)/shard_map/ppermute | solution.py:546
  24.1 0.0 copy-start.1
  24.2 0.0 copy-start.10
  24.2 3.8 %shard_map.135.part_ref = bf16[1152,512]{1,0:T(8,128)(2,1)S(1)} custom-call(s32[8,384]{1,0:T(8,128)S(1)} %copy-done.9, f32[4,144,144]{2,1,0:T(8,128)S(1)} %get-tuple-element.26.bias, bf16[288,512]{1,0:T(8,128)(2,1)S(1)} %get-tuple-element.27.first_ref, bf16[288,512]{1,0:T(8,128)(2,1)S(1)} %get-tuple-element.32.right_ref, ...), custom_call_target="tpu_custom_call" | custom-call | flops 4000000000 | bytes 3696640 | tf_op jit(solution)/shard_map/pallas_call | solution.py:578
  28.0 1.4 %collective-permute-done.3.lat_ref = bf16[224,512]{1,0:T(8,128)(2,1)S(1)} collective-permute-done((bf16[224,512]{1,0:T(8,128)(2,1)S(1)}, bf16[224,512]{1,0:T(8,128)(2,1)S(1)}, u32[]{:S(2)}, u32[]{:S(2)}) %collective-permute-start.3) | collective-permute-done | bytes 229408 | tf_op jit(solution)/shard_map/ppermute | solution.py:546
  29.5 7.8 %shard_map.136 = (bf16[1152,512]{1,0:T(8,128)(2,1)S(1)}, bf16[288,1024]{1,0:T(8,128)(2,1)S(1)}, f32[4,512]{1,0:T(4,128)S(1)}) custom-call(s32[8,384]{1,0:T(8,128)S(1)} %copy-done.9, f32[4,144,144]{2,1,0:T(8,128)S(1)} %get-tuple-element.26.bias, bf16[1152,512]{1,0:T(8,128)(2,1)S(1)} %shard_map.135.part_ref, ...), custom_call_target="tpu_custom_call" | custom-call | flops 8000000000 | bytes 18879492 | tf_op jit(solution)/shard_map/pallas_call | solution.py:578
  37.3 2.1 %shard_map.137 = (bf16[288,512]{1,0:T(8,128)(2,1)S(1)}, bf16[288,512]{1,0:T(8,128)(2,1)S(1)}, bf16[288,512]{1,0:T(8,128)(2,1)S(1)}, bf16[288,512]{1,0:T(8,128)(2,1)S(1)}) custom-call(s32[8,384]{1,0:T(8,128)S(1)} %copy-done.9, bf16[1152,512]{1,0:T(8,128)(2,1)S(1)} %get-tuple-element.43.fine_ref, bf16[288,1024]{1,0:T(8,128)(2,1)S(1)} %get-tuple-element.44.upper_ref, ...), custom_call_target="tpu_custom_call" | custom-call | flops 2000000000 | bytes 5976064 | tf_op jit(solution)/shard_map/pallas_call | solution.py:578
  39.4 0.1 collective-permute-start.6
  39.5 0.1 collective-permute-start.7
  39.5 1.3 %collective-permute-start.8 = (bf16[288,512]{1,0:T(8,128)(2,1)S(1)}, bf16[288,512]{1,0:T(8,128)(2,1)S(1)}, u32[]{:S(2)}, u32[]{:S(2)}) collective-permute-start(bf16[288,512]{1,0:T(8,128)(2,1)S(1)} %get-tuple-element.48), channel_id=1, source_target_pairs={{0,9},{1,10},{2,11},{3,12},{4,13},{5,14},{6,15},{7,8},{8,17},{9,18... | collective-permute-start | bytes 884744 | tf_op jit(solution)/shard_map/ppermute | solution.py:546
  40.8 3.1 %collective-permute-start.9 = (f32[4,512]{1,0:T(4,128)S(1)}, f32[4,512]{1,0:T(4,128)S(1)}, u32[]{:S(2)}, u32[]{:S(2)}) collective-permute-start(f32[4,512]{1,0:T(4,128)S(1)} %get-tuple-element.49), channel_id=1, source_target_pairs={{0,8},{8,0},{16,24},{24,16},{1,9},{9,1},{17,25},{25,17},{2,10},{10... | collective-permute-start | bytes 24584 | tf_op jit(solution)/shard_map/ppermute | solution.py:526
  43.9 13.4 %collective-permute-done.9 = f32[4,512]{1,0:T(4,128)S(1)} collective-permute-done((f32[4,512]{1,0:T(4,128)S(1)}, f32[4,512]{1,0:T(4,128)S(1)}, u32[]{:S(2)}, u32[]{:S(2)}) %collective-permute-start.9) | collective-permute-done | bytes 8224 | tf_op jit(solution)/shard_map/ppermute | solution.py:526
  57.3 1.0 %collective-permute-start.10 = (f32[4,512]{1,0:T(4,128)S(1)}, f32[4,512]{1,0:T(4,128)S(1)}, u32[]{:S(2)}, u32[]{:S(2)}) collective-permute-start(f32[4,512]{1,0:T(4,128)S(1)} %add.15), channel_id=1, source_target_pairs={{0,2},{1,3},{2,0},{3,1},{4,6},{5,7},{6,4},{7,5},{8,10},{9,11},{10,... | collective-permute-start | bytes 24584 | tf_op jit(solution)/shard_map/ppermute | solution.py:526
  58.3 2.7 %collective-permute-done.10 = f32[4,512]{1,0:T(4,128)S(1)} collective-permute-done((f32[4,512]{1,0:T(4,128)S(1)}, f32[4,512]{1,0:T(4,128)S(1)}, u32[]{:S(2)}, u32[]{:S(2)}) %collective-permute-start.10) | collective-permute-done | bytes 8224 | tf_op jit(solution)/shard_map/ppermute | solution.py:526
  61.0 1.4 %collective-permute-start.11 = (f32[4,512]{1,0:T(4,128)S(1)}, f32[4,512]{1,0:T(4,128)S(1)}, u32[]{:S(2)}, u32[]{:S(2)}) collective-permute-start(f32[4,512]{1,0:T(4,128)S(1)} %add.16), channel_id=1, source_target_pairs={{0,4},{1,5},{2,6},{3,7},{4,0},{5,1},{6,2},{7,3},{8,12},{9,13},{10,... | collective-permute-start | bytes 24584 | tf_op jit(solution)/shard_map/ppermute | solution.py:526
  62.3 2.3 %collective-permute-done.11 = f32[4,512]{1,0:T(4,128)S(1)} collective-permute-done((f32[4,512]{1,0:T(4,128)S(1)}, f32[4,512]{1,0:T(4,128)S(1)}, u32[]{:S(2)}, u32[]{:S(2)}) %collective-permute-start.11) | collective-permute-done | bytes 8224 | tf_op jit(solution)/shard_map/ppermute | solution.py:526
  64.6 1.2 %collective-permute-done.12 = f32[4,512]{1,0:T(4,128)S(1)} collective-permute-done((f32[4,512]{1,0:T(4,128)S(1)}, f32[4,512]{1,0:T(4,128)S(1)}, u32[]{:S(2)}, u32[]{:S(2)}) %collective-permute-start.12) | collective-permute-done | bytes 8224 | tf_op jit(solution)/shard_map/ppermute | solution.py:526
  65.8 0.6 collective-permute-start.13
  66.4 4.0 %collective-permute-done.13 = f32[4,512]{1,0:T(4,128)S(1)} collective-permute-done((f32[4,512]{1,0:T(4,128)S(1)}, f32[4,512]{1,0:T(4,128)S(1)}, u32[]{:S(2)}, u32[]{:S(2)}) %collective-permute-start.13) | collective-permute-done | bytes 8224 | tf_op jit(solution)/shard_map/ppermute | solution.py:526
  70.3 0.6 add.19
  71.0 1.8 %shard_map.138 = bf16[1152,512]{1,0:T(8,128)(2,1)} custom-call(s32[8,384]{1,0:T(8,128)S(1)} %copy-done.9, bf16[288,512]{1,0:T(8,128)(2,1)S(1)} %get-tuple-element.45.own_ref, bf16[288,512]{1,0:T(8,128)(2,1)S(1)} %collective-permute-done.6.lon_ref, bf16[288,512]{1,0:T(8,128)(2,1)S(1)} %collective-permute-done.7.lat_ref, ...), custom_call_target="tpu_custom_call" | custom-call | flops 1000000000 | bytes 1191936 | tf_op jit(solution)/shard_map/pallas_call | solution.py:578
  (36 shorter events, 0.1 us)
Async XLA Ops:
  0.6 10.2 %copy-start.4 = (bf16[4,12,24,512]{3,2,1,0:T(8,128)(2,1)S(1)}, bf16[4,12,24,512]{3,2,1,0:T(8,128)(2,1)}, u32[]{:S(2)}) copy-start(bf16[4,12,24,512]{3,2,1,0:T(8,128)(2,1)} %x_hbm.1) | copy-start | bytes 3538948
  0.6 10.2 %copy-start.5 = (bf16[512,512]{1,0:T(8,128)(2,1)S(1)}, bf16[512,512]{1,0:T(8,128)(2,1)}, u32[]{:S(2)}) copy-start(bf16[512,512]{1,0:T(8,128)(2,1)} %wo_ref.4) | copy-start | bytes 1572868
  0.7 10.2 %copy-start.3 = (bf16[512,1536]{1,0:T(8,128)(2,1)S(1)}, bf16[512,1536]{1,0:T(8,128)(2,1)}, u32[]{:S(2)}) copy-start(bf16[512,1536]{1,0:T(8,128)(2,1)} %w_ref.3) | copy-start | bytes 4718596
  0.7 10.2 %copy-start.8 = (f32[512]{0:T(512)S(1)}, f32[512]{0:T(512)}, u32[]{:S(2)}) copy-start(f32[512]{0:T(512)} %param.13) | copy-start | bytes 6148
  3.1 21.0 %collective-permute-start.2 = (bf16[72,512]{1,0:T(8,128)(2,1)}, bf16[72,512]{1,0:T(8,128)(2,1)}, u32[]{:S(2)}, u32[]{:S(2)}) collective-permute-start(bf16[72,512]{1,0:T(8,128)(2,1)} %get-tuple-element.39), channel_id=1, source_target_pairs={{0,31},{1,24},{2,25},{3,26},{4,27},{5,28},{6,29},{7,30},{8,7},{9,0... | collective-permute-start | bytes 221192 | tf_op jit(solution)/shard_map/ppermute | solution.py:546
  9.5 4.6 %collective-permute-start = (bf16[216,512]{1,0:T(8,128)(2,1)}, bf16[216,512]{1,0:T(8,128)(2,1)}, u32[]{:S(2)}, u32[]{:S(2)}) collective-permute-start(bf16[216,512]{1,0:T(8,128)(2,1)} %get-tuple-element.31), channel_id=1, source_target_pairs={{0,7},{1,0},{2,1},{3,2},{4,3},{5,4},{6,5},{7,6},{8,15},{9,8},{10,9... | collective-permute-start | bytes 663560 | tf_op jit(solution)/shard_map/ppermute | solution.py:546
  10.4 8.3 %collective-permute-start.1 = (bf16[216,512]{1,0:T(8,128)(2,1)}, bf16[216,512]{1,0:T(8,128)(2,1)S(1)}, u32[]{:S(2)}, u32[]{:S(2)}) collective-permute-start(bf16[216,512]{1,0:T(8,128)(2,1)} %get-tuple-element.36), channel_id=1, source_target_pairs={{0,24},{1,25},{2,26},{3,27},{4,28},{5,29},{6,30},{7,31},{8,0},{9,1... | collective-permute-start | bytes 663560 | tf_op jit(solution)/shard_map/ppermute | solution.py:546
  13.4 14.6 %collective-permute-start.5 = (bf16[96,512]{1,0:T(8,128)(2,1)S(1)}, bf16[96,512]{1,0:T(8,128)(2,1)S(1)}, u32[]{:S(2)}, u32[]{:S(2)}) collective-permute-start(bf16[96,512]{1,0:T(8,128)(2,1)S(1)} %get-tuple-element.42), channel_id=1, source_target_pairs={{0,31},{1,24},{2,25},{3,26},{4,27},{5,28},{6,29},{7,30},{8,7},{9,0... | collective-permute-start | bytes 294920 | tf_op jit(solution)/shard_map/ppermute | solution.py:546
  18.6 5.5 %copy-start.9 = (s32[8,384]{1,0:T(8,128)S(1)}, s32[8,384]{1,0:T(8,128)}, u32[]{:S(2)}) copy-start(s32[8,384]{1,0:T(8,128)} %constant.11.clone.maps_ref) | copy-start | bytes 36868
  18.6 10.8 %slice-start = ((s8[6291456]{0:T(1024)(128)(4,1)}), s8[4194304]{0:T(1024)(128)(4,1)S(1)}, s32[]{:S(2)}) async-start(s8[6291456]{0:T(1024)(128)(4,1)} %bitcast.7), calls=%async_computation | async-start | bytes 8388608
  21.0 6.9 %collective-permute-start.4 = (bf16[224,512]{1,0:T(8,128)(2,1)S(1)}, bf16[224,512]{1,0:T(8,128)(2,1)S(1)}, u32[]{:S(2)}, u32[]{:S(2)}) collective-permute-start(bf16[224,512]{1,0:T(8,128)(2,1)S(1)} %get-tuple-element.41), channel_id=1, source_target_pairs={{0,7},{1,0},{2,1},{3,2},{4,3},{5,4},{6,5},{7,6},{8,15},{9,8},{10,9... | collective-permute-start | bytes 688136 | tf_op jit(solution)/shard_map/ppermute | solution.py:546
  22.7 6.6 %collective-permute-start.3 = (bf16[224,512]{1,0:T(8,128)(2,1)S(1)}, bf16[224,512]{1,0:T(8,128)(2,1)S(1)}, u32[]{:S(2)}, u32[]{:S(2)}) collective-permute-start(bf16[224,512]{1,0:T(8,128)(2,1)S(1)} %get-tuple-element.40), channel_id=1, source_target_pairs={{0,24},{1,25},{2,26},{3,27},{4,28},{5,29},{6,30},{7,31},{8,0},{9,1... | collective-permute-start | bytes 688136 | tf_op jit(solution)/shard_map/ppermute | solution.py:546
  24.1 5.3 %slice-start.1 = ((s8[6291456]{0:T(1024)(128)(4,1)}), s8[2097152]{0:T(1024)(128)(4,1)S(1)}, s32[]{:S(2)}) async-start(s8[6291456]{0:T(1024)(128)(4,1)} %bitcast.7), calls=%async_computation.1 | async-start | bytes 4194304
  24.1 5.3 %copy-start = (bf16[2048,1024]{1,0:T(8,128)(2,1)S(1)}, bf16[2048,1024]{1,0:T(8,128)(2,1)}, u32[]{:S(2)}) copy-start(bf16[2048,1024]{1,0:T(8,128)(2,1)} %wm_ref.1) | copy-start | bytes 12582916
  24.1 5.3 %copy-start.1 = (bf16[1024,2048]{1,0:T(8,128)(2,1)S(1)}, bf16[1024,2048]{1,0:T(8,128)(2,1)}, u32[]{:S(2)}) copy-start(bf16[1024,2048]{1,0:T(8,128)(2,1)} %wsp_ref.3) | copy-start | bytes 12582916
  24.1 5.3 %copy-start.2 = (bf16[1024,1024]{1,0:T(8,128)(2,1)S(1)}, bf16[1024,1024]{1,0:T(8,128)(2,1)}, u32[]{:S(2)}) copy-start(bf16[1024,1024]{1,0:T(8,128)(2,1)} %wo_ref.5) | copy-start | bytes 6291460
  24.1 5.3 %copy-start.6 = (f32[2048]{0:T(1024)S(1)}, f32[2048]{0:T(1024)}, u32[]{:S(2)}) copy-start(f32[2048]{0:T(1024)} %param.16) | copy-start | bytes 24580
  24.2 5.3 %copy-start.7 = (f32[1024]{0:T(1024)S(1)}, f32[1024]{0:T(1024)}, u32[]{:S(2)}) copy-start(f32[1024]{0:T(1024)} %param.18) | copy-start | bytes 12292
  24.2 5.3 %copy-start.10 = (f32[4,2,288]{2,1,0:T(2,128)S(1)}, f32[4,2,288]{2,1,0:T(2,128)}, u32[]{:S(2)}) copy-start(f32[4,2,288]{2,1,0:T(2,128)} %constant.12.clone.weight_ref) | copy-start | bytes 27652
  39.4 31.6 %collective-permute-start.6 = (bf16[288,512]{1,0:T(8,128)(2,1)S(1)}, bf16[288,512]{1,0:T(8,128)(2,1)S(1)}, u32[]{:S(2)}, u32[]{:S(2)}) collective-permute-start(bf16[288,512]{1,0:T(8,128)(2,1)S(1)} %get-tuple-element.46), channel_id=1, source_target_pairs={{0,1},{1,2},{2,3},{3,4},{4,5},{5,6},{6,7},{7,0},{8,9},{9,10},{10,1... | collective-permute-start | bytes 884744 | tf_op jit(solution)/shard_map/ppermute | solution.py:546
  39.5 31.5 %collective-permute-start.7 = (bf16[288,512]{1,0:T(8,128)(2,1)S(1)}, bf16[288,512]{1,0:T(8,128)(2,1)S(1)}, u32[]{:S(2)}, u32[]{:S(2)}) collective-permute-start(bf16[288,512]{1,0:T(8,128)(2,1)S(1)} %get-tuple-element.47), channel_id=1, source_target_pairs={{0,8},{1,9},{2,10},{3,11},{4,12},{5,13},{6,14},{7,15},{8,16},{9,17... | collective-permute-start | bytes 884744 | tf_op jit(solution)/shard_map/ppermute | solution.py:546
  39.5 31.4 %collective-permute-start.8 = (bf16[288,512]{1,0:T(8,128)(2,1)S(1)}, bf16[288,512]{1,0:T(8,128)(2,1)S(1)}, u32[]{:S(2)}, u32[]{:S(2)}) collective-permute-start(bf16[288,512]{1,0:T(8,128)(2,1)S(1)} %get-tuple-element.48), channel_id=1, source_target_pairs={{0,9},{1,10},{2,11},{3,12},{4,13},{5,14},{6,15},{7,8},{8,17},{9,18... | collective-permute-start | bytes 884744 | tf_op jit(solution)/shard_map/ppermute | solution.py:546
  40.8 16.5 %collective-permute-start.9 = (f32[4,512]{1,0:T(4,128)S(1)}, f32[4,512]{1,0:T(4,128)S(1)}, u32[]{:S(2)}, u32[]{:S(2)}) collective-permute-start(f32[4,512]{1,0:T(4,128)S(1)} %get-tuple-element.49), channel_id=1, source_target_pairs={{0,8},{8,0},{16,24},{24,16},{1,9},{9,1},{17,25},{25,17},{2,10},{10... | collective-permute-start | bytes 24584 | tf_op jit(solution)/shard_map/ppermute | solution.py:526
  57.3 3.7 %collective-permute-start.10 = (f32[4,512]{1,0:T(4,128)S(1)}, f32[4,512]{1,0:T(4,128)S(1)}, u32[]{:S(2)}, u32[]{:S(2)}) collective-permute-start(f32[4,512]{1,0:T(4,128)S(1)} %add.15), channel_id=1, source_target_pairs={{0,2},{1,3},{2,0},{3,1},{4,6},{5,7},{6,4},{7,5},{8,10},{9,11},{10,... | collective-permute-start | bytes 24584 | tf_op jit(solution)/shard_map/ppermute | solution.py:526
  61.0 3.7 %collective-permute-start.11 = (f32[4,512]{1,0:T(4,128)S(1)}, f32[4,512]{1,0:T(4,128)S(1)}, u32[]{:S(2)}, u32[]{:S(2)}) collective-permute-start(f32[4,512]{1,0:T(4,128)S(1)} %add.16), channel_id=1, source_target_pairs={{0,4},{1,5},{2,6},{3,7},{4,0},{5,1},{6,2},{7,3},{8,12},{9,13},{10,... | collective-permute-start | bytes 24584 | tf_op jit(solution)/shard_map/ppermute | solution.py:526
  64.6 1.2 %collective-permute-start.12 = (f32[4,512]{1,0:T(4,128)S(1)}, f32[4,512]{1,0:T(4,128)S(1)}, u32[]{:S(2)}, u32[]{:S(2)}) collective-permute-start(f32[4,512]{1,0:T(4,128)S(1)} %add.17), channel_id=1, source_target_pairs={{0,1},{1,0},{2,3},{3,2},{4,5},{5,4},{6,7},{7,6},{8,9},{9,8},{10,11... | collective-permute-start | bytes 24584 | tf_op jit(solution)/shard_map/ppermute | solution.py:526
  65.8 4.5 %collective-permute-start.13 = (f32[4,512]{1,0:T(4,128)S(1)}, f32[4,512]{1,0:T(4,128)S(1)}, u32[]{:S(2)}, u32[]{:S(2)}) collective-permute-start(f32[4,512]{1,0:T(4,128)S(1)} %add.18), channel_id=1, source_target_pairs={{0,16},{8,24},{16,0},{24,8},{1,17},{9,25},{17,1},{25,9},{2,18},{10... | collective-permute-start | bytes 24584 | tf_op jit(solution)/shard_map/ppermute | solution.py:526
